TPU v7x, 32 devices: a whole 2x2x4 slice. The times are simulated.
32 devices in a mesh: section: 2 (over x), mirror: 2 (over y), dp: 8 (over z, core).
Axes of the slice: x: 2, y: 2, z: 4, core: 2. Of those that a mesh axis runs over, the one named last changes fastest.
Arguments:
- sent_fwd: bfloat16 [2, 2, 8, 4096], P('section', 'mirror', 'dp'), may hold values from -36 to 36
- sent_bwd: bfloat16 [2, 2, 8, 4096], P('section', 'mirror', 'dp'), may hold values from -6 to 6
- stash: bfloat16 [2, 2, 8, 4096], P('section', 'mirror', 'dp'), may hold values from -36 to 36
- gain: float32 [2, 4096], P('section'), may hold values from 0.5 to 1.5
- w_in: bfloat16 [2, 4096, 1024], P('section', None, 'dp'), may hold values from -0.09375 to 0.09375
- w_out: bfloat16 [2, 1024, 4096], P('section', 'dp'), may hold values from -0.375 to 0.375
Outputs:
- fwd_out: bfloat16 [2, 2, 8, 4096], P('section', 'mirror', 'dp')
- bwd_out: bfloat16 [2, 2, 8, 4096], P('section', 'mirror', 'dp')
- w_in_grad: bfloat16 [2, 4096, 1024], P('section', 'mirror', 'dp')
- w_out_grad: bfloat16 [2, 1024, 4096], P('section', 'dp', 'mirror')
All inputs are finite; a program needn't handle non-finite values.
Results may differ from a plain program's by a relative error of at most 0.0068.
Values may be sent and summed in bfloat16 or wider, within the bound.
No kernel may reach another device: no remote copies, remote signals or barrier semaphores. Data moves between devices by JAX's collectives and lax.ppermute only.
A program may use at most 64 MiB of HBM per device.

v0:
```python
import jax
import jax.numpy as jnp
from jax import lax
from jax.sharding import PartitionSpec as P


def extended_2(block, sides, width):
    for axis, dim in sides:
        count = lax.axis_size(axis)
        forward = [(i, i + 1) for i in range(count - 1)]
        forward.append((count - 1, 0))
        backward = [(target, source) for source, target in forward]
        low = lax.ppermute(
            lax.slice_in_dim(block, block.shape[dim] - width, None, axis=dim), axis, forward
        )
        high = lax.ppermute(lax.slice_in_dim(block, 0, width, axis=dim), axis, backward)
        block = jnp.concatenate([low, block, high], axis=dim)
    return block


def swapped(value, axis, apart):
    mask = 2**apart
    pairs = [(source, source ^ mask) for source in range(lax.axis_size(axis))]
    return lax.ppermute(value, axis, pairs)


def norm_rows(x):
    centre = x - jnp.mean(x, axis=-1, keepdims=True)
    rstd = lax.rsqrt(jnp.mean(centre * centre, axis=-1, keepdims=True) + 1e-05)
    return (centre * rstd, rstd)


def gelu_pair(h):
    coeff = 0.7978845608028654
    inner = coeff * (h + 0.044715 * h * h * h)
    tanh_val = jnp.tanh(inner)
    value = 0.5 * h * (1.0 + tanh_val)
    slope = 0.5 * (1.0 + tanh_val) + 0.5 * h * (1.0 - tanh_val * tanh_val) * coeff * (
        1.0 + 3.0 * 0.044715 * h * h
    )
    return (value, slope)


def rounded(values):
    return lax.optimization_barrier(values.astype(jnp.bfloat16)).astype(jnp.float32)


def on_device(sent_fwd, sent_bwd, stash, gain, w_in, w_out):
    mirror_pos = lax.axis_index("mirror")
    downward = mirror_pos == 0
    fwd_local = sent_fwd[0, 0]
    bwd_local = sent_bwd[0, 0]
    upward_load = jnp.where(downward, fwd_local, bwd_local)
    lower_load = jnp.where(downward, bwd_local, fwd_local)
    block = jnp.stack([lower_load, upward_load])
    extended = extended_2(block, (("section", 0),), 1)
    from_lower = extended[0]
    from_upper = extended[3]
    fwd_in = jnp.where(downward, from_lower, from_upper)
    bwd_in = jnp.where(downward, from_upper, from_lower)
    gain_row = gain[0]
    w_first = w_in[0]
    w_second = w_out[0]
    x_fwd = fwd_in.astype(jnp.float32)
    nhat_fwd, _ = norm_rows(x_fwd)
    normed_fwd = (nhat_fwd * gain_row).astype(jnp.bfloat16)
    nhat_bwd, rstd_bwd = norm_rows(stash[0, 0].astype(jnp.float32))
    normed_bwd = (nhat_bwd * gain_row).astype(jnp.bfloat16)
    whole_fwd, whole_bwd, whole_cotan = (
        lax.all_gather(normed_fwd, "dp", axis=0, tiled=True),
        lax.all_gather(normed_bwd, "dp", axis=0, tiled=True),
        lax.all_gather(bwd_in, "dp", axis=0, tiled=True),
    )
    hidden_fwd = jnp.dot(whole_fwd, w_first, preferred_element_type=jnp.float32)
    acted_fwd = gelu_pair(hidden_fwd)[0].astype(jnp.bfloat16)
    hidden_bwd = jnp.dot(whole_bwd, w_first, preferred_element_type=jnp.float32)
    value_bwd, slope_bwd = gelu_pair(hidden_bwd)
    acted_bwd = value_bwd.astype(jnp.bfloat16)
    d_acted = jnp.dot(whole_cotan, w_second.T, preferred_element_type=jnp.float32)
    d_hidden = (d_acted * slope_bwd).astype(jnp.bfloat16)
    piece = acted_fwd
    branch_sum = lax.psum_scatter(
        jnp.dot(piece, w_second, preferred_element_type=jnp.float32),
        "dp",
        scatter_dimension=0,
        tiled=True,
    )
    piece = d_hidden
    d_normed = lax.psum_scatter(
        jnp.dot(piece, w_first.T, preferred_element_type=jnp.float32),
        "dp",
        scatter_dimension=0,
        tiled=True,
    )
    fwd_result = (x_fwd + branch_sum).astype(jnp.bfloat16)
    scaled = d_normed * gain_row
    d_input = rstd_bwd * (
        scaled
        - jnp.mean(scaled, axis=-1, keepdims=True)
        - nhat_bwd * jnp.mean(scaled * nhat_bwd, axis=-1, keepdims=True)
    )
    bwd_result = (bwd_in.astype(jnp.float32) + d_input).astype(jnp.bfloat16)
    half_width = w_first.shape[0] // 2
    own_start = mirror_pos * half_width
    other_start = (1 - mirror_pos) * half_width
    grad_first = rounded(jnp.dot(whole_bwd.T, d_hidden, preferred_element_type=jnp.float32))
    summed_first = lax.psum_scatter(
        grad_first.astype(jnp.bfloat16), "mirror", scatter_dimension=0, tiled=True
    )
    outgoing = (acted_bwd, lax.dynamic_slice_in_dim(whole_cotan, other_start, half_width, 1))
    far_acted, far_cotan = swapped((outgoing[0], outgoing[1]), "mirror", 0)
    own_second = jnp.dot(
        acted_bwd.T,
        lax.dynamic_slice_in_dim(whole_cotan, own_start, half_width, 1),
        preferred_element_type=jnp.float32,
    )
    far_second = jnp.dot(far_acted.T, far_cotan, preferred_element_type=jnp.float32)
    summed_second = rounded(own_second) + rounded(far_second)
    return (
        fwd_result[None, None],
        bwd_result[None, None],
        summed_first[None],
        summed_second.astype(jnp.bfloat16)[None],
    )


def solution(mesh):
    in_specs = (
        P("section", "mirror", "dp", None),
        P("section", "mirror", "dp", None),
        P("section", "mirror", "dp", None),
        P("section", None),
        P("section", None, "dp"),
        P("section", "dp", None),
    )
    out_specs = (
        P("section", "mirror", "dp", None),
        P("section", "mirror", "dp", None),
        P("section", "mirror", "dp"),
        P("section", "dp", "mirror"),
    )
    return jax.shard_map(
        on_device, mesh=mesh, in_specs=in_specs, out_specs=out_specs, check_vma=False
    )
```

profile of v0, /device:TPU:0, one launch (start us, length us, event | category | flops | bytes accessed | tf_op | source)
XLA Modules:
  0.0 135.8 jit_solution(11940512752795791094)
XLA Ops:
  8.0 0.0 all-reduce.5.cloned.1.call-start
  8.1 0.9 fusion.21
  9.0 3.0 %collective-permute-start.1 = (bf16[1,1,4096]{2,1,0:T(2,128)(2,1)S(1)}, bf16[1,1,4096]{2,1,0:T(2,128)(2,1)S(1)}, u32[]{:S(2)}, u32[]{:S(2)}) collective-permute-start(bf16[1,1,4096]{2,1,0:T(2,128)(2,1)S(1)} %get-tuple-element.13), channel_id=1, source_target_pairs={{16,0},{0,16},{17,1},{1,17},{18,2},{2,18},{19,3},{3,19},{20,4},{4,... | collective-permute-start | bytes 24584 | tf_op jit(solution)/shard_map/ppermute | solution.py:16
  12.0 0.1 collective-permute-start
  12.1 1.4 convert_reduce_fusion
  14.1 1.4 %multiply_reduce_fusion = f32[]{:T(128)} fusion(bf16[1,1,1,4096]{3,2,1,0:T(2,128)(2,1)} %param.8, f32[]{:T(128)S(6)} %div.20), kind=kLoop, calls=%fused_computation.49 | loop fusion | flops 16383 | bytes 8200 | tf_op jit(solution)/shard_map/reduce_sum | solution.py:29
  16.1 1.3 dynamic-slice.2
  17.4 0.6 fusion.59
  18.7 0.6 multiply_reduce_fusion.1
  20.0 0.8 fusion.27
  20.8 14.7 %all-gather.1 = bf16[8,1,4096]{2,1,0:T(2,128)(2,1)S(1)} all-gather(bf16[1,1,4096]{2,1,0:T(2,128)(2,1)S(1)} %get-tuple-element.16), channel_id=1, replica_groups=mesh['section'=2,'mirror'=2,'dp'=8] {'dp'}, dimensions={0}, use_global_device_ids=true | all-gather | bytes 73728 | tf_op jit(solution)/shard_map/all_gather | solution.py:70
  35.6 14.0 %all-gather = bf16[8,1,4096]{2,1,0:T(2,128)(2,1)S(1)} all-gather(bf16[1,1,4096]{2,1,0:T(2,128)(2,1)S(1)} %broadcast_select_fusion.2), channel_id=2, replica_groups=mesh['section'=2,'mirror'=2,'dp'=8] {'dp'}, dimensions={0}, use_global_device_ids=true | all-gather | bytes 73728 | tf_op jit(solution)/shard_map/all_gather | solution.py:72
  49.5 14.0 %all-gather.2 = bf16[8,1,4096]{2,1,0:T(2,128)(2,1)S(1)} all-gather(bf16[1,1,4096]{2,1,0:T(2,128)(2,1)S(1)} %get-tuple-element.15), channel_id=1, replica_groups=mesh['section'=2,'mirror'=2,'dp'=8] {'dp'}, dimensions={0}, use_global_device_ids=true | all-gather | bytes 73728 | tf_op jit(solution)/shard_map/all_gather | solution.py:71
  63.5 0.3 multiply_convert_fusion
  63.8 1.2 fusion.2
  65.0 0.4 fusion
  65.4 1.0 fusion.4
  66.4 0.0 all-reduce.5.cloned.1.call-update
  66.5 0.0 reduce-scatter.2.cloned.1.call-start
  66.5 1.5 %convolution_convert_fusion = bf16[4096,128]{1,0:T(8,128)(2,1)} fusion(bf16[8,128]{1,0:T(8,128)(2,1)S(1)} %fusion, bf16[8,1,4096]{2,1,0:T(2,128)(2,1)S(1)} %all-gather.2), kind=kOutput, calls=%fused_computation | convolution fusion | flops 8912896 | bytes 1116160 | tf_op jit(solution)/shard_map/dot_general | solution.py:106
  68.0 1.5 %collective-permute-start.2 = (bf16[8,128]{1,0:T(8,128)(2,1)S(1)}, bf16[8,128]{1,0:T(8,128)(2,1)S(1)}, u32[]{:S(2)}, u32[]{:S(2)}) collective-permute-start(bf16[8,128]{1,0:T(8,128)(2,1)S(1)} %get-tuple-element.17), channel_id=1, source_target_pairs={{0,8},{8,0},{1,9},{9,1},{2,10},{10,2},{3,11},{11,3},{4,12},{12,4},... | collective-permute-start | bytes 6152 | tf_op jit(solution)/shard_map/ppermute | solution.py:24
  69.6 0.0 reduce-scatter.2.cloned.1.call-update
  69.6 0.1 constant_dynamic-slice_fusion.1
  69.8 0.6 collective-permute-start.3
  70.3 0.3 convolution_convert_fusion.2
  70.7 0.9 collective-permute-done.2
  71.6 2.1 %collective-permute-done.3 = bf16[8,2048]{1,0:T(8,128)(2,1)S(1)} collective-permute-done((bf16[8,2048]{1,0:T(8,128)(2,1)S(1)}, bf16[8,2048]{1,0:T(8,128)(2,1)S(1)}, u32[]{:S(2)}, u32[]{:S(2)}) %collective-permute-start.3) | collective-permute-done | bytes 32800 | tf_op jit(solution)/shard_map/ppermute | solution.py:24
  73.7 0.3 convolution_convert_fusion.1
  74.1 0.9 fusion.10
  75.0 47.7 %all-reduce.5.cloned.1.call-done = (f32[8,4096]{1,0:T(8,128)}, f32[8,4096]{1,0:T(8,128)}) async-done(((f32[8,4096]{1,0:T(8,128)}, f32[8,4096]{1,0:T(8,128)}), (f32[8,4096]{1,0:T(8,128)}, f32[8,4096]{1,0:T(8,128)})) %all-reduce.5.cloned.1.call-update) | async-done | bytes 262160
  122.7 2.2 %fusion.58 = (f32[]{:T(128)}, f32[]{:T(128)}, f32[1,4096]{1,0:T(1,128)S(1)}) fusion(f32[]{:T(128)S(6)} %rsqrt.9, f32[]{:T(128)S(6)} %div.20, bf16[1,1,1,4096]{3,2,1,0:T(2,128)(2,1)S(1)} %copy-done.2, f32[1,4096]{1,0:T(1,128)S(1)} %copy-done.3, f32[8,4096]{1,0:T(8,128)} %get-tuple-element.7, u32[]{:T(128)} %bitcast.15), kind=kLoop, calls=%fused_computation.79 | loop fusion | flops 28670 | bytes 57364 | tf_op jit(solution)/shard_map/reduce_sum | solution.py:99
  126.2 2.2 %fusion.23 = (bf16[1,1,1,4096]{3,2,1,0:T(2,128)(2,1)}, bf16[1,1,1,4096]{3,2,1,0:T(2,128)(2,1)}) fusion(bf16[1,1,4096]{2,1,0:T(2,128)(2,1)S(1)} %broadcast_select_fusion.2, f32[1,4096]{1,0:T(1,128)S(1)} %get-tuple-element.8, f32[]{:T(128)S(6)} %div.23, f32[]{:T(128)S(6)} %div.22, f32[]{:T(128)S(6)} %rsqrt.9, f32[]{:T(128)S(6)} %div.20, ...), kind=kLoop, calls=%fused_computation.35 | loop fusion | flops 49152 | bytes 84484 | tf_op jit(solution)/shard_map/broadcast_in_dim | solution.py:121
  (13 shorter events, 0.1 us)
Async XLA Ops:
  8.0 55.5 %copy-start = (bf16[1,4096,128]{2,1,0:T(8,128)(2,1)S(1)}, bf16[1,4096,128]{2,1,0:T(8,128)(2,1)}, u32[]{:S(2)}) copy-start(bf16[1,4096,128]{2,1,0:T(8,128)(2,1)} %param.10) | copy-start | bytes 3145732
  8.0 55.8 %copy-start.1 = (bf16[1,128,4096]{2,1,0:T(8,128)(2,1)S(1)}, bf16[1,128,4096]{2,1,0:T(8,128)(2,1)}, u32[]{:S(2)}) copy-start(bf16[1,128,4096]{2,1,0:T(8,128)(2,1)} %param.11) | copy-start | bytes 3145732
  8.0 114.7 %all-reduce.5.cloned.1.call-start = ((), (), s32[]{:S(2)}) async-start(), calls=%async_computation.2 | async-start | bytes 524288
  9.0 8.4 %collective-permute-start.1 = (bf16[1,1,4096]{2,1,0:T(2,128)(2,1)S(1)}, bf16[1,1,4096]{2,1,0:T(2,128)(2,1)S(1)}, u32[]{:S(2)}, u32[]{:S(2)}) collective-permute-start(bf16[1,1,4096]{2,1,0:T(2,128)(2,1)S(1)} %get-tuple-element.13), channel_id=1, source_target_pairs={{16,0},{0,16},{17,1},{1,17},{18,2},{2,18},{19,3},{3,19},{20,4},{4,... | collective-permute-start | bytes 24584 | tf_op jit(solution)/shard_map/ppermute | solution.py:16
  12.0 5.4 %collective-permute-start = (bf16[1,1,4096]{2,1,0:T(2,128)(2,1)S(1)}, bf16[1,1,4096]{2,1,0:T(2,128)(2,1)S(1)}, u32[]{:S(2)}, u32[]{:S(2)}) collective-permute-start(bf16[1,1,4096]{2,1,0:T(2,128)(2,1)S(1)} %get-tuple-element.14), channel_id=1, source_target_pairs={{0,16},{16,0},{1,17},{17,1},{2,18},{18,2},{3,19},{19,3},{4,20},{20... | collective-permute-start | bytes 24584 | tf_op jit(solution)/shard_map/ppermute | solution.py:13
  66.5 61.9 %reduce-scatter.2.cloned.1.call-start = ((), (), s32[]{:S(2)}) async-start(), calls=%async_computation.1 | async-start | bytes 1572864 | tf_op jit(solution)/shard_map/reduce_scatter | solution.py:107
  68.0 3.6 %collective-permute-start.2 = (bf16[8,128]{1,0:T(8,128)(2,1)S(1)}, bf16[8,128]{1,0:T(8,128)(2,1)S(1)}, u32[]{:S(2)}, u32[]{:S(2)}) collective-permute-start(bf16[8,128]{1,0:T(8,128)(2,1)S(1)} %get-tuple-element.17), channel_id=1, source_target_pairs={{0,8},{8,0},{1,9},{9,1},{2,10},{10,2},{3,11},{11,3},{4,12},{12,4},... | collective-permute-start | bytes 6152 | tf_op jit(solution)/shard_map/ppermute | solution.py:24
  69.8 4.0 %collective-permute-start.3 = (bf16[8,2048]{1,0:T(8,128)(2,1)S(1)}, bf16[8,2048]{1,0:T(8,128)(2,1)S(1)}, u32[]{:S(2)}, u32[]{:S(2)}) collective-permute-start(bf16[8,2048]{1,0:T(8,128)(2,1)S(1)} %bitcast.88), channel_id=1, source_target_pairs={{0,8},{8,0},{1,9},{9,1},{2,10},{10,2},{3,11},{11,3},{4,12},{12,4},... | collective-permute-start | bytes 98312 | tf_op jit(solution)/shard_map/ppermute | solution.py:24
  70.7 52.0 %copy-start.2 = (bf16[1,1,1,4096]{3,2,1,0:T(2,128)(2,1)S(1)}, bf16[1,1,1,4096]{3,2,1,0:T(2,128)(2,1)}, u32[]{:S(2)}) copy-start(bf16[1,1,1,4096]{3,2,1,0:T(2,128)(2,1)} %param.8) | copy-start | bytes 24580
  70.7 52.0 %copy-start.3 = (f32[1,4096]{1,0:T(1,128)S(1)}, f32[1,4096]{1,0:T(1,128)}, u32[]{:S(2)}) copy-start(f32[1,4096]{1,0:T(1,128)} %param.9) | copy-start | bytes 49156
Sparse Core Ops, SparseCore 0:
  66.6 56.0 all-reduce.4
Sparse Core Ops, SparseCore 1:
  69.8 21.2 reduce-scatter.1
where the time goes:
time: 136 us
  waiting for transfers between devices  50.8 us (37%)
  blocking collectives  42.7 us (31%)
  between operations  19.6 us (14%)
  other arithmetic  11 us (8%)
  starting transfers between devices  5.25 us (4%)
  matrix products  5.1 us (4%)
  local copies, waits for them, and re-layouts  1.47 us (1%)
    unnamed x3, waiting for transfers between devices  47.7 us
    all_gather x1, blocking collectives, on_device(): lax.all_gather(normed_fwd, 'dp', axis=0, tiled=True)  14.7 us
    all_gather x1, blocking collectives, on_device(): lax.all_gather(bwd_in, 'dp', axis=0, tiled=True)  14 us
    all_gather x1, blocking collectives, on_device(): lax.all_gather(normed_bwd, 'dp', axis=0, tiled=True)  14 us
    ppermute x2, waiting for transfers between devices, swapped(): return lax.ppermute(value, axis, pairs)  3.04 us
    ppermute x1, starting transfers between devices, extended_2(): lax.ppermute(lax.slice_in_dim(block, 0, width, axis=dim), axis, backward)  3 us
  transfers between devices with their start and end apart: 6, of which 3 were waited for; matrix products, arithmetic and copies ran while one was open for 9% of the time, Pallas kernels for 0%

commit v1 on v0

v1 whole, which is shorter than its diff:
```python
import jax
import jax.numpy as jnp
from jax import lax
from jax.sharding import PartitionSpec as P

AXES = ("section", "mirror", "dp")


def xor_pairs(count, mask):
    return [(source, source ^ mask) for source in range(count)]


def relay_pairs(sections, mirrors, count, mask):
    pairs = []
    for section in range(sections):
        for mirror in range(mirrors):
            step = 1 if mirror == 0 else -1
            for dp in range(count):
                source = (section * mirrors + mirror) * count + dp
                target = ((section + step) % sections * mirrors + mirror) * count + (dp ^ mask)
                pairs.append((source, target))
    return pairs


def norm_rows(x):
    centre = x - jnp.mean(x, axis=-1, keepdims=True)
    rstd = lax.rsqrt(jnp.mean(centre * centre, axis=-1, keepdims=True) + 1e-05)
    return (centre * rstd, rstd)


def gelu_pair(h):
    coeff = 0.7978845608028654
    inner = coeff * (h + 0.044715 * h * h * h)
    tanh_val = jnp.tanh(inner)
    value = 0.5 * h * (1.0 + tanh_val)
    slope = 0.5 * (1.0 + tanh_val) + 0.5 * h * (1.0 - tanh_val * tanh_val) * coeff * (
        1.0 + 3.0 * 0.044715 * h * h
    )
    return (value, slope)


def rounded(values):
    return lax.optimization_barrier(values.astype(jnp.bfloat16)).astype(jnp.float32)


def on_device(sent_fwd, sent_bwd, stash, gain, w_in, w_out):
    sections, mirrors = lax.axis_size("section"), lax.axis_size("mirror")
    count = lax.axis_size("dp")
    bits = count.bit_length() - 1
    masks = [(1 << bit) | 1 for bit in range(bits - 1, 0, -1)]
    mirror_pos = lax.axis_index("mirror")
    rows, width = sent_fwd.shape[2], sent_fwd.shape[3]
    gain_row = gain[0]
    w_first = w_in[0]
    w_second = w_out[0]
    fwd_in = lax.ppermute(sent_fwd[0, 0], AXES, relay_pairs(sections, mirrors, count, 1))
    back = [(target ^ 1, source ^ 1) for source, target in relay_pairs(sections, mirrors, count, 1)]
    bwd_in = lax.ppermute(sent_bwd[0, 0], AXES, back)
    held = jnp.stack([fwd_in, bwd_in, stash[0, 0]])
    for mask in masks:
        other = lax.ppermute(held, "dp", xor_pairs(count, mask))
        held = jnp.concatenate([held, other], axis=1)
    other = lax.ppermute(held, "dp", xor_pairs(count, 1))
    whole_fin = jnp.concatenate([other[0], held[0]], axis=0)
    whole_cotan = jnp.concatenate([other[1], held[1]], axis=0)
    whole_stash = jnp.concatenate([held[2], other[2]], axis=0)
    nhat_fwd, _ = norm_rows(whole_fin.astype(jnp.float32))
    whole_fwd = (nhat_fwd * gain_row).astype(jnp.bfloat16)
    nhat_bwd, rstd_bwd = norm_rows(whole_stash.astype(jnp.float32))
    whole_bwd = (nhat_bwd * gain_row).astype(jnp.bfloat16)
    hidden_fwd = jnp.dot(whole_fwd, w_first, preferred_element_type=jnp.float32)
    acted_fwd = gelu_pair(hidden_fwd)[0].astype(jnp.bfloat16)
    hidden_bwd = jnp.dot(whole_bwd, w_first, preferred_element_type=jnp.float32)
    value_bwd, slope_bwd = gelu_pair(hidden_bwd)
    acted_bwd = value_bwd.astype(jnp.bfloat16)
    d_acted = jnp.dot(whole_cotan, w_second.T, preferred_element_type=jnp.float32)
    d_hidden = (d_acted * slope_bwd).astype(jnp.bfloat16)
    part_fwd = jnp.dot(acted_fwd, w_second, preferred_element_type=jnp.float32)
    part_bwd = jnp.dot(d_hidden, w_first.T, preferred_element_type=jnp.float32)
    part = jnp.stack([part_fwd, part_bwd])
    for mask in [1] + masks[::-1]:
        half = part.shape[1] // 2
        sent = part[:, half:].astype(jnp.bfloat16)
        came = lax.ppermute(sent, "dp", xor_pairs(count, mask))
        part = part[:, :half] + came.astype(jnp.float32)
    branch_sum, d_normed = part[0], part[1]
    fwd_result = (whole_fin[:rows].astype(jnp.float32) + branch_sum).astype(jnp.bfloat16)
    scaled = d_normed * gain_row
    nhat_own = nhat_bwd[:rows]
    d_input = rstd_bwd[:rows] * (
        scaled
        - jnp.mean(scaled, axis=-1, keepdims=True)
        - nhat_own * jnp.mean(scaled * nhat_own, axis=-1, keepdims=True)
    )
    bwd_result = (whole_cotan[:rows].astype(jnp.float32) + d_input).astype(jnp.bfloat16)
    half_width = width // 2
    own_start = mirror_pos * half_width
    other_start = (1 - mirror_pos) * half_width

    def columns(value, start):
        return lax.dynamic_slice_in_dim(value, start, half_width, 1)

    outgoing = jnp.concatenate(
        [columns(whole_bwd, other_start), columns(whole_cotan, other_start), acted_bwd, d_hidden], axis=1
    )
    far = lax.ppermute(outgoing, "mirror", xor_pairs(mirrors, 1))
    far_bwd, far_cotan = far[:, :half_width], far[:, half_width : 2 * half_width]
    far_acted, far_hidden = jnp.split(far[:, 2 * half_width :], 2, axis=1)

    def outer(left, right):
        return jnp.dot(left.T, right, preferred_element_type=jnp.float32)

    summed_first = rounded(outer(columns(whole_bwd, own_start), d_hidden)) + rounded(outer(far_bwd, far_hidden))
    summed_second = rounded(outer(acted_bwd, columns(whole_cotan, own_start))) + rounded(outer(far_acted, far_cotan))
    return (
        fwd_result[None, None],
        bwd_result[None, None],
        summed_first.astype(jnp.bfloat16)[None],
        summed_second.astype(jnp.bfloat16)[None],
    )


def solution(mesh):
    in_specs = (
        P("section", "mirror", "dp", None),
        P("section", "mirror", "dp", None),
        P("section", "mirror", "dp", None),
        P("section", None),
        P("section", None, "dp"),
        P("section", "dp", None),
    )
    out_specs = (
        P("section", "mirror", "dp", None),
        P("section", "mirror", "dp", None),
        P("section", "mirror", "dp"),
        P("section", "dp", "mirror"),
    )
    return jax.shard_map(
        on_device, mesh=mesh, in_specs=in_specs, out_specs=out_specs, check_vma=False
    )
```

time: 136 us -> 36.2 us (0.27)
  blocking collectives: 42.7 us -> 0 us
  waiting for transfers between devices: 50.8 us -> 12.1 us
  between operations: 19.6 us -> 2.11 us
  starting transfers between devices: 5.25 us -> 12.5 us
  other arithmetic: 11 us -> 6.09 us
  matrix products: 5.1 us -> 2.94 us
    unnamed x3 -> x0, waiting for transfers between devices: 47.7 us -> none
    all_gather x3 -> x0, blocking collectives: 42.7 us -> none  [the longest x1 14.7 us: on_device(): lax.all_gather(normed_fwd, 'dp', axis=0, tiled=True)]
    ppermute x4 -> x9, waiting for transfers between devices: 3.04 us -> 12.1 us  [the longest x2 3.73 us: on_device(): other = lax.ppermute(held, 'dp', xor_pairs(count, mask))]
    ppermute x4 -> x9, starting transfers between devices: 5.17 us -> 12.5 us  [the longest x2 4.63 us: on_device(): other = lax.ppermute(held, 'dp', xor_pairs(count, mask))]
    dot_general x5 -> x6, matrix products: 4.43 us -> 2.31 us  [the longest x4 1.38 us: outer(): return jnp.dot(left.T, right, preferred_element_type=jnp.float32)]
    reduce_sum x2, other arithmetic: 1.99 us -> 0.31 us  [norm_rows(): centre = x - jnp.mean(x, axis=-1, keepdims=True)]
    reduce_sum x2, other arithmetic: 1.99 us -> 0.44 us  [norm_rows(): rstd = lax.rsqrt(jnp.mean(centre * centre, axis=-1, keepdims=True) + 1e-05)]
    reduce_sum x1, other arithmetic: 2.17 us -> 0.64 us  [on_device(): jnp.mean(scaled, axis=-1, keepdims=True)]
  transfers between devices with their start and end apart: 6 -> 9, of which waited for: 3 -> 7; matrix products, arithmetic and copies ran while one was open for 9% -> 9% of each run, Pallas kernels for 0% -> 0%
where the time goes in v1:
time: 36.2 us; the launch traced here: 36 us
  starting transfers between devices  12.5 us (35%)
  waiting for transfers between devices  12.1 us (33%)
  other arithmetic  6.09 us (17%)
  matrix products  2.94 us (8%)
  between operations  2.11 us (6%)
    ppermute x2, starting transfers between devices, on_device(): other = lax.ppermute(held, 'dp', xor_pairs(count, mask))  4.63 us
    ppermute x2, waiting for transfers between devices, on_device(): other = lax.ppermute(held, 'dp', xor_pairs(count, mask))  3.73 us
    ppermute x1, starting transfers between devices, on_device(): bwd_in = lax.ppermute(sent_bwd[0, 0], AXES, back)  2.44 us
    ppermute x3, starting transfers between devices, on_device(): came = lax.ppermute(sent, 'dp', xor_pairs(count, mask))  2.29 us
    ppermute x3, waiting for transfers between devices, on_device(): came = lax.ppermute(sent, 'dp', xor_pairs(count, mask))  2.28 us
    ppermute x1, waiting for transfers between devices, on_device(): far = lax.ppermute(outgoing, 'mirror', xor_pairs(mirrors, 1))  1.94 us
    ppermute x1, waiting for transfers between devices, on_device(): lax.ppermute(sent_fwd[0, 0], AXES, relay_pairs(sections, mirrors, count, 1))  1.72 us
    ppermute x1, starting transfers between devices, on_device(): far = lax.ppermute(outgoing, 'mirror', xor_pairs(mirrors, 1))  1.58 us
  transfers between devices with their start and end apart: 9, of which 7 were waited for; matrix products, arithmetic and copies ran while one was open for 9% of the time, Pallas kernels for 0%

profile of v1, /device:TPU:0, one launch (start us, length us, event | category | flops | bytes accessed | tf_op | source)
XLA Modules:
  0.0 36.0 jit_solution(10586608223292037243)
XLA Ops:
  0.6 2.4 %collective-permute-start.1 = (bf16[1,4096]{1,0:T(2,128)(2,1)}, bf16[1,4096]{1,0:T(2,128)(2,1)S(1)}, u32[]{:S(2)}, u32[]{:S(2)}) collective-permute-start(bf16[1,4096]{1,0:T(2,128)(2,1)} %bitcast.82), channel_id=1, source_target_pairs={{16,1},{17,0},{18,3},{19,2},{20,5},{21,4},{22,7},{23,6},{24,9},{25... | collective-permute-start | bytes 24584 | tf_op jit(solution)/shard_map/ppermute | solution.py:58
  3.2 1.6 %collective-permute-done.1 = bf16[1,4096]{1,0:T(2,128)(2,1)S(1)} collective-permute-done((bf16[1,4096]{1,0:T(2,128)(2,1)}, bf16[1,4096]{1,0:T(2,128)(2,1)S(1)}, u32[]{:S(2)}, u32[]{:S(2)}) %collective-permute-start.1) | collective-permute-done | bytes 8224 | tf_op jit(solution)/shard_map/ppermute | solution.py:58
  4.7 1.7 %collective-permute-done = bf16[1,4096]{1,0:T(2,128)(2,1)S(1)} collective-permute-done((bf16[1,4096]{1,0:T(2,128)(2,1)}, bf16[1,4096]{1,0:T(2,128)(2,1)S(1)}, u32[]{:S(2)}, u32[]{:S(2)}) %collective-permute-start) | collective-permute-done | bytes 8224 | tf_op jit(solution)/shard_map/ppermute | solution.py:56
  6.5 0.9 %pad_maximum_fusion.7 = bf16[3,1,4096]{2,1,0:T(2,128)(2,1)S(1)} fusion(bf16[1,1,4096]{2,1,0:T(2,128)(2,1)} %bitcast.72, bf16[1,1,4096]{2,1,0:T(2,128)(2,1)S(1)} %bitcast.75, bf16[1,1,4096]{2,1,0:T(2,128)(2,1)S(1)} %bitcast.78), kind=kLoop, calls=%fused_computation.52 | loop fusion | flops 24576 | bytes 49152 | tf_op jit(solution)/shard_map/stack | solution.py:59
  7.3 2.9 %collective-permute-start.2 = (bf16[3,1,4096]{2,1,0:T(2,128)(2,1)S(1)}, bf16[3,1,4096]{2,1,0:T(2,128)(2,1)S(1)}, u32[]{:S(2)}, u32[]{:S(2)}) collective-permute-start(bf16[3,1,4096]{2,1,0:T(2,128)(2,1)S(1)} %pad_maximum_fusion.7), channel_id=1, source_target_pairs={{0,5},{1,4},{2,7},{3,6},{4,1},{5,0},{6,3},{7,2},{8,13},{9,12},{10,... | collective-permute-start | bytes 73736 | tf_op jit(solution)/shard_map/ppermute | solution.py:61
  10.3 1.8 %collective-permute-done.2 = bf16[3,1,4096]{2,1,0:T(2,128)(2,1)S(1)} collective-permute-done((bf16[3,1,4096]{2,1,0:T(2,128)(2,1)S(1)}, bf16[3,1,4096]{2,1,0:T(2,128)(2,1)S(1)}, u32[]{:S(2)}, u32[]{:S(2)}) %collective-permute-start.2) | collective-permute-done | bytes 24608 | tf_op jit(solution)/shard_map/ppermute | solution.py:61
  12.2 1.7 %collective-permute-start.3 = (bf16[3,2,4096]{2,1,0:T(2,128)(2,1)S(1)}, bf16[3,2,4096]{2,1,0:T(2,128)(2,1)S(1)}, u32[]{:S(2)}, u32[]{:S(2)}) collective-permute-start(bf16[3,2,4096]{2,1,0:T(2,128)(2,1)S(1)} %pad_maximum_fusion.8), channel_id=1, source_target_pairs={{0,3},{1,2},{2,1},{3,0},{4,7},{5,6},{6,5},{7,4},{8,11},{9,10},{10,... | collective-permute-start | bytes 147464 | tf_op jit(solution)/shard_map/ppermute | solution.py:61
  13.9 2.0 %collective-permute-done.3 = bf16[3,2,4096]{2,1,0:T(2,128)(2,1)S(1)} collective-permute-done((bf16[3,2,4096]{2,1,0:T(2,128)(2,1)S(1)}, bf16[3,2,4096]{2,1,0:T(2,128)(2,1)S(1)}, u32[]{:S(2)}, u32[]{:S(2)}) %collective-permute-start.3) | collective-permute-done | bytes 49184 | tf_op jit(solution)/shard_map/ppermute | solution.py:61
  15.8 0.2 pad_maximum_fusion.1
  16.0 1.5 %collective-permute-start.4 = (bf16[3,4,4096]{2,1,0:T(4,128)(2,1)S(1)}, bf16[3,4,4096]{2,1,0:T(4,128)(2,1)S(1)}, u32[]{:S(2)}, u32[]{:S(2)}) collective-permute-start(bf16[3,4,4096]{2,1,0:T(4,128)(2,1)S(1)} %pad_maximum_fusion.1), channel_id=1, source_target_pairs={{0,1},{1,0},{2,3},{3,2},{4,5},{5,4},{6,7},{7,6},{8,9},{9,8},{10,11... | collective-permute-start | bytes 294920 | tf_op jit(solution)/shard_map/ppermute | solution.py:63
  17.5 0.9 %collective-permute-done.4 = bf16[3,4,4096]{2,1,0:T(4,128)(2,1)S(1)} collective-permute-done((bf16[3,4,4096]{2,1,0:T(4,128)(2,1)S(1)}, bf16[3,4,4096]{2,1,0:T(4,128)(2,1)S(1)}, u32[]{:S(2)}, u32[]{:S(2)}) %collective-permute-start.4) | collective-permute-done | bytes 98336 | tf_op jit(solution)/shard_map/ppermute | solution.py:63
  18.6 0.2 fusion.15
  19.0 0.2 fusion.14
  19.4 0.3 multiply_convert_fusion.1
  19.7 0.5 %convolution_bitcast_fusion.1 = f32[1,8,4096]{2,1,0:T(8,128)S(1)} fusion(bf16[1,128,4096]{2,1,0:T(8,128)(2,1)S(1)} %copy-done.1, bf16[1,4096,128]{2,1,0:T(8,128)(2,1)S(1)} %copy-done, f32[4096]{0:T(1024)S(1)} %bitcast.71, f32[8]{0:T(128)S(1)} %add_rsqrt_fusion.1, f32[8]{0:T(128)S(1)} %broadcast_multiply_fusion.1, bf16[4,4096]{1,0:T(4,128)(2,1)S(1)} %get-tuple-element.9, ...), kind=kOutput, calls=%fused_computation.1 | convolution fusion | flops 17048576 | bytes 2310208 | tf_op jit(solution)/shard_map/dot_general | solution.py:78
  20.3 0.4 %fusion = bf16[8,128]{1,0:T(8,128)(2,1)S(1)} fusion(bf16[1,128,4096]{2,1,0:T(8,128)(2,1)S(1)} %copy-done.1, bf16[4,4096]{1,0:T(4,128)(2,1)S(1)} %get-tuple-element.8, bf16[4,4096]{1,0:T(4,128)(2,1)S(1)} %get-tuple-element.11, f32[8,128]{1,0:T(8,128)S(1)} %get-tuple-element.16), kind=kOutput, calls=%fused_computation.7 | convolution fusion | flops 8539136 | bytes 1120256 | tf_op jit(solution)/shard_map/dot_general | solution.py:76
  20.7 0.4 %convolution_bitcast_fusion = f32[1,8,4096]{2,1,0:T(8,128)S(1)} fusion(bf16[8,128]{1,0:T(8,128)(2,1)S(1)} %fusion, bf16[1,4096,128]{2,1,0:T(8,128)(2,1)S(1)} %copy-done), kind=kOutput, calls=%fused_computation | convolution fusion | flops 8388608 | bytes 1181696 | tf_op jit(solution)/shard_map/dot_general | solution.py:79
  21.1 0.4 %collective-permute-start.5 = (bf16[2,4,4096]{2,1,0:T(4,128)(2,1)S(1)}, bf16[2,4,4096]{2,1,0:T(4,128)(2,1)S(1)}, u32[]{:S(2)}, u32[]{:S(2)}) collective-permute-start(bf16[2,4,4096]{2,1,0:T(4,128)(2,1)S(1)} %fusion.20), channel_id=1, source_target_pairs={{0,1},{1,0},{2,3},{3,2},{4,5},{5,4},{6,7},{7,6},{8,9},{9,8},{10,11... | collective-permute-start | bytes 196616 | tf_op jit(solution)/shard_map/ppermute | solution.py:84
  21.6 0.4 convolution_convert_fusion.3
  21.9 0.3 convolution_convert_fusion.1
  22.3 1.6 %collective-permute-start.8 = (bf16[8,4352]{1,0:T(8,128)(2,1)S(1)}, bf16[8,4352]{1,0:T(8,128)(2,1)S(1)}, u32[]{:S(2)}, u32[]{:S(2)}) collective-permute-start(bf16[8,4352]{1,0:T(8,128)(2,1)S(1)} %pad_maximum_fusion.3), channel_id=1, source_target_pairs={{0,8},{8,0},{1,9},{9,1},{2,10},{10,2},{3,11},{11,3},{4,12},{12,4},... | collective-permute-start | bytes 208904 | tf_op jit(solution)/shard_map/ppermute | solution.py:106
  24.0 0.8 %collective-permute-start.6 = (bf16[2,2,4096]{2,1,0:T(2,128)(2,1)S(1)}, bf16[2,2,4096]{2,1,0:T(2,128)(2,1)S(1)}, u32[]{:S(2)}, u32[]{:S(2)}) collective-permute-start(bf16[2,2,4096]{2,1,0:T(2,128)(2,1)S(1)} %slice.154), channel_id=1, source_target_pairs={{0,3},{1,2},{2,1},{3,0},{4,7},{5,6},{6,5},{7,4},{8,11},{9,10},{10,... | collective-permute-start | bytes 98312 | tf_op jit(solution)/shard_map/ppermute | solution.py:84
  24.7 1.9 %collective-permute-done.8 = bf16[8,4352]{1,0:T(8,128)(2,1)S(1)} collective-permute-done((bf16[8,4352]{1,0:T(8,128)(2,1)S(1)}, bf16[8,4352]{1,0:T(8,128)(2,1)S(1)}, u32[]{:S(2)}, u32[]{:S(2)}) %collective-permute-start.8) | collective-permute-done | bytes 69664 | tf_op jit(solution)/shard_map/ppermute | solution.py:106
  26.7 0.4 convolution_convert_fusion.2
  27.0 0.9 %fusion.8 = bf16[1,2048,128]{2,1,0:T(8,128)(2,1)} fusion(bf16[2048,128]{1,0:T(8,128)(2,1)S(1)} %convolution_convert_fusion.2, bf16[2048,128]{1,0:T(8,128)(2,1)S(1)} %convolution_convert_fusion.3), kind=kLoop, calls=%fused_computation.17 | loop fusion | flops 1048576 | bytes 1572864 | tf_op jit(solution)/shard_map/broadcast_in_dim | solution.py:118
  27.9 0.3 convolution_convert_fusion
  28.4 1.1 %collective-permute-start.7 = (bf16[2,1,4096]{2,1,0:T(2,128)(2,1)S(1)}, bf16[2,1,4096]{2,1,0:T(2,128)(2,1)S(1)}, u32[]{:S(2)}, u32[]{:S(2)}) collective-permute-start(bf16[2,1,4096]{2,1,0:T(2,128)(2,1)S(1)} %slice.155), channel_id=1, source_target_pairs={{0,5},{1,4},{2,7},{3,6},{4,1},{5,0},{6,3},{7,2},{8,13},{9,12},{10,... | collective-permute-start | bytes 49160 | tf_op jit(solution)/shard_map/ppermute | solution.py:84
  29.5 0.9 %fusion.9 = bf16[1,128,2048]{2,1,0:T(8,128)(2,1)} fusion(bf16[128,2048]{1,0:T(8,128)(2,1)S(1)} %convolution_convert_fusion, bf16[128,2048]{1,0:T(8,128)(2,1)S(1)} %convolution_convert_fusion.1), kind=kLoop, calls=%fused_computation.18 | loop fusion | flops 1048576 | bytes 1572864 | tf_op jit(solution)/shard_map/broadcast_in_dim | solution.py:119
  30.4 2.3 %collective-permute-done.7 = bf16[2,1,4096]{2,1,0:T(2,128)(2,1)S(1)} collective-permute-done((bf16[2,1,4096]{2,1,0:T(2,128)(2,1)S(1)}, bf16[2,1,4096]{2,1,0:T(2,128)(2,1)S(1)}, u32[]{:S(2)}, u32[]{:S(2)}) %collective-permute-start.7) | collective-permute-done | bytes 16416 | tf_op jit(solution)/shard_map/ppermute | solution.py:84
  32.7 0.6 %fusion.72 = (f32[]{:T(128)}, f32[]{:T(128)}, f32[1,4096]{1,0:T(1,128)S(1)}) fusion(f32[8,4096]{1,0:T(8,128)S(1)} %get-tuple-element.13, f32[1,4096]{1,0:T(1,128)S(1)} %copy-done.2, f32[2,1,4096]{2,1,0:T(1,128)S(1)} %slice_add_fusion.1), kind=kLoop, calls=%fused_computation.113 | loop fusion | flops 16382 | bytes 65544 | tf_op jit(solution)/shard_map/reduce_sum | solution.py:92
  34.7 0.6 %fusion.37 = bf16[1,1,1,4096]{3,2,1,0:T(2,128)(2,1)} fusion(f32[2,1,4096]{2,1,0:T(1,128)S(1)} %slice_add_fusion.1, bf16[3,4,4096]{2,1,0:T(4,128)(2,1)S(1)} %collective-permute-done.4), kind=kLoop, calls=%fused_computation.76 | loop fusion | flops 12288 | bytes 32768 | tf_op jit(solution)/shard_map/convert_element_type | solution.py:87
  35.3 0.7 %fusion.35 = bf16[1,1,1,4096]{3,2,1,0:T(2,128)(2,1)} fusion(bf16[3,4,4096]{2,1,0:T(4,128)(2,1)S(1)} %collective-permute-done.4, f32[1,4096]{1,0:T(1,128)S(1)} %get-tuple-element.6, f32[8,4096]{1,0:T(8,128)S(1)} %get-tuple-element.13, f32[]{:T(128)S(6)} %div.23, f32[]{:T(128)S(6)} %div.22, f32[]{:T(128)S(1)} %bitcast.81), kind=kLoop, calls=%fused_computation.73 | loop fusion | flops 28672 | bytes 49164 | tf_op jit(solution)/shard_map/broadcast_in_dim | solution.py:117
  (30 shorter events, 1.1 us)
Async XLA Ops:
  0.6 18.7 %copy-start = (bf16[1,4096,128]{2,1,0:T(8,128)(2,1)S(1)}, bf16[1,4096,128]{2,1,0:T(8,128)(2,1)}, u32[]{:S(2)}) copy-start(bf16[1,4096,128]{2,1,0:T(8,128)(2,1)} %param.10) | copy-start | bytes 3145732
  0.6 4.1 %collective-permute-start.1 = (bf16[1,4096]{1,0:T(2,128)(2,1)}, bf16[1,4096]{1,0:T(2,128)(2,1)S(1)}, u32[]{:S(2)}, u32[]{:S(2)}) collective-permute-start(bf16[1,4096]{1,0:T(2,128)(2,1)} %bitcast.82), channel_id=1, source_target_pairs={{16,1},{17,0},{18,3},{19,2},{20,5},{21,4},{22,7},{23,6},{24,9},{25... | collective-permute-start | bytes 24584 | tf_op jit(solution)/shard_map/ppermute | solution.py:58
  3.1 3.4 %collective-permute-start = (bf16[1,4096]{1,0:T(2,128)(2,1)}, bf16[1,4096]{1,0:T(2,128)(2,1)S(1)}, u32[]{:S(2)}, u32[]{:S(2)}) collective-permute-start(bf16[1,4096]{1,0:T(2,128)(2,1)} %bitcast.83), channel_id=1, source_target_pairs={{0,17},{1,16},{2,19},{3,18},{4,21},{5,20},{6,23},{7,22},{8,25},{9,... | collective-permute-start | bytes 24584 | tf_op jit(solution)/shard_map/ppermute | solution.py:56
  6.5 5.6 %copy-start.3 = (bf16[1,1,1,4096]{3,2,1,0:T(2,128)(2,1)S(1)}, bf16[1,1,1,4096]{3,2,1,0:T(2,128)(2,1)}, u32[]{:S(2)}) copy-start(bf16[1,1,1,4096]{3,2,1,0:T(2,128)(2,1)} %param.8) | copy-start | bytes 24580
  7.3 4.7 %collective-permute-start.2 = (bf16[3,1,4096]{2,1,0:T(2,128)(2,1)S(1)}, bf16[3,1,4096]{2,1,0:T(2,128)(2,1)S(1)}, u32[]{:S(2)}, u32[]{:S(2)}) collective-permute-start(bf16[3,1,4096]{2,1,0:T(2,128)(2,1)S(1)} %pad_maximum_fusion.7), channel_id=1, source_target_pairs={{0,5},{1,4},{2,7},{3,6},{4,1},{5,0},{6,3},{7,2},{8,13},{9,12},{10,... | collective-permute-start | bytes 73736 | tf_op jit(solution)/shard_map/ppermute | solution.py:61
  12.2 3.6 %collective-permute-start.3 = (bf16[3,2,4096]{2,1,0:T(2,128)(2,1)S(1)}, bf16[3,2,4096]{2,1,0:T(2,128)(2,1)S(1)}, u32[]{:S(2)}, u32[]{:S(2)}) collective-permute-start(bf16[3,2,4096]{2,1,0:T(2,128)(2,1)S(1)} %pad_maximum_fusion.8), channel_id=1, source_target_pairs={{0,3},{1,2},{2,1},{3,0},{4,7},{5,6},{6,5},{7,4},{8,11},{9,10},{10,... | collective-permute-start | bytes 147464 | tf_op jit(solution)/shard_map/ppermute | solution.py:61
  15.8 3.5 %copy-start.2 = (f32[1,4096]{1,0:T(1,128)S(1)}, f32[1,4096]{1,0:T(1,128)}, u32[]{:S(2)}) copy-start(f32[1,4096]{1,0:T(1,128)} %param.9) | copy-start | bytes 49156
  16.0 3.7 %copy-start.1 = (bf16[1,128,4096]{2,1,0:T(8,128)(2,1)S(1)}, bf16[1,128,4096]{2,1,0:T(8,128)(2,1)}, u32[]{:S(2)}) copy-start(bf16[1,128,4096]{2,1,0:T(8,128)(2,1)} %param.11) | copy-start | bytes 3145732
  16.0 2.4 %collective-permute-start.4 = (bf16[3,4,4096]{2,1,0:T(4,128)(2,1)S(1)}, bf16[3,4,4096]{2,1,0:T(4,128)(2,1)S(1)}, u32[]{:S(2)}, u32[]{:S(2)}) collective-permute-start(bf16[3,4,4096]{2,1,0:T(4,128)(2,1)S(1)} %pad_maximum_fusion.1), channel_id=1, source_target_pairs={{0,1},{1,0},{2,3},{3,2},{4,5},{5,4},{6,7},{7,6},{8,9},{9,8},{10,11... | collective-permute-start | bytes 294920 | tf_op jit(solution)/shard_map/ppermute | solution.py:63
  21.1 2.7 %collective-permute-start.5 = (bf16[2,4,4096]{2,1,0:T(4,128)(2,1)S(1)}, bf16[2,4,4096]{2,1,0:T(4,128)(2,1)S(1)}, u32[]{:S(2)}, u32[]{:S(2)}) collective-permute-start(bf16[2,4,4096]{2,1,0:T(4,128)(2,1)S(1)} %fusion.20), channel_id=1, source_target_pairs={{0,1},{1,0},{2,3},{3,2},{4,5},{5,4},{6,7},{7,6},{8,9},{9,8},{10,11... | collective-permute-start | bytes 196616 | tf_op jit(solution)/shard_map/ppermute | solution.py:84
  22.3 4.4 %collective-permute-start.8 = (bf16[8,4352]{1,0:T(8,128)(2,1)S(1)}, bf16[8,4352]{1,0:T(8,128)(2,1)S(1)}, u32[]{:S(2)}, u32[]{:S(2)}) collective-permute-start(bf16[8,4352]{1,0:T(8,128)(2,1)S(1)} %pad_maximum_fusion.3), channel_id=1, source_target_pairs={{0,8},{8,0},{1,9},{9,1},{2,10},{10,2},{3,11},{11,3},{4,12},{12,4},... | collective-permute-start | bytes 208904 | tf_op jit(solution)/shard_map/ppermute | solution.py:106
  24.0 4.3 %collective-permute-start.6 = (bf16[2,2,4096]{2,1,0:T(2,128)(2,1)S(1)}, bf16[2,2,4096]{2,1,0:T(2,128)(2,1)S(1)}, u32[]{:S(2)}, u32[]{:S(2)}) collective-permute-start(bf16[2,2,4096]{2,1,0:T(2,128)(2,1)S(1)} %slice.154), channel_id=1, source_target_pairs={{0,3},{1,2},{2,1},{3,0},{4,7},{5,6},{6,5},{7,4},{8,11},{9,10},{10,... | collective-permute-start | bytes 98312 | tf_op jit(solution)/shard_map/ppermute | solution.py:84
  28.4 4.3 %collective-permute-start.7 = (bf16[2,1,4096]{2,1,0:T(2,128)(2,1)S(1)}, bf16[2,1,4096]{2,1,0:T(2,128)(2,1)S(1)}, u32[]{:S(2)}, u32[]{:S(2)}) collective-permute-start(bf16[2,1,4096]{2,1,0:T(2,128)(2,1)S(1)} %slice.155), channel_id=1, source_target_pairs={{0,5},{1,4},{2,7},{3,6},{4,1},{5,0},{6,3},{7,2},{8,13},{9,12},{10,... | collective-permute-start | bytes 49160 | tf_op jit(solution)/shard_map/ppermute | solution.py:84

commit v2 on v1

v2 whole, which is shorter than its diff:
```python
import functools

import jax
import jax.numpy as jnp
from jax import lax
from jax.experimental import pallas as pl
from jax.experimental.pallas import tpu as pltpu
from jax.sharding import PartitionSpec as P

AXES = ("section", "mirror", "dp")
VMEM = pl.BlockSpec(memory_space=pltpu.VMEM)


def xor_pairs(count, mask):
    return [(source, source ^ mask) for source in range(count)]


def relay_pairs(sections, mirrors, count, mask, sign):
    pairs = []
    for section in range(sections):
        for mirror in range(mirrors):
            step = sign if mirror == 0 else -sign
            for dp in range(count):
                source = (section * mirrors + mirror) * count + dp
                target = ((section + step) % sections * mirrors + mirror) * count + (dp ^ mask)
                pairs.append((source, target))
    return sorted(pairs)


def norm_rows(x):
    centre = x - jnp.mean(x, axis=-1, keepdims=True)
    rstd = lax.rsqrt(jnp.mean(centre * centre, axis=-1, keepdims=True) + 1e-05)
    return (centre * rstd, rstd)


def gelu_pair(h):
    coeff = 0.7978845608028654
    inner = coeff * (h + 0.044715 * h * h * h)
    tanh_val = jnp.tanh(inner)
    value = 0.5 * h * (1.0 + tanh_val)
    slope = 0.5 * (1.0 + tanh_val) + 0.5 * h * (1.0 - tanh_val * tanh_val) * coeff * (
        1.0 + 3.0 * 0.044715 * h * h
    )
    return (value, slope)


def dot(left, right, contract):
    return lax.dot_general(left, right, ((contract[:1], contract[1:]), ((), ())), preferred_element_type=jnp.float32)


def block_kernel(rows, held, other, gain, w_in, w_out, send, keep, own_out, far_out, tail, tail_rstd):
    half, width = held.shape[1], held.shape[2]
    f32, bf16 = jnp.float32, jnp.bfloat16

    def joined(first, second):
        return jnp.concatenate([first.astype(f32), second.astype(f32)], axis=0)

    fin = joined(other[0], held[0])
    cotan = joined(other[1], held[1])
    stash = joined(held[2], other[2])
    nhat_fwd, _ = norm_rows(fin)
    nhat_bwd, rstd_bwd = norm_rows(stash)
    normed_bwd = nhat_bwd * gain[...]
    both = jnp.concatenate([nhat_fwd * gain[...], normed_bwd], axis=0).astype(bf16)
    hidden = dot(both, w_in[...], (1, 0))
    cotan_low = cotan.astype(bf16)
    d_acted = dot(cotan_low, w_out[...], (1, 1))
    value, slope = gelu_pair(hidden)
    value_low = value.astype(bf16)
    d_hidden = (d_acted * slope[2 * half :]).astype(bf16)
    part_bwd = dot(d_hidden, w_in[...], (1, 1))
    part_fwd = dot(value_low[: 2 * half], w_out[...], (1, 0))
    keep[0] = part_fwd[:half]
    keep[1] = part_bwd[:half]
    send[0] = part_fwd[half:].astype(bf16)
    send[1] = part_bwd[half:].astype(bf16)
    tail[0] = fin[:rows]
    tail[1] = cotan[:rows]
    tail[2] = nhat_bwd[:rows]
    tail_rstd[...] = jnp.broadcast_to(rstd_bwd[:rows], tail_rstd.shape)
    mid = width // 2
    units = w_in.shape[1]
    normed_low = normed_bwd.astype(bf16)
    upper = lax.axis_index("mirror") == 0
    for ref in (own_out, far_out):
        ref[:, 2 * mid : 2 * mid + units] = value_low[2 * half :]
        ref[:, 2 * mid + units :] = d_hidden

    @pl.when(upper)
    def _():
        own_out[:, :mid] = normed_low[:, :mid]
        own_out[:, mid : 2 * mid] = cotan_low[:, :mid]
        far_out[:, :mid] = normed_low[:, mid:]
        far_out[:, mid : 2 * mid] = cotan_low[:, mid:]

    @pl.when(jnp.logical_not(upper))
    def _():
        own_out[:, :mid] = normed_low[:, mid:]
        own_out[:, mid : 2 * mid] = cotan_low[:, mid:]
        far_out[:, :mid] = normed_low[:, :mid]
        far_out[:, mid : 2 * mid] = cotan_low[:, :mid]


def load_kernel(chunks, source, target, sems):
    step = source.shape[0] // chunks
    copies = [
        pltpu.make_async_copy(source.at[pl.ds(i * step, step)], target.at[pl.ds(i * step, step)], sems.at[i])
        for i in range(chunks)
    ]
    for copy in copies:
        copy.start()
    for copy in copies:
        copy.wait()


def loaded(weights, chunks):
    size = weights.size * weights.dtype.itemsize
    return pl.pallas_call(
        functools.partial(load_kernel, chunks),
        out_shape=jax.ShapeDtypeStruct(weights.shape, weights.dtype),
        in_specs=[pl.BlockSpec(memory_space=pl.ANY)],
        out_specs=VMEM,
        scratch_shapes=[pltpu.SemaphoreType.DMA((chunks,))],
        compiler_params=pltpu.CompilerParams(vmem_limit_bytes=max(4 << 20, 2 * size)),
        cost_estimate=pl.CostEstimate(flops=0, bytes_accessed=3 * size, transcendentals=0),
    )(weights)


def tail_kernel(rows, part, came, gain, tail, tail_rstd, fwd_out, bwd_out):
    f32 = jnp.float32
    branch = part[0, :rows] + came[0].astype(f32)
    fwd_out[...] = (tail[0] + branch).astype(fwd_out.dtype)
    scaled = (part[1, :rows] + came[1].astype(f32)) * gain[...]
    nhat = tail[2]
    d_input = tail_rstd[:, :1] * (
        scaled
        - jnp.mean(scaled, axis=-1, keepdims=True)
        - nhat * jnp.mean(scaled * nhat, axis=-1, keepdims=True)
    )
    bwd_out[...] = (tail[1] + d_input).astype(bwd_out.dtype)


def on_device(sent_fwd, sent_bwd, stash, gain, w_in, w_out):
    sections, mirrors = lax.axis_size("section"), lax.axis_size("mirror")
    count = lax.axis_size("dp")
    bits = count.bit_length() - 1
    masks = [(1 << bit) | 1 for bit in range(bits - 1, 0, -1)]
    rows, width = sent_fwd.shape[2], sent_fwd.shape[3]
    units = w_in.shape[2]
    fwd_in = lax.ppermute(sent_fwd[0, 0], AXES, relay_pairs(sections, mirrors, count, 1, 1))
    bwd_in = lax.ppermute(sent_bwd[0, 0], AXES, relay_pairs(sections, mirrors, count, 1, -1))
    w_first = loaded(w_in[0], 4)
    fwd_in, bwd_in, w_first = lax.optimization_barrier((fwd_in, bwd_in, w_first))
    w_second = loaded(w_out[0], 4)
    held = jnp.stack([fwd_in, bwd_in, stash[0, 0]])
    for mask in masks:
        other = lax.ppermute(held, "dp", xor_pairs(count, mask))
        if mask == masks[0]:
            other, w_second = lax.optimization_barrier((other, w_second))
        held = jnp.concatenate([held, other], axis=1)
    other = lax.ppermute(held, "dp", xor_pairs(count, 1))
    half = held.shape[1]
    low = jax.ShapeDtypeStruct((2 * half, width + 2 * units), jnp.bfloat16)
    send, keep, own, away, tail, tail_rstd = pl.pallas_call(
        functools.partial(block_kernel, rows),
        out_shape=(
            jax.ShapeDtypeStruct((2, half, width), jnp.bfloat16),
            jax.ShapeDtypeStruct((2, half, width), jnp.float32),
            low,
            low,
            jax.ShapeDtypeStruct((3, rows, width), jnp.float32),
            jax.ShapeDtypeStruct((rows, 128), jnp.float32),
        ),
        in_specs=[VMEM] * 5,
        out_specs=[VMEM] * 6,
        compiler_params=pltpu.CompilerParams(vmem_limit_bytes=max(8 << 20, 40 * half * width * 4)),
    )(held, other, gain, w_first, w_second)
    part = None
    for mask in [1] + masks[::-1]:
        if part is not None:
            half = part.shape[1] // 2
            send, keep = part[:, half:].astype(jnp.bfloat16), part[:, :half]
        came = lax.ppermute(send, "dp", xor_pairs(count, mask))
        if mask != (masks or [1])[0]:
            part = keep + came.astype(jnp.float32)
            if mask == 1:
                part, away = lax.optimization_barrier((part, away))
    far = lax.ppermute(away, "mirror", xor_pairs(mirrors, 1))
    pair = jnp.concatenate([own, far], axis=0)
    mid = width // 2
    grad_first = dot(pair[:, :mid], pair[:, 2 * mid + units :], (0, 0)).astype(jnp.bfloat16)
    grad_second = dot(pair[:, 2 * mid : 2 * mid + units], pair[:, mid : 2 * mid], (0, 0)).astype(jnp.bfloat16)
    part, grad_first, grad_second = lax.optimization_barrier((part, grad_first, grad_second))
    fwd_out, bwd_out = pl.pallas_call(
        functools.partial(tail_kernel, rows),
        out_shape=(jax.ShapeDtypeStruct((rows, width), jnp.bfloat16),) * 2,
        in_specs=[VMEM] * 5,
        out_specs=[VMEM] * 2,
        compiler_params=pltpu.CompilerParams(vmem_limit_bytes=max(4 << 20, 40 * rows * width * 4)),
    )(part, came, gain, tail, tail_rstd)
    return (fwd_out[None, None], bwd_out[None, None], grad_first[None], grad_second[None])


def solution(mesh):
    in_specs = (
        P("section", "mirror", "dp", None),
        P("section", "mirror", "dp", None),
        P("section", "mirror", "dp", None),
        P("section", None),
        P("section", None, "dp"),
        P("section", "dp", None),
    )
    out_specs = (
        P("section", "mirror", "dp", None),
        P("section", "mirror", "dp", None),
        P("section", "mirror", "dp"),
        P("section", "dp", "mirror"),
    )
    return jax.shard_map(
        on_device, mesh=mesh, in_specs=in_specs, out_specs=out_specs, check_vma=False
    )
```

time: 36.2 us -> 29.7 us (0.82)
  other arithmetic: 6.09 us -> 0.42 us
  waiting for transfers between devices: 12.1 us -> 8.21 us
  Pallas kernels: 0 us -> 2.78 us
  between operations: 2.11 us -> 0.71 us
  starting transfers between devices: 12.5 us -> 13.8 us
  local copies, waits for them, and re-layouts: 0.18 us -> 1.32 us
  matrix products: 2.94 us -> 2.23 us
    ppermute x6, waiting for transfers between devices: 7.52 us -> 3.67 us  [the longest x1 1.72 us: on_device(): lax.ppermute(sent_bwd[0, 0], AXES, relay_pairs(sections, mirrors, count,...]
    pallas_call x0 -> x4, Pallas kernels: none -> 2.78 us  [the longest x1 1.8 us: on_device(): pl.pallas_call(functools.partial(block_kernel, rows), out_shape=(jax.Shap...]
    broadcast_in_dim x3 -> x0, other arithmetic: 2.53 us -> none  [the longest x1 0.93 us: on_device(): summed_first.astype(jnp.bfloat16)[None]]
    reduce_sum x5 -> x0, other arithmetic: 1.38 us -> none  [the longest x1 0.64 us: on_device(): jnp.mean(scaled, axis=-1, keepdims=True)]
    ppermute x6, starting transfers between devices: 6.39 us -> 7.7 us  [the longest x3 3.63 us: on_device(): came = lax.ppermute(send, 'dp', xor_pairs(count, mask))]
    unnamed x8 -> x9, local copies, waits for them, and re-layouts: 0.02 us -> 1.24 us
    another operation x1, other arithmetic: 0.87 us -> 0.08 us  [on_device(): held = jnp.stack([fwd_in, bwd_in, stash[0, 0]])]
    dot_general x8 -> x2, matrix products: 2.94 us -> 2.23 us  [dot(): lax.dot_general(left, right, ((contract[:1], contract[1:]), ((), ())), pr...]
  transfers between devices with their start and end apart: 9 -> 9, of which waited for: 7 -> 7; matrix products, arithmetic and copies ran while one was open for 9% -> 8% of each run, Pallas kernels for 0% -> 1%
where the time goes in v2:
time: 29.7 us; the launch traced here: 29.5 us
  starting transfers between devices  13.8 us (46%)
  waiting for transfers between devices  8.21 us (28%)
  Pallas kernels  2.78 us (9%)
  matrix products  2.23 us (8%)
  local copies, waits for them, and re-layouts  1.32 us (4%)
  between operations  0.71 us (2%)
  other arithmetic  0.42 us (1%)
    ppermute x2, starting transfers between devices, on_device(): other = lax.ppermute(held, 'dp', xor_pairs(count, mask))  4.63 us
    ppermute x3, starting transfers between devices, on_device(): came = lax.ppermute(send, 'dp', xor_pairs(count, mask))  3.63 us
    ppermute x2, waiting for transfers between devices, on_device(): other = lax.ppermute(held, 'dp', xor_pairs(count, mask))  3.6 us
    ppermute x1, starting transfers between devices, on_device(): lax.ppermute(sent_fwd[0, 0], AXES, relay_pairs(sections, mirrors, count,...  2.44 us
    dot_general x2, matrix products, dot(): lax.dot_general(left, right, ((contract[:1], contract[1:]), ((), ())), pr...  2.23 us
    pallas_call x1, Pallas kernels, on_device(): pl.pallas_call(functools.partial(block_kernel, rows), out_shape=(jax.Shap...  1.8 us
    ppermute x1, waiting for transfers between devices, on_device(): lax.ppermute(sent_bwd[0, 0], AXES, relay_pairs(sections, mirrors, count,...  1.72 us
    ppermute x3, waiting for transfers between devices, on_device(): came = lax.ppermute(send, 'dp', xor_pairs(count, mask))  1.72 us
  transfers between devices with their start and end apart: 9, of which 7 were waited for; matrix products, arithmetic and copies ran while one was open for 8% of the time, Pallas kernels for 1%

profile of v2, /device:TPU:0, one launch (start us, length us, event | category | flops | bytes accessed | tf_op | source)
XLA Modules:
  0.0 29.5 jit_solution(1859735001230112037)
XLA Ops:
  0.6 2.4 %collective-permute-start = (bf16[1,4096]{1,0:T(2,128)(2,1)}, bf16[1,4096]{1,0:T(2,128)(2,1)S(1)}, u32[]{:S(2)}, u32[]{:S(2)}) collective-permute-start(bf16[1,4096]{1,0:T(2,128)(2,1)} %bitcast.31), channel_id=1, source_target_pairs={{0,17},{1,16},{2,19},{3,18},{4,21},{5,20},{6,23},{7,22},{8,25},{9,... | collective-permute-start | bytes 24584 | tf_op jit(solution)/shard_map/ppermute | solution.py:150
  3.1 0.1 collective-permute-start.1
  3.2 1.2 %copy-done = bf16[1,4096,128]{2,1,0:T(8,128)(2,1)S(1)} copy-done((bf16[1,4096,128]{2,1,0:T(8,128)(2,1)S(1)}, bf16[1,4096,128]{2,1,0:T(8,128)(2,1)}, u32[]{:S(2)}) %copy-start) | copy-done | bytes 1048600
  4.4 0.1 shard_map.93.w_in
  4.5 0.2 collective-permute-done
  4.7 1.7 %collective-permute-done.1 = bf16[1,4096]{1,0:T(2,128)(2,1)S(1)} collective-permute-done((bf16[1,4096]{1,0:T(2,128)(2,1)}, bf16[1,4096]{1,0:T(2,128)(2,1)S(1)}, u32[]{:S(2)}, u32[]{:S(2)}) %collective-permute-start.1) | collective-permute-done | bytes 8224 | tf_op jit(solution)/shard_map/ppermute | solution.py:151
  6.5 0.0 copy-done.3
  6.5 0.1 pad_maximum_fusion.1
  6.5 2.9 %collective-permute-start.2 = (bf16[3,1,4096]{2,1,0:T(2,128)(2,1)S(1)}, bf16[3,1,4096]{2,1,0:T(2,128)(2,1)S(1)}, u32[]{:S(2)}, u32[]{:S(2)}) collective-permute-start(bf16[3,1,4096]{2,1,0:T(2,128)(2,1)S(1)} %pad_maximum_fusion.1), channel_id=1, source_target_pairs={{0,5},{1,4},{2,7},{3,6},{4,1},{5,0},{6,3},{7,2},{8,13},{9,12},{10,... | collective-permute-start | bytes 73736 | tf_op jit(solution)/shard_map/ppermute | solution.py:157
  9.5 0.0 copy-done.1
  9.5 0.1 shard_map.94.w_out
  9.6 1.6 %collective-permute-done.2 = bf16[3,1,4096]{2,1,0:T(2,128)(2,1)S(1)} collective-permute-done((bf16[3,1,4096]{2,1,0:T(2,128)(2,1)S(1)}, bf16[3,1,4096]{2,1,0:T(2,128)(2,1)S(1)}, u32[]{:S(2)}, u32[]{:S(2)}) %collective-permute-start.2) | collective-permute-done | bytes 24608 | tf_op jit(solution)/shard_map/ppermute | solution.py:157
  11.3 0.1 pad_maximum_fusion.2
  11.4 0.0 copy-start.2
  11.4 1.7 %collective-permute-start.3 = (bf16[3,2,4096]{2,1,0:T(2,128)(2,1)S(1)}, bf16[3,2,4096]{2,1,0:T(2,128)(2,1)S(1)}, u32[]{:S(2)}, u32[]{:S(2)}) collective-permute-start(bf16[3,2,4096]{2,1,0:T(2,128)(2,1)S(1)} %pad_maximum_fusion.2), channel_id=1, source_target_pairs={{0,3},{1,2},{2,1},{3,0},{4,7},{5,6},{6,5},{7,4},{8,11},{9,10},{10,... | collective-permute-start | bytes 147464 | tf_op jit(solution)/shard_map/ppermute | solution.py:157
  13.1 2.0 %collective-permute-done.3 = bf16[3,2,4096]{2,1,0:T(2,128)(2,1)S(1)} collective-permute-done((bf16[3,2,4096]{2,1,0:T(2,128)(2,1)S(1)}, bf16[3,2,4096]{2,1,0:T(2,128)(2,1)S(1)}, u32[]{:S(2)}, u32[]{:S(2)}) %collective-permute-start.3) | collective-permute-done | bytes 49184 | tf_op jit(solution)/shard_map/ppermute | solution.py:157
  15.0 0.2 pad_maximum_fusion.held
  15.2 1.5 %collective-permute-start.4 = (bf16[3,4,4096]{2,1,0:T(4,128)(2,1)S(1)}, bf16[3,4,4096]{2,1,0:T(4,128)(2,1)S(1)}, u32[]{:S(2)}, u32[]{:S(2)}) collective-permute-start(bf16[3,4,4096]{2,1,0:T(4,128)(2,1)S(1)} %pad_maximum_fusion.held), channel_id=1, source_target_pairs={{0,1},{1,0},{2,3},{3,2},{4,5},{5,4},{6,7},{7,6},{8,9},{9,8},{10,11... | collective-permute-start | bytes 294920 | tf_op jit(solution)/shard_map/ppermute | solution.py:161
  16.7 0.9 %collective-permute-done.4.other = bf16[3,4,4096]{2,1,0:T(4,128)(2,1)S(1)} collective-permute-done((bf16[3,4,4096]{2,1,0:T(4,128)(2,1)S(1)}, bf16[3,4,4096]{2,1,0:T(4,128)(2,1)S(1)}, u32[]{:S(2)}, u32[]{:S(2)}) %collective-permute-start.4) | collective-permute-done | bytes 98336 | tf_op jit(solution)/shard_map/ppermute | solution.py:161
  17.6 0.0 copy-done.2
  17.6 1.8 %shard_map.95 = (bf16[2,4,4096]{2,1,0:T(4,128)(2,1)S(1)}, f32[2,4,4096]{2,1,0:T(4,128)S(1)}, bf16[8,4352]{1,0:T(8,128)(2,1)S(1)}, bf16[8,4352]{1,0:T(8,128)(2,1)...) custom-call(bf16[3,4,4096]{2,1,0:T(4,128)(2,1)S(1)} %pad_maximum_fusion.held, ...), custom_call_target="tpu_custom_call" | custom-call | tf_op jit(solution)/shard_map/pallas_call | solution.py:164
  19.5 0.4 %collective-permute-start.5 = (bf16[2,4,4096]{2,1,0:T(4,128)(2,1)S(1)}, bf16[2,4,4096]{2,1,0:T(4,128)(2,1)S(1)}, u32[]{:S(2)}, u32[]{:S(2)}) collective-permute-start(bf16[2,4,4096]{2,1,0:T(4,128)(2,1)S(1)} %get-tuple-element.28), channel_id=1, source_target_pairs={{0,1},{1,0},{2,3},{3,2},{4,5},{5,4},{6,7},{7,6},{8,9},{9,8},{10,11... | collective-permute-start | bytes 196616 | tf_op jit(solution)/shard_map/ppermute | solution.py:183
  19.9 0.9 %collective-permute-done.5 = bf16[2,4,4096]{2,1,0:T(4,128)(2,1)S(1)} collective-permute-done((bf16[2,4,4096]{2,1,0:T(4,128)(2,1)S(1)}, bf16[2,4,4096]{2,1,0:T(4,128)(2,1)S(1)}, u32[]{:S(2)}, u32[]{:S(2)}) %collective-permute-start.5) | collective-permute-done | bytes 65568 | tf_op jit(solution)/shard_map/ppermute | solution.py:183
  20.8 1.0 %collective-permute-start.6 = (bf16[2,2,4096]{2,1,0:T(2,128)(2,1)S(1)}, bf16[2,2,4096]{2,1,0:T(2,128)(2,1)S(1)}, u32[]{:S(2)}, u32[]{:S(2)}) collective-permute-start(bf16[2,2,4096]{2,1,0:T(2,128)(2,1)S(1)} %slice.47), channel_id=1, source_target_pairs={{0,3},{1,2},{2,1},{3,0},{4,7},{5,6},{6,5},{7,4},{8,11},{9,10},{10,... | collective-permute-start | bytes 98312 | tf_op jit(solution)/shard_map/ppermute | solution.py:183
  21.9 1.5 %collective-permute-start.7 = (bf16[8,4352]{1,0:T(8,128)(2,1)S(1)}, bf16[8,4352]{1,0:T(8,128)(2,1)S(1)}, u32[]{:S(2)}, u32[]{:S(2)}) collective-permute-start(bf16[8,4352]{1,0:T(8,128)(2,1)S(1)} %get-tuple-element.32), channel_id=1, source_target_pairs={{0,8},{8,0},{1,9},{9,1},{2,10},{10,2},{3,11},{11,3},{4,12},{12,4},... | collective-permute-start | bytes 208904 | tf_op jit(solution)/shard_map/ppermute | solution.py:188
  23.4 0.8 %collective-permute-done.6 = bf16[2,2,4096]{2,1,0:T(2,128)(2,1)S(1)} collective-permute-done((bf16[2,2,4096]{2,1,0:T(2,128)(2,1)S(1)}, bf16[2,2,4096]{2,1,0:T(2,128)(2,1)S(1)}, u32[]{:S(2)}, u32[]{:S(2)}) %collective-permute-start.6) | collective-permute-done | bytes 32800 | tf_op jit(solution)/shard_map/ppermute | solution.py:183
  24.3 2.2 %collective-permute-start.8 = (bf16[2,1,4096]{2,1,0:T(2,128)(2,1)S(1)}, bf16[2,1,4096]{2,1,0:T(2,128)(2,1)S(1)}, u32[]{:S(2)}, u32[]{:S(2)}) collective-permute-start(bf16[2,1,4096]{2,1,0:T(2,128)(2,1)S(1)} %slice.48), channel_id=1, source_target_pairs={{0,5},{1,4},{2,7},{3,6},{4,1},{5,0},{6,3},{7,2},{8,13},{9,12},{10,... | collective-permute-start | bytes 49160 | tf_op jit(solution)/shard_map/ppermute | solution.py:183
  26.5 0.0 collective-permute-done.7
  26.5 1.1 %convolution_convert_fusion = bf16[128,2048]{1,0:T(8,128)(2,1)} fusion(bf16[16,4352]{1,0:T(8,128)(2,1)S(1)} %constant_dynamic-update-slice_fusion), kind=kOutput, calls=%fused_computation | convolution fusion | flops 8650752 | bytes 593920 | tf_op jit(solution)/shard_map/dot_general | solution.py:48
  27.6 1.1 %convolution_convert_fusion.1 = bf16[2048,128]{1,0:T(8,128)(2,1)} fusion(bf16[16,4352]{1,0:T(8,128)(2,1)S(1)} %constant_dynamic-update-slice_fusion), kind=kOutput, calls=%fused_computation.1 | convolution fusion | flops 8650752 | bytes 593920 | tf_op jit(solution)/shard_map/dot_general | solution.py:48
  28.8 0.0 collective-permute-done.8.came
  28.8 0.7 %shard_map.96 = (bf16[1,4096]{1,0:T(2,128)(2,1)}, bf16[1,4096]{1,0:T(2,128)(2,1)}) custom-call(f32[2,2,4096]{2,1,0:T(2,128)S(1)} %convert_add_fusion.1.part, bf16[2,1,4096]{2,1,0:T(2,128)(2,1)S(1)} %collective-permute-done.8.came, f32[1,4096]{1,0:T(1,128)S(1)} %copy-done.2, f32[3,1,4096]{2,1,0:T(1,128)S(1)} %get-tuple-element.34.tail, ...), custom_call_target="tpu_custom_call" | custom-call | tf_op jit(solution)/shard_map/pallas_call | solution.py:194
  (9 shorter events, 0.1 us)
Async XLA Ops:
  0.6 4.1 %collective-permute-start = (bf16[1,4096]{1,0:T(2,128)(2,1)}, bf16[1,4096]{1,0:T(2,128)(2,1)S(1)}, u32[]{:S(2)}, u32[]{:S(2)}) collective-permute-start(bf16[1,4096]{1,0:T(2,128)(2,1)} %bitcast.31), channel_id=1, source_target_pairs={{0,17},{1,16},{2,19},{3,18},{4,21},{5,20},{6,23},{7,22},{8,25},{9,... | collective-permute-start | bytes 24584 | tf_op jit(solution)/shard_map/ppermute | solution.py:150
  3.1 3.4 %collective-permute-start.1 = (bf16[1,4096]{1,0:T(2,128)(2,1)}, bf16[1,4096]{1,0:T(2,128)(2,1)S(1)}, u32[]{:S(2)}, u32[]{:S(2)}) collective-permute-start(bf16[1,4096]{1,0:T(2,128)(2,1)} %bitcast.32), channel_id=1, source_target_pairs={{0,17},{1,16},{2,19},{3,18},{4,21},{5,20},{6,23},{7,22},{8,25},{9,... | collective-permute-start | bytes 24584 | tf_op jit(solution)/shard_map/ppermute | solution.py:151
  3.2 1.2 %copy-start = (bf16[1,4096,128]{2,1,0:T(8,128)(2,1)S(1)}, bf16[1,4096,128]{2,1,0:T(8,128)(2,1)}, u32[]{:S(2)}) copy-start(bf16[1,4096,128]{2,1,0:T(8,128)(2,1)} %param.10) | copy-start | bytes 3145732
  4.4 2.1 %copy-start.3 = (bf16[1,1,1,4096]{3,2,1,0:T(2,128)(2,1)S(1)}, bf16[1,1,1,4096]{3,2,1,0:T(2,128)(2,1)}, u32[]{:S(2)}) copy-start(bf16[1,1,1,4096]{3,2,1,0:T(2,128)(2,1)} %param.8) | copy-start | bytes 24580
  4.4 5.1 %copy-start.1 = (bf16[1,128,4096]{2,1,0:T(8,128)(2,1)S(1)}, bf16[1,128,4096]{2,1,0:T(8,128)(2,1)}, u32[]{:S(2)}) copy-start(bf16[1,128,4096]{2,1,0:T(8,128)(2,1)} %param.11) | copy-start | bytes 3145732
  6.5 4.7 %collective-permute-start.2 = (bf16[3,1,4096]{2,1,0:T(2,128)(2,1)S(1)}, bf16[3,1,4096]{2,1,0:T(2,128)(2,1)S(1)}, u32[]{:S(2)}, u32[]{:S(2)}) collective-permute-start(bf16[3,1,4096]{2,1,0:T(2,128)(2,1)S(1)} %pad_maximum_fusion.1), channel_id=1, source_target_pairs={{0,5},{1,4},{2,7},{3,6},{4,1},{5,0},{6,3},{7,2},{8,13},{9,12},{10,... | collective-permute-start | bytes 73736 | tf_op jit(solution)/shard_map/ppermute | solution.py:157
  11.4 6.3 %copy-start.2 = (f32[1,4096]{1,0:T(1,128)S(1)}, f32[1,4096]{1,0:T(1,128)}, u32[]{:S(2)}) copy-start(f32[1,4096]{1,0:T(1,128)} %gain.3) | copy-start | bytes 49156
  11.4 3.6 %collective-permute-start.3 = (bf16[3,2,4096]{2,1,0:T(2,128)(2,1)S(1)}, bf16[3,2,4096]{2,1,0:T(2,128)(2,1)S(1)}, u32[]{:S(2)}, u32[]{:S(2)}) collective-permute-start(bf16[3,2,4096]{2,1,0:T(2,128)(2,1)S(1)} %pad_maximum_fusion.2), channel_id=1, source_target_pairs={{0,3},{1,2},{2,1},{3,0},{4,7},{5,6},{6,5},{7,4},{8,11},{9,10},{10,... | collective-permute-start | bytes 147464 | tf_op jit(solution)/shard_map/ppermute | solution.py:157
  15.2 2.4 %collective-permute-start.4 = (bf16[3,4,4096]{2,1,0:T(4,128)(2,1)S(1)}, bf16[3,4,4096]{2,1,0:T(4,128)(2,1)S(1)}, u32[]{:S(2)}, u32[]{:S(2)}) collective-permute-start(bf16[3,4,4096]{2,1,0:T(4,128)(2,1)S(1)} %pad_maximum_fusion.held), channel_id=1, source_target_pairs={{0,1},{1,0},{2,3},{3,2},{4,5},{5,4},{6,7},{7,6},{8,9},{9,8},{10,11... | collective-permute-start | bytes 294920 | tf_op jit(solution)/shard_map/ppermute | solution.py:161
  19.5 1.3 %collective-permute-start.5 = (bf16[2,4,4096]{2,1,0:T(4,128)(2,1)S(1)}, bf16[2,4,4096]{2,1,0:T(4,128)(2,1)S(1)}, u32[]{:S(2)}, u32[]{:S(2)}) collective-permute-start(bf16[2,4,4096]{2,1,0:T(4,128)(2,1)S(1)} %get-tuple-element.28), channel_id=1, source_target_pairs={{0,1},{1,0},{2,3},{3,2},{4,5},{5,4},{6,7},{7,6},{8,9},{9,8},{10,11... | collective-permute-start | bytes 196616 | tf_op jit(solution)/shard_map/ppermute | solution.py:183
  20.8 3.4 %collective-permute-start.6 = (bf16[2,2,4096]{2,1,0:T(2,128)(2,1)S(1)}, bf16[2,2,4096]{2,1,0:T(2,128)(2,1)S(1)}, u32[]{:S(2)}, u32[]{:S(2)}) collective-permute-start(bf16[2,2,4096]{2,1,0:T(2,128)(2,1)S(1)} %slice.47), channel_id=1, source_target_pairs={{0,3},{1,2},{2,1},{3,0},{4,7},{5,6},{6,5},{7,4},{8,11},{9,10},{10,... | collective-permute-start | bytes 98312 | tf_op jit(solution)/shard_map/ppermute | solution.py:183
  21.9 4.6 %collective-permute-start.7 = (bf16[8,4352]{1,0:T(8,128)(2,1)S(1)}, bf16[8,4352]{1,0:T(8,128)(2,1)S(1)}, u32[]{:S(2)}, u32[]{:S(2)}) collective-permute-start(bf16[8,4352]{1,0:T(8,128)(2,1)S(1)} %get-tuple-element.32), channel_id=1, source_target_pairs={{0,8},{8,0},{1,9},{9,1},{2,10},{10,2},{3,11},{11,3},{4,12},{12,4},... | collective-permute-start | bytes 208904 | tf_op jit(solution)/shard_map/ppermute | solution.py:188
  24.3 4.4 %collective-permute-start.8 = (bf16[2,1,4096]{2,1,0:T(2,128)(2,1)S(1)}, bf16[2,1,4096]{2,1,0:T(2,128)(2,1)S(1)}, u32[]{:S(2)}, u32[]{:S(2)}) collective-permute-start(bf16[2,1,4096]{2,1,0:T(2,128)(2,1)S(1)} %slice.48), channel_id=1, source_target_pairs={{0,5},{1,4},{2,7},{3,6},{4,1},{5,0},{6,3},{7,2},{8,13},{9,12},{10,... | collective-permute-start | bytes 49160 | tf_op jit(solution)/shard_map/ppermute | solution.py:183

commit v3 on v2

--- a/solution.py
+++ b/solution.py
@@ -126,11 +126,33 @@
     )(weights)
 
 
+def outer_kernel(chunks, own, far, first_out, second_out, pair, first, second, sems):
+    rows, (mid, units) = own.shape[0], first.shape
+    pair[:rows] = own[...]
+    pair[rows:] = far[...]
+    value = pair[:, 2 * mid : 2 * mid + units]
+    d_hidden = pair[:, 2 * mid + units :]
+    copies = []
+    step = mid // chunks
+    for i in range(chunks):
+        part = slice(i * step, (i + 1) * step)
+        first[part] = dot(pair[:, part], d_hidden, (0, 0)).astype(first.dtype)
+        copies.append(pltpu.make_async_copy(first.at[part], first_out.at[part], sems.at[0, i]))
+        copies[-1].start()
+    for i in range(chunks):
+        part = slice(i * step, (i + 1) * step)
+        second[:, part] = dot(value, pair[:, mid + i * step : mid + (i + 1) * step], (0, 0)).astype(second.dtype)
+        copies.append(pltpu.make_async_copy(second.at[:, part], second_out.at[:, part], sems.at[1, i]))
+        copies[-1].start()
+    for copy in copies:
+        copy.wait()
+
+
 def tail_kernel(rows, part, came, gain, tail, tail_rstd, fwd_out, bwd_out):
     f32 = jnp.float32
-    branch = part[0, :rows] + came[0].astype(f32)
+    branch = part[0, :rows] + came[:rows].astype(f32)
     fwd_out[...] = (tail[0] + branch).astype(fwd_out.dtype)
-    scaled = (part[1, :rows] + came[1].astype(f32)) * gain[...]
+    scaled = (part[1, :rows] + came[rows:].astype(f32)) * gain[...]
     nhat = tail[2]
     d_input = tail_rstd[:, :1] * (
         scaled
@@ -154,7 +176,8 @@
     w_second = loaded(w_out[0], 4)
     held = jnp.stack([fwd_in, bwd_in, stash[0, 0]])
     for mask in masks:
-        other = lax.ppermute(held, "dp", xor_pairs(count, mask))
+        flat = held.reshape(-1, width) if held.shape[1] == 1 else held
+        other = lax.ppermute(flat, "dp", xor_pairs(count, mask)).reshape(held.shape)
         if mask == masks[0]:
             other, w_second = lax.optimization_barrier((other, w_second))
         held = jnp.concatenate([held, other], axis=1)
@@ -180,16 +203,31 @@
         if part is not None:
             half = part.shape[1] // 2
             send, keep = part[:, half:].astype(jnp.bfloat16), part[:, :half]
-        came = lax.ppermute(send, "dp", xor_pairs(count, mask))
-        if mask != (masks or [1])[0]:
+        last = mask == (masks or [1])[0]
+        came = lax.ppermute(send.reshape(-1, width) if last else send, "dp", xor_pairs(count, mask))
+        if not last:
             part = keep + came.astype(jnp.float32)
             if mask == 1:
                 part, away = lax.optimization_barrier((part, away))
     far = lax.ppermute(away, "mirror", xor_pairs(mirrors, 1))
-    pair = jnp.concatenate([own, far], axis=0)
     mid = width // 2
-    grad_first = dot(pair[:, :mid], pair[:, 2 * mid + units :], (0, 0)).astype(jnp.bfloat16)
-    grad_second = dot(pair[:, 2 * mid : 2 * mid + units], pair[:, mid : 2 * mid], (0, 0)).astype(jnp.bfloat16)
+    grad_first, grad_second = pl.pallas_call(
+        functools.partial(outer_kernel, 8),
+        out_shape=(
+            jax.ShapeDtypeStruct((mid, units), jnp.bfloat16),
+            jax.ShapeDtypeStruct((units, mid), jnp.bfloat16),
+        ),
+        in_specs=[VMEM] * 2,
+        out_specs=[pl.BlockSpec(memory_space=pl.ANY)] * 2,
+        scratch_shapes=[
+            pltpu.VMEM((2 * own.shape[0], own.shape[1]), jnp.bfloat16),
+            pltpu.VMEM((mid, units), jnp.bfloat16),
+            pltpu.VMEM((units, mid), jnp.bfloat16),
+            pltpu.SemaphoreType.DMA((2, 8)),
+        ],
+        compiler_params=pltpu.CompilerParams(vmem_limit_bytes=max(6 << 20, 24 * own.size)),
+        cost_estimate=pl.CostEstimate(flops=0, bytes_accessed=8 * mid * units, transcendentals=0),
+    )(own, far)
     part, grad_first, grad_second = lax.optimization_barrier((part, grad_first, grad_second))
     fwd_out, bwd_out = pl.pallas_call(
         functools.partial(tail_kernel, rows),

time: 29.7 us -> 28.4 us (0.956)
  matrix products: 2.23 us -> 0 us
  Pallas kernels: 2.78 us -> 4.08 us
  waiting for transfers between devices: 8.21 us -> 7.53 us
    dot_general x2 -> x0, matrix products: 2.23 us -> none  [dot(): lax.dot_general(left, right, ((contract[:1], contract[1:]), ((), ())), pr...]
    pallas_call x0 -> x1, Pallas kernels: none -> 1.31 us  [on_device(): pl.pallas_call(functools.partial(outer_kernel, 8), out_shape=(jax.ShapeDt...]
    ppermute x5, starting transfers between devices: 8.26 us -> 9.29 us  [the longest x3 4.66 us: on_device(): lax.ppermute(send.reshape(-1, width) if last else send, 'dp', xor_pairs(c...]
    ppermute x1, starting transfers between devices: 1.5 us -> 0.51 us  [on_device(): other = lax.ppermute(held, 'dp', xor_pairs(count, 1))]
    ppermute x5, waiting for transfers between devices: 5.32 us -> 4.64 us  [the longest x2 3.36 us: on_device(): other = lax.ppermute(flat, 'dp', xor_pairs(count, mask)).reshape(held.shape)]
  transfers between devices with their start and end apart: 9 -> 9, of which waited for: 7 -> 8; matrix products, arithmetic and copies ran while one was open for 8% -> 0% of each run, Pallas kernels for 1% -> 5%
where the time goes in v3:
time: 28.4 us; the launch traced here: 28.2 us
  starting transfers between devices  13.9 us (49%)
  waiting for transfers between devices  7.53 us (27%)
  Pallas kernels  4.08 us (14%)
  local copies, waits for them, and re-layouts  1.48 us (5%)
  between operations  0.75 us (3%)
  other arithmetic  0.55 us (2%)
    ppermute x3, starting transfers between devices, on_device(): lax.ppermute(send.reshape(-1, width) if last else send, 'dp', xor_pairs(c...  4.66 us
    ppermute x2, starting transfers between devices, on_device(): other = lax.ppermute(flat, 'dp', xor_pairs(count, mask)).reshape(held.shape)  4.63 us
    ppermute x2, waiting for transfers between devices, on_device(): other = lax.ppermute(flat, 'dp', xor_pairs(count, mask)).reshape(held.shape)  3.36 us
    ppermute x1, starting transfers between devices, on_device(): lax.ppermute(sent_fwd[0, 0], AXES, relay_pairs(sections, mirrors, count,...  2.44 us
    pallas_call x1, Pallas kernels, on_device(): pl.pallas_call(functools.partial(block_kernel, rows), out_shape=(jax.Shap...  1.8 us
    ppermute x1, waiting for transfers between devices, on_device(): lax.ppermute(sent_bwd[0, 0], AXES, relay_pairs(sections, mirrors, count,...  1.72 us
    ppermute x1, starting transfers between devices, on_device(): far = lax.ppermute(away, 'mirror', xor_pairs(mirrors, 1))  1.54 us
    pallas_call x1, Pallas kernels, on_device(): pl.pallas_call(functools.partial(outer_kernel, 8), out_shape=(jax.ShapeDt...  1.31 us
  transfers between devices with their start and end apart: 9, of which 8 were waited for; matrix products, arithmetic and copies ran while one was open for 0% of the time, Pallas kernels for 5%

profile of v3, /device:TPU:0, one launch (start us, length us, event | category | flops | bytes accessed | tf_op | source)
XLA Modules:
  0.0 28.2 jit_solution(874654618148100227)
XLA Ops:
  0.6 2.4 %collective-permute-start = (bf16[1,4096]{1,0:T(2,128)(2,1)}, bf16[1,4096]{1,0:T(2,128)(2,1)S(1)}, u32[]{:S(2)}, u32[]{:S(2)}) collective-permute-start(bf16[1,4096]{1,0:T(2,128)(2,1)} %bitcast.32), channel_id=1, source_target_pairs={{0,17},{1,16},{2,19},{3,18},{4,21},{5,20},{6,23},{7,22},{8,25},{9,... | collective-permute-start | bytes 24584 | tf_op jit(solution)/shard_map/ppermute | solution.py:172
  3.1 0.1 collective-permute-start.1
  3.2 1.2 %copy-done = bf16[1,4096,128]{2,1,0:T(8,128)(2,1)S(1)} copy-done((bf16[1,4096,128]{2,1,0:T(8,128)(2,1)S(1)}, bf16[1,4096,128]{2,1,0:T(8,128)(2,1)}, u32[]{:S(2)}) %copy-start) | copy-done | bytes 1048600
  4.4 0.1 shard_map.93.w_in
  4.5 0.2 collective-permute-done
  4.7 1.7 %collective-permute-done.1 = bf16[1,4096]{1,0:T(2,128)(2,1)S(1)} collective-permute-done((bf16[1,4096]{1,0:T(2,128)(2,1)}, bf16[1,4096]{1,0:T(2,128)(2,1)S(1)}, u32[]{:S(2)}, u32[]{:S(2)}) %collective-permute-start.1) | collective-permute-done | bytes 8224 | tf_op jit(solution)/shard_map/ppermute | solution.py:173
  6.5 0.0 copy-done.3
  6.5 0.1 pad_maximum_fusion.1
  6.6 2.9 %collective-permute-start.2 = (bf16[3,4096]{1,0:T(4,128)(2,1)S(1)}, bf16[3,4096]{1,0:T(4,128)(2,1)S(1)}, u32[]{:S(2)}, u32[]{:S(2)}) collective-permute-start(bf16[3,4096]{1,0:T(4,128)(2,1)S(1)} %bitcast.28), channel_id=1, source_target_pairs={{0,5},{1,4},{2,7},{3,6},{4,1},{5,0},{6,3},{7,2},{8,13},{9,12},{10,... | collective-permute-start | bytes 73736 | tf_op jit(solution)/shard_map/ppermute | solution.py:180
  9.5 0.1 shard_map.94.w_out
  9.6 1.5 %collective-permute-done.2 = bf16[3,4096]{1,0:T(4,128)(2,1)S(1)} collective-permute-done((bf16[3,4096]{1,0:T(4,128)(2,1)S(1)}, bf16[3,4096]{1,0:T(4,128)(2,1)S(1)}, u32[]{:S(2)}, u32[]{:S(2)}) %collective-permute-start.2) | collective-permute-done | bytes 24608 | tf_op jit(solution)/shard_map/ppermute | solution.py:180
  11.2 0.1 pad_maximum_fusion.2
  11.3 0.0 copy-start.2
  11.3 1.7 %collective-permute-start.3 = (bf16[3,2,4096]{2,1,0:T(2,128)(2,1)S(1)}, bf16[3,2,4096]{2,1,0:T(2,128)(2,1)S(1)}, u32[]{:S(2)}, u32[]{:S(2)}) collective-permute-start(bf16[3,2,4096]{2,1,0:T(2,128)(2,1)S(1)} %pad_maximum_fusion.2), channel_id=1, source_target_pairs={{0,3},{1,2},{2,1},{3,0},{4,7},{5,6},{6,5},{7,4},{8,11},{9,10},{10,... | collective-permute-start | bytes 147464 | tf_op jit(solution)/shard_map/ppermute | solution.py:180
  13.0 1.9 %collective-permute-done.3 = bf16[3,2,4096]{2,1,0:T(2,128)(2,1)S(1)} collective-permute-done((bf16[3,2,4096]{2,1,0:T(2,128)(2,1)S(1)}, bf16[3,2,4096]{2,1,0:T(2,128)(2,1)S(1)}, u32[]{:S(2)}, u32[]{:S(2)}) %collective-permute-start.3) | collective-permute-done | bytes 49184 | tf_op jit(solution)/shard_map/ppermute | solution.py:180
  14.9 0.2 pad_maximum_fusion.held
  15.1 0.5 %collective-permute-start.4 = (bf16[3,4,4096]{2,1,0:T(4,128)(2,1)S(1)}, bf16[3,4,4096]{2,1,0:T(4,128)(2,1)S(1)}, u32[]{:S(2)}, u32[]{:S(2)}) collective-permute-start(bf16[3,4,4096]{2,1,0:T(4,128)(2,1)S(1)} %pad_maximum_fusion.held), channel_id=1, source_target_pairs={{0,1},{1,0},{2,3},{3,2},{4,5},{5,4},{6,7},{7,6},{8,9},{9,8},{10,11... | collective-permute-start | bytes 294920 | tf_op jit(solution)/shard_map/ppermute | solution.py:184
  15.6 0.9 %collective-permute-done.4.other = bf16[3,4,4096]{2,1,0:T(4,128)(2,1)S(1)} collective-permute-done((bf16[3,4,4096]{2,1,0:T(4,128)(2,1)S(1)}, bf16[3,4,4096]{2,1,0:T(4,128)(2,1)S(1)}, u32[]{:S(2)}, u32[]{:S(2)}) %collective-permute-start.4) | collective-permute-done | bytes 98336 | tf_op jit(solution)/shard_map/ppermute | solution.py:184
  16.5 1.8 %shard_map.95 = (bf16[2,4,4096]{2,1,0:T(4,128)(2,1)S(1)}, f32[2,4,4096]{2,1,0:T(4,128)S(1)}, bf16[8,4352]{1,0:T(8,128)(2,1)S(1)}, bf16[8,4352]{1,0:T(8,128)(2,1)...) custom-call(bf16[3,4,4096]{2,1,0:T(4,128)(2,1)S(1)} %pad_maximum_fusion.held, ...), custom_call_target="tpu_custom_call" | custom-call | tf_op jit(solution)/shard_map/pallas_call | solution.py:187
  18.3 0.1 copy.22
  18.4 0.4 %collective-permute-start.5 = (bf16[2,4,4096]{2,0,1:T(2,128)(2,1)S(1)}, bf16[2,4,4096]{2,0,1:T(2,128)(2,1)S(1)}, u32[]{:S(2)}, u32[]{:S(2)}) collective-permute-start(bf16[2,4,4096]{2,0,1:T(2,128)(2,1)S(1)} %copy.22), channel_id=1, source_target_pairs={{0,1},{1,0},{2,3},{3,2},{4,5},{5,4},{6,7},{7,6},{8,9},{9,8},{10,11... | collective-permute-start | bytes 196616 | tf_op jit(solution)/shard_map/ppermute | solution.py:207
  18.8 0.9 %collective-permute-done.5 = bf16[2,4,4096]{2,0,1:T(2,128)(2,1)S(1)} collective-permute-done((bf16[2,4,4096]{2,0,1:T(2,128)(2,1)S(1)}, bf16[2,4,4096]{2,0,1:T(2,128)(2,1)S(1)}, u32[]{:S(2)}, u32[]{:S(2)}) %collective-permute-start.5) | collective-permute-done | bytes 65568 | tf_op jit(solution)/shard_map/ppermute | solution.py:207
  19.7 0.1 copy_add_fusion
  19.9 1.6 %collective-permute-start.6 = (bf16[2,2,4096]{2,0,1:T(2,128)(2,1)S(1)}, bf16[2,2,4096]{2,0,1:T(2,128)(2,1)S(1)}, u32[]{:S(2)}, u32[]{:S(2)}) collective-permute-start(bf16[2,2,4096]{2,0,1:T(2,128)(2,1)S(1)} %slice.21), channel_id=1, source_target_pairs={{0,3},{1,2},{2,1},{3,0},{4,7},{5,6},{6,5},{7,4},{8,11},{9,10},{10,... | collective-permute-start | bytes 98312 | tf_op jit(solution)/shard_map/ppermute | solution.py:207
  21.5 1.5 %collective-permute-start.7 = (bf16[8,4352]{1,0:T(8,128)(2,1)S(1)}, bf16[8,4352]{1,0:T(8,128)(2,1)S(1)}, u32[]{:S(2)}, u32[]{:S(2)}) collective-permute-start(bf16[8,4352]{1,0:T(8,128)(2,1)S(1)} %get-tuple-element.34), channel_id=1, source_target_pairs={{0,8},{8,0},{1,9},{9,1},{2,10},{10,2},{3,11},{11,3},{4,12},{12,4},... | collective-permute-start | bytes 208904 | tf_op jit(solution)/shard_map/ppermute | solution.py:212
  23.1 0.3 collective-permute-done.6
  23.4 2.6 %collective-permute-start.8 = (bf16[2,4096]{1,0:T(2,128)(2,1)S(1)}, bf16[2,4096]{1,0:T(2,128)(2,1)S(1)}, u32[]{:S(2)}, u32[]{:S(2)}) collective-permute-start(bf16[2,4096]{1,0:T(2,128)(2,1)S(1)} %fusion), channel_id=1, source_target_pairs={{0,5},{1,4},{2,7},{3,6},{4,1},{5,0},{6,3},{7,2},{8,13},{9,12},{10,... | collective-permute-start | bytes 49160 | tf_op jit(solution)/shard_map/ppermute | solution.py:207
  26.0 0.0 collective-permute-done.7.far
  26.0 1.3 %shard_map.96 = (bf16[2048,128]{1,0:T(8,128)(2,1)}, bf16[128,2048]{1,0:T(8,128)(2,1)}) custom-call(bf16[8,4352]{1,0:T(8,128)(2,1)S(1)} %get-tuple-element.33.own, bf16[8,4352]{1,0:T(8,128)(2,1)S(1)} %collective-permute-done.7.far), custom_call_target="tpu_custom_call" | custom-call | bytes 2097152 | tf_op jit(solution)/shard_map/pallas_call | solution.py:214
  27.3 0.1 copy.24.part
  27.4 0.1 collective-permute-done.8.came
  27.5 0.7 %shard_map.97 = (bf16[1,4096]{1,0:T(2,128)(2,1)}, bf16[1,4096]{1,0:T(2,128)(2,1)}) custom-call(f32[2,2,4096]{2,1,0:T(2,128)S(1)} %copy.24.part, bf16[2,4096]{1,0:T(2,128)(2,1)S(1)} %collective-permute-done.8.came, f32[1,4096]{1,0:T(1,128)S(1)} %copy-done.2, f32[3,1,4096]{2,1,0:T(1,128)S(1)} %get-tuple-element.38.tail, f32[1,128]{1,0:T(1,128)S(1)} %get-tuple-element.39.tail_rstd), custom_call_target="tpu_custom_call" | custom-call | tf_op jit(solution)/shard_map/pallas_call | solution.py:232
  (10 shorter events, 0.2 us)
Async XLA Ops:
  0.6 4.1 %collective-permute-start = (bf16[1,4096]{1,0:T(2,128)(2,1)}, bf16[1,4096]{1,0:T(2,128)(2,1)S(1)}, u32[]{:S(2)}, u32[]{:S(2)}) collective-permute-start(bf16[1,4096]{1,0:T(2,128)(2,1)} %bitcast.32), channel_id=1, source_target_pairs={{0,17},{1,16},{2,19},{3,18},{4,21},{5,20},{6,23},{7,22},{8,25},{9,... | collective-permute-start | bytes 24584 | tf_op jit(solution)/shard_map/ppermute | solution.py:172
  3.1 3.4 %collective-permute-start.1 = (bf16[1,4096]{1,0:T(2,128)(2,1)}, bf16[1,4096]{1,0:T(2,128)(2,1)S(1)}, u32[]{:S(2)}, u32[]{:S(2)}) collective-permute-start(bf16[1,4096]{1,0:T(2,128)(2,1)} %bitcast.33), channel_id=1, source_target_pairs={{0,17},{1,16},{2,19},{3,18},{4,21},{5,20},{6,23},{7,22},{8,25},{9,... | collective-permute-start | bytes 24584 | tf_op jit(solution)/shard_map/ppermute | solution.py:173
  3.2 1.2 %copy-start = (bf16[1,4096,128]{2,1,0:T(8,128)(2,1)S(1)}, bf16[1,4096,128]{2,1,0:T(8,128)(2,1)}, u32[]{:S(2)}) copy-start(bf16[1,4096,128]{2,1,0:T(8,128)(2,1)} %param.10) | copy-start | bytes 3145732
  4.4 2.1 %copy-start.3 = (bf16[1,1,1,4096]{3,2,1,0:T(2,128)(2,1)S(1)}, bf16[1,1,1,4096]{3,2,1,0:T(2,128)(2,1)}, u32[]{:S(2)}) copy-start(bf16[1,1,1,4096]{3,2,1,0:T(2,128)(2,1)} %param.8) | copy-start | bytes 24580
  4.4 5.1 %copy-start.1 = (bf16[1,128,4096]{2,1,0:T(8,128)(2,1)S(1)}, bf16[1,128,4096]{2,1,0:T(8,128)(2,1)}, u32[]{:S(2)}) copy-start(bf16[1,128,4096]{2,1,0:T(8,128)(2,1)} %param.11) | copy-start | bytes 3145732
  6.6 4.5 %collective-permute-start.2 = (bf16[3,4096]{1,0:T(4,128)(2,1)S(1)}, bf16[3,4096]{1,0:T(4,128)(2,1)S(1)}, u32[]{:S(2)}, u32[]{:S(2)}) collective-permute-start(bf16[3,4096]{1,0:T(4,128)(2,1)S(1)} %bitcast.28), channel_id=1, source_target_pairs={{0,5},{1,4},{2,7},{3,6},{4,1},{5,0},{6,3},{7,2},{8,13},{9,12},{10,... | collective-permute-start | bytes 73736 | tf_op jit(solution)/shard_map/ppermute | solution.py:180
  11.3 5.2 %copy-start.2 = (f32[1,4096]{1,0:T(1,128)S(1)}, f32[1,4096]{1,0:T(1,128)}, u32[]{:S(2)}) copy-start(f32[1,4096]{1,0:T(1,128)} %gain.3) | copy-start | bytes 49156
  11.3 3.6 %collective-permute-start.3 = (bf16[3,2,4096]{2,1,0:T(2,128)(2,1)S(1)}, bf16[3,2,4096]{2,1,0:T(2,128)(2,1)S(1)}, u32[]{:S(2)}, u32[]{:S(2)}) collective-permute-start(bf16[3,2,4096]{2,1,0:T(2,128)(2,1)S(1)} %pad_maximum_fusion.2), channel_id=1, source_target_pairs={{0,3},{1,2},{2,1},{3,0},{4,7},{5,6},{6,5},{7,4},{8,11},{9,10},{10,... | collective-permute-start | bytes 147464 | tf_op jit(solution)/shard_map/ppermute | solution.py:180
  15.1 1.5 %collective-permute-start.4 = (bf16[3,4,4096]{2,1,0:T(4,128)(2,1)S(1)}, bf16[3,4,4096]{2,1,0:T(4,128)(2,1)S(1)}, u32[]{:S(2)}, u32[]{:S(2)}) collective-permute-start(bf16[3,4,4096]{2,1,0:T(4,128)(2,1)S(1)} %pad_maximum_fusion.held), channel_id=1, source_target_pairs={{0,1},{1,0},{2,3},{3,2},{4,5},{5,4},{6,7},{7,6},{8,9},{9,8},{10,11... | collective-permute-start | bytes 294920 | tf_op jit(solution)/shard_map/ppermute | solution.py:184
  18.4 1.3 %collective-permute-start.5 = (bf16[2,4,4096]{2,0,1:T(2,128)(2,1)S(1)}, bf16[2,4,4096]{2,0,1:T(2,128)(2,1)S(1)}, u32[]{:S(2)}, u32[]{:S(2)}) collective-permute-start(bf16[2,4,4096]{2,0,1:T(2,128)(2,1)S(1)} %copy.22), channel_id=1, source_target_pairs={{0,1},{1,0},{2,3},{3,2},{4,5},{5,4},{6,7},{7,6},{8,9},{9,8},{10,11... | collective-permute-start | bytes 196616 | tf_op jit(solution)/shard_map/ppermute | solution.py:207
  19.9 3.4 %collective-permute-start.6 = (bf16[2,2,4096]{2,0,1:T(2,128)(2,1)S(1)}, bf16[2,2,4096]{2,0,1:T(2,128)(2,1)S(1)}, u32[]{:S(2)}, u32[]{:S(2)}) collective-permute-start(bf16[2,2,4096]{2,0,1:T(2,128)(2,1)S(1)} %slice.21), channel_id=1, source_target_pairs={{0,3},{1,2},{2,1},{3,0},{4,7},{5,6},{6,5},{7,4},{8,11},{9,10},{10,... | collective-permute-start | bytes 98312 | tf_op jit(solution)/shard_map/ppermute | solution.py:207
  21.5 4.5 %collective-permute-start.7 = (bf16[8,4352]{1,0:T(8,128)(2,1)S(1)}, bf16[8,4352]{1,0:T(8,128)(2,1)S(1)}, u32[]{:S(2)}, u32[]{:S(2)}) collective-permute-start(bf16[8,4352]{1,0:T(8,128)(2,1)S(1)} %get-tuple-element.34), channel_id=1, source_target_pairs={{0,8},{8,0},{1,9},{9,1},{2,10},{10,2},{3,11},{11,3},{4,12},{12,4},... | collective-permute-start | bytes 208904 | tf_op jit(solution)/shard_map/ppermute | solution.py:212
  23.4 4.1 %collective-permute-start.8 = (bf16[2,4096]{1,0:T(2,128)(2,1)S(1)}, bf16[2,4096]{1,0:T(2,128)(2,1)S(1)}, u32[]{:S(2)}, u32[]{:S(2)}) collective-permute-start(bf16[2,4096]{1,0:T(2,128)(2,1)S(1)} %fusion), channel_id=1, source_target_pairs={{0,5},{1,4},{2,7},{3,6},{4,1},{5,0},{6,3},{7,2},{8,13},{9,12},{10,... | collective-permute-start | bytes 49160 | tf_op jit(solution)/shard_map/ppermute | solution.py:207

commit v4 on v3

--- a/solution.py
+++ b/solution.py
@@ -48,57 +48,59 @@
     return lax.dot_general(left, right, ((contract[:1], contract[1:]), ((), ())), preferred_element_type=jnp.float32)
 
 
-def block_kernel(rows, held, other, gain, w_in, w_out, send, keep, own_out, far_out, tail, tail_rstd):
+def block_kernel(rows, held, other, gain, wide, tall, send, keep, full, leaving):
     half, width = held.shape[1], held.shape[2]
+    count, units = 2 * half, wide.shape[1] // 2
     f32, bf16 = jnp.float32, jnp.bfloat16
 
     def joined(first, second):
         return jnp.concatenate([first.astype(f32), second.astype(f32)], axis=0)
 
-    fin = joined(other[0], held[0])
-    cotan = joined(other[1], held[1])
-    stash = joined(held[2], other[2])
-    nhat_fwd, _ = norm_rows(fin)
-    nhat_bwd, rstd_bwd = norm_rows(stash)
+    cotan = joined(other[1], held[1]).astype(bf16)
+    d_acted = dot(cotan, wide[:, :units], (1, 0))
+    nhat_fwd, _ = norm_rows(joined(other[0], held[0]))
+    nhat_bwd, _ = norm_rows(joined(held[2], other[2]))
     normed_bwd = nhat_bwd * gain[...]
-    both = jnp.concatenate([nhat_fwd * gain[...], normed_bwd], axis=0).astype(bf16)
-    hidden = dot(both, w_in[...], (1, 0))
-    cotan_low = cotan.astype(bf16)
-    d_acted = dot(cotan_low, w_out[...], (1, 1))
+    entering = jnp.concatenate([nhat_fwd * gain[...], normed_bwd], axis=0).astype(bf16)
+    hidden = dot(entering, wide[:, units:], (1, 0))
     value, slope = gelu_pair(hidden)
-    value_low = value.astype(bf16)
-    d_hidden = (d_acted * slope[2 * half :]).astype(bf16)
-    part_bwd = dot(d_hidden, w_in[...], (1, 1))
-    part_fwd = dot(value_low[: 2 * half], w_out[...], (1, 0))
-    keep[0] = part_fwd[:half]
-    keep[1] = part_bwd[:half]
-    send[0] = part_fwd[half:].astype(bf16)
-    send[1] = part_bwd[half:].astype(bf16)
-    tail[0] = fin[:rows]
-    tail[1] = cotan[:rows]
-    tail[2] = nhat_bwd[:rows]
-    tail_rstd[...] = jnp.broadcast_to(rstd_bwd[:rows], tail_rstd.shape)
+    d_hidden = d_acted * slope[count:]
+    leaving[...] = jnp.zeros_like(leaving)
+    for slot in range(count // rows):
+        source = slice(slot * rows, (slot + 1) * rows)
+        leaving[2 * slot * rows : (2 * slot + 1) * rows, :units] = value[source]
+        leaving[(2 * slot + 1) * rows : (2 * slot + 2) * rows, units:] = d_hidden[source]
+    part = dot(leaving[...].astype(bf16), tall[...], (1, 0))
+    send[...] = part[count:].astype(bf16)
+    keep[...] = part[:count]
+    full[:, :width] = normed_bwd.astype(bf16)
+    full[:, width : 2 * width] = cotan
+    full[:, 2 * width : 2 * width + units] = value[count:].astype(bf16)
+    full[:, 2 * width + units :] = d_hidden.astype(bf16)
+
+
+def side_kernel(rows, held, other, full, away, tail, tail_rstd):
+    f32 = jnp.float32
+    width = held.shape[2]
     mid = width // 2
-    units = w_in.shape[1]
-    normed_low = normed_bwd.astype(bf16)
+    away[:, width:] = full[:, 2 * width :]
     upper = lax.axis_index("mirror") == 0
-    for ref in (own_out, far_out):
-        ref[:, 2 * mid : 2 * mid + units] = value_low[2 * half :]
-        ref[:, 2 * mid + units :] = d_hidden
 
     @pl.when(upper)
     def _():
-        own_out[:, :mid] = normed_low[:, :mid]
-        own_out[:, mid : 2 * mid] = cotan_low[:, :mid]
-        far_out[:, :mid] = normed_low[:, mid:]
-        far_out[:, mid : 2 * mid] = cotan_low[:, mid:]
+        away[:, :mid] = full[:, mid:width]
+        away[:, mid:width] = full[:, width + mid : 2 * width]
 
     @pl.when(jnp.logical_not(upper))
     def _():
-        own_out[:, :mid] = normed_low[:, mid:]
-        own_out[:, mid : 2 * mid] = cotan_low[:, mid:]
-        far_out[:, :mid] = normed_low[:, :mid]
-        far_out[:, mid : 2 * mid] = cotan_low[:, :mid]
+        away[:, :mid] = full[:, :mid]
+        away[:, mid:width] = full[:, width : width + mid]
+
+    nhat, rstd = norm_rows(held[2, :rows].astype(f32))
+    tail[0] = other[0, :rows].astype(f32)
+    tail[1] = other[1, :rows].astype(f32)
+    tail[2] = nhat
+    tail_rstd[...] = jnp.broadcast_to(rstd, tail_rstd.shape)
 
 
 def load_kernel(chunks, source, target, sems):
@@ -126,10 +128,48 @@
     )(weights)
 
 
-def outer_kernel(chunks, own, far, first_out, second_out, pair, first, second, sems):
-    rows, (mid, units) = own.shape[0], first.shape
-    pair[:rows] = own[...]
+def prepare_kernel(w_in, w_out, wide, tall):
+    units = w_in.shape[1]
+    first, second = w_in[...], w_out[...]
+    tall[:units] = second
+    tall[units:] = first.T
+    wide[:, :units] = second.T
+    wide[:, units:] = first
+
+
+def prepared(w_in, w_out):
+    width, units = w_in.shape
+    size = w_in.size * w_in.dtype.itemsize
+    return pl.pallas_call(
+        prepare_kernel,
+        out_shape=(
+            jax.ShapeDtypeStruct((width, 2 * units), w_in.dtype),
+            jax.ShapeDtypeStruct((2 * units, width), w_in.dtype),
+        ),
+        in_specs=[VMEM] * 2,
+        out_specs=[VMEM] * 2,
+        compiler_params=pltpu.CompilerParams(vmem_limit_bytes=max(4 << 20, 10 * size)),
+        cost_estimate=pl.CostEstimate(flops=0, bytes_accessed=4 * size, transcendentals=0),
+    )(w_in, w_out)
+
+
+def outer_kernel(chunks, full, far, first_out, second_out, pair, first, second, sems):
+    rows, (mid, units) = far.shape[0], first.shape
+    width = 2 * mid
     pair[rows:] = far[...]
+    pair[:rows, width:] = full[:, 2 * width :]
+    upper = lax.axis_index("mirror") == 0
+
+    @pl.when(upper)
+    def _():
+        pair[:rows, :mid] = full[:, :mid]
+        pair[:rows, mid:width] = full[:, width : width + mid]
+
+    @pl.when(jnp.logical_not(upper))
+    def _():
+        pair[:rows, :mid] = full[:, mid:width]
+        pair[:rows, mid:width] = full[:, width + mid : 2 * width]
+
     value = pair[:, 2 * mid : 2 * mid + units]
     d_hidden = pair[:, 2 * mid + units :]
     copies = []
@@ -150,9 +190,9 @@
 
 def tail_kernel(rows, part, came, gain, tail, tail_rstd, fwd_out, bwd_out):
     f32 = jnp.float32
-    branch = part[0, :rows] + came[:rows].astype(f32)
+    branch = part[:rows] + came[:rows].astype(f32)
     fwd_out[...] = (tail[0] + branch).astype(fwd_out.dtype)
-    scaled = (part[1, :rows] + came[rows:].astype(f32)) * gain[...]
+    scaled = (part[rows : 2 * rows] + came[rows:].astype(f32)) * gain[...]
     nhat = tail[2]
     d_input = tail_rstd[:, :1] * (
         scaled
@@ -174,41 +214,49 @@
     w_first = loaded(w_in[0], 4)
     fwd_in, bwd_in, w_first = lax.optimization_barrier((fwd_in, bwd_in, w_first))
     w_second = loaded(w_out[0], 4)
+    wide, tall = prepared(w_first, w_second)
     held = jnp.stack([fwd_in, bwd_in, stash[0, 0]])
     for mask in masks:
         flat = held.reshape(-1, width) if held.shape[1] == 1 else held
         other = lax.ppermute(flat, "dp", xor_pairs(count, mask)).reshape(held.shape)
         if mask == masks[0]:
-            other, w_second = lax.optimization_barrier((other, w_second))
+            other, wide, tall = lax.optimization_barrier((other, wide, tall))
         held = jnp.concatenate([held, other], axis=1)
     other = lax.ppermute(held, "dp", xor_pairs(count, 1))
     half = held.shape[1]
-    low = jax.ShapeDtypeStruct((2 * half, width + 2 * units), jnp.bfloat16)
-    send, keep, own, away, tail, tail_rstd = pl.pallas_call(
+    limit = pltpu.CompilerParams(vmem_limit_bytes=max(8 << 20, 40 * half * width * 4))
+    send, keep, full = pl.pallas_call(
         functools.partial(block_kernel, rows),
         out_shape=(
-            jax.ShapeDtypeStruct((2, half, width), jnp.bfloat16),
-            jax.ShapeDtypeStruct((2, half, width), jnp.float32),
-            low,
-            low,
+            jax.ShapeDtypeStruct((2 * half, width), jnp.bfloat16),
+            jax.ShapeDtypeStruct((2 * half, width), jnp.float32),
+            jax.ShapeDtypeStruct((2 * half, 2 * width + 2 * units), jnp.bfloat16),
+        ),
+        in_specs=[VMEM] * 5,
+        out_specs=[VMEM] * 3,
+        scratch_shapes=[pltpu.VMEM((4 * half, 2 * units), jnp.float32)],
+        compiler_params=limit,
+    )(held, other, gain, wide, tall)
+    away, tail, tail_rstd = pl.pallas_call(
+        functools.partial(side_kernel, rows),
+        out_shape=(
+            jax.ShapeDtypeStruct((2 * half, width + 2 * units), jnp.bfloat16),
             jax.ShapeDtypeStruct((3, rows, width), jnp.float32),
             jax.ShapeDtypeStruct((rows, 128), jnp.float32),
         ),
-        in_specs=[VMEM] * 5,
-        out_specs=[VMEM] * 6,
-        compiler_params=pltpu.CompilerParams(vmem_limit_bytes=max(8 << 20, 40 * half * width * 4)),
-    )(held, other, gain, w_first, w_second)
-    part = None
-    for mask in [1] + masks[::-1]:
-        if part is not None:
-            half = part.shape[1] // 2
-            send, keep = part[:, half:].astype(jnp.bfloat16), part[:, :half]
-        last = mask == (masks or [1])[0]
-        came = lax.ppermute(send.reshape(-1, width) if last else send, "dp", xor_pairs(count, mask))
-        if not last:
+        in_specs=[VMEM] * 3,
+        out_specs=[VMEM] * 3,
+        compiler_params=pltpu.CompilerParams(vmem_limit_bytes=max(4 << 20, 40 * rows * width * 4)),
+    )(held, other, full)
+    scatter = [1] + masks[::-1]
+    for step, mask in enumerate(scatter):
+        came = lax.ppermute(send, "dp", xor_pairs(count, mask))
+        if step + 1 < len(scatter):
             part = keep + came.astype(jnp.float32)
-            if mask == 1:
-                part, away = lax.optimization_barrier((part, away))
+            if step == 0:
+                part, away, tail, tail_rstd = lax.optimization_barrier((part, away, tail, tail_rstd))
+            half = part.shape[0] // 2
+            send, keep = part[half:].astype(jnp.bfloat16), part[:half]
     far = lax.ppermute(away, "mirror", xor_pairs(mirrors, 1))
     mid = width // 2
     grad_first, grad_second = pl.pallas_call(
@@ -220,14 +268,14 @@
         in_specs=[VMEM] * 2,
         out_specs=[pl.BlockSpec(memory_space=pl.ANY)] * 2,
         scratch_shapes=[
-            pltpu.VMEM((2 * own.shape[0], own.shape[1]), jnp.bfloat16),
+            pltpu.VMEM((2 * far.shape[0], far.shape[1]), jnp.bfloat16),
             pltpu.VMEM((mid, units), jnp.bfloat16),
             pltpu.VMEM((units, mid), jnp.bfloat16),
             pltpu.SemaphoreType.DMA((2, 8)),
         ],
-        compiler_params=pltpu.CompilerParams(vmem_limit_bytes=max(6 << 20, 24 * own.size)),
+        compiler_params=pltpu.CompilerParams(vmem_limit_bytes=max(6 << 20, 24 * far.size)),
         cost_estimate=pl.CostEstimate(flops=0, bytes_accessed=8 * mid * units, transcendentals=0),
-    )(own, far)
+    )(full, far)
     part, grad_first, grad_second = lax.optimization_barrier((part, grad_first, grad_second))
     fwd_out, bwd_out = pl.pallas_call(
         functools.partial(tail_kernel, rows),

time: 28.4 us -> 27.2 us (0.958)
  waiting for transfers between devices: 7.53 us -> 6.68 us
    pallas_call x0 -> x2, Pallas kernels: none -> 0.91 us  [the longest x1 0.67 us: prepared(): pl.pallas_call(prepare_kernel, out_shape=(jax.ShapeDtypeStruct((width, 2...]
    pallas_call x1, Pallas kernels: 1.8 us -> 0.91 us  [on_device(): pl.pallas_call(functools.partial(block_kernel, rows), out_shape=(jax.Shap...]
    ppermute x2, waiting for transfers between devices: 3.36 us -> 2.69 us  [on_device(): other = lax.ppermute(flat, 'dp', xor_pairs(count, mask)).reshape(held.shape)]
  transfers between devices with their start and end apart: 9 -> 9, of which waited for: 8 -> 8; matrix products, arithmetic and copies ran while one was open for 0% -> 0% of each run, Pallas kernels for 5% -> 9%
where the time goes in v4:
time: 27.2 us; the launch traced here: 27.1 us
  starting transfers between devices  13.8 us (51%)
  waiting for transfers between devices  6.68 us (25%)
  Pallas kernels  4.11 us (15%)
  local copies, waits for them, and re-layouts  1.35 us (5%)
  between operations  0.73 us (3%)
  other arithmetic  0.4 us (1%)
    ppermute x2, starting transfers between devices, on_device(): other = lax.ppermute(flat, 'dp', xor_pairs(count, mask)).reshape(held.shape)  4.63 us
    ppermute x3, starting transfers between devices, on_device(): came = lax.ppermute(send, 'dp', xor_pairs(count, mask))  4.63 us
    ppermute x2, waiting for transfers between devices, on_device(): other = lax.ppermute(flat, 'dp', xor_pairs(count, mask)).reshape(held.shape)  2.69 us
    ppermute x1, starting transfers between devices, on_device(): lax.ppermute(sent_fwd[0, 0], AXES, relay_pairs(sections, mirrors, count,...  2.44 us
    ppermute x1, waiting for transfers between devices, on_device(): lax.ppermute(sent_bwd[0, 0], AXES, relay_pairs(sections, mirrors, count,...  1.72 us
    ppermute x1, starting transfers between devices, on_device(): far = lax.ppermute(away, 'mirror', xor_pairs(mirrors, 1))  1.52 us
    pallas_call x1, Pallas kernels, on_device(): pl.pallas_call(functools.partial(outer_kernel, 8), out_shape=(jax.ShapeDt...  1.32 us
    unnamed x9, local copies, waits for them, and re-layouts  1.27 us
  transfers between devices with their start and end apart: 9, of which 8 were waited for; matrix products, arithmetic and copies ran while one was open for 0% of the time, Pallas kernels for 9%

profile of v4, /device:TPU:0, one launch (start us, length us, event | category | flops | bytes accessed | tf_op | source)
XLA Modules:
  0.0 27.1 jit_solution(8010660021362102827)
XLA Ops:
  0.6 2.4 %collective-permute-start = (bf16[1,4096]{1,0:T(2,128)(2,1)}, bf16[1,4096]{1,0:T(2,128)(2,1)S(1)}, u32[]{:S(2)}, u32[]{:S(2)}) collective-permute-start(bf16[1,4096]{1,0:T(2,128)(2,1)} %bitcast.30), channel_id=1, source_target_pairs={{0,17},{1,16},{2,19},{3,18},{4,21},{5,20},{6,23},{7,22},{8,25},{9,... | collective-permute-start | bytes 24584 | tf_op jit(solution)/shard_map/ppermute | solution.py:212
  3.1 0.1 collective-permute-start.1
  3.2 1.2 %copy-done = bf16[1,4096,128]{2,1,0:T(8,128)(2,1)S(1)} copy-done((bf16[1,4096,128]{2,1,0:T(8,128)(2,1)S(1)}, bf16[1,4096,128]{2,1,0:T(8,128)(2,1)}, u32[]{:S(2)}) %copy-start) | copy-done | bytes 1048600
  4.4 0.1 shard_map.93.w_in
  4.5 0.2 collective-permute-done
  4.7 1.7 %collective-permute-done.1 = bf16[1,4096]{1,0:T(2,128)(2,1)S(1)} collective-permute-done((bf16[1,4096]{1,0:T(2,128)(2,1)}, bf16[1,4096]{1,0:T(2,128)(2,1)S(1)}, u32[]{:S(2)}, u32[]{:S(2)}) %collective-permute-start.1) | collective-permute-done | bytes 8224 | tf_op jit(solution)/shard_map/ppermute | solution.py:213
  6.5 0.0 copy-done.3
  6.5 0.1 pad_maximum_fusion.1
  6.6 2.9 %collective-permute-start.2 = (bf16[3,4096]{1,0:T(4,128)(2,1)S(1)}, bf16[3,4096]{1,0:T(4,128)(2,1)S(1)}, u32[]{:S(2)}, u32[]{:S(2)}) collective-permute-start(bf16[3,4096]{1,0:T(4,128)(2,1)S(1)} %bitcast.27), channel_id=1, source_target_pairs={{0,5},{1,4},{2,7},{3,6},{4,1},{5,0},{6,3},{7,2},{8,13},{9,12},{10,... | collective-permute-start | bytes 73736 | tf_op jit(solution)/shard_map/ppermute | solution.py:221
  9.5 0.0 copy-done.1
  9.5 0.1 shard_map.94.w_out
  9.6 0.7 %shard_map.95 = (bf16[4096,256]{1,0:T(8,128)(2,1)S(1)}, bf16[256,4096]{1,0:T(8,128)(2,1)S(1)}) custom-call(bf16[4096,128]{1,0:T(8,128)(2,1)S(1)} %shard_map.93.w_in, bf16[128,4096]{1,0:T(8,128)(2,1)S(1)} %shard_map.94.w_out), custom_call_target="tpu_custom_call" | custom-call | bytes 4194304 | tf_op jit(solution)/shard_map/pallas_call | solution.py:143
  10.3 0.8 %collective-permute-done.2 = bf16[3,4096]{1,0:T(4,128)(2,1)S(1)} collective-permute-done((bf16[3,4096]{1,0:T(4,128)(2,1)S(1)}, bf16[3,4096]{1,0:T(4,128)(2,1)S(1)}, u32[]{:S(2)}, u32[]{:S(2)}) %collective-permute-start.2) | collective-permute-done | bytes 24608 | tf_op jit(solution)/shard_map/ppermute | solution.py:221
  11.2 0.1 pad_maximum_fusion.2
  11.3 1.7 %collective-permute-start.3 = (bf16[3,2,4096]{2,1,0:T(2,128)(2,1)S(1)}, bf16[3,2,4096]{2,1,0:T(2,128)(2,1)S(1)}, u32[]{:S(2)}, u32[]{:S(2)}) collective-permute-start(bf16[3,2,4096]{2,1,0:T(2,128)(2,1)S(1)} %pad_maximum_fusion.2), channel_id=1, source_target_pairs={{0,3},{1,2},{2,1},{3,0},{4,7},{5,6},{6,5},{7,4},{8,11},{9,10},{10,... | collective-permute-start | bytes 147464 | tf_op jit(solution)/shard_map/ppermute | solution.py:221
  13.0 1.9 %collective-permute-done.3 = bf16[3,2,4096]{2,1,0:T(2,128)(2,1)S(1)} collective-permute-done((bf16[3,2,4096]{2,1,0:T(2,128)(2,1)S(1)}, bf16[3,2,4096]{2,1,0:T(2,128)(2,1)S(1)}, u32[]{:S(2)}, u32[]{:S(2)}) %collective-permute-start.3) | collective-permute-done | bytes 49184 | tf_op jit(solution)/shard_map/ppermute | solution.py:221
  14.9 0.2 pad_maximum_fusion.held
  15.0 0.5 %collective-permute-start.4 = (bf16[3,4,4096]{2,1,0:T(4,128)(2,1)S(1)}, bf16[3,4,4096]{2,1,0:T(4,128)(2,1)S(1)}, u32[]{:S(2)}, u32[]{:S(2)}) collective-permute-start(bf16[3,4,4096]{2,1,0:T(4,128)(2,1)S(1)} %pad_maximum_fusion.held), channel_id=1, source_target_pairs={{0,1},{1,0},{2,3},{3,2},{4,5},{5,4},{6,7},{7,6},{8,9},{9,8},{10,11... | collective-permute-start | bytes 294920 | tf_op jit(solution)/shard_map/ppermute | solution.py:225
  15.6 0.9 %collective-permute-done.4.other = bf16[3,4,4096]{2,1,0:T(4,128)(2,1)S(1)} collective-permute-done((bf16[3,4,4096]{2,1,0:T(4,128)(2,1)S(1)}, bf16[3,4,4096]{2,1,0:T(4,128)(2,1)S(1)}, u32[]{:S(2)}, u32[]{:S(2)}) %collective-permute-start.4) | collective-permute-done | bytes 98336 | tf_op jit(solution)/shard_map/ppermute | solution.py:225
  16.5 0.0 copy-done.2
  16.5 0.9 %shard_map.96 = (bf16[8,4096]{1,0:T(8,128)(2,1)S(1)}, f32[8,4096]{1,0:T(8,128)S(1)}, bf16[8,8448]{1,0:T(8,128)(2,1)S(1)}) custom-call(bf16[3,4,4096]{2,1,0:T(4,128)(2,1)S(1)} %pad_maximum_fusion.held, bf16[3,4,4096]{2,1,0:T(4,128)(2,1)S(1)} %collective-permute-done.4.other, f32[1,4096]{1,0:T(1,128)S(1)} %copy-done.2, ...), custom_call_target="tpu_custom_call" | custom-call | tf_op jit(solution)/shard_map/pallas_call | solution.py:228
  17.4 0.4 %collective-permute-start.5 = (bf16[8,4096]{1,0:T(8,128)(2,1)S(1)}, bf16[8,4096]{1,0:T(8,128)(2,1)S(1)}, u32[]{:S(2)}, u32[]{:S(2)}) collective-permute-start(bf16[8,4096]{1,0:T(8,128)(2,1)S(1)} %get-tuple-element.38), channel_id=1, source_target_pairs={{0,1},{1,0},{2,3},{3,2},{4,5},{5,4},{6,7},{7,6},{8,9},{9,8},{10,11... | collective-permute-start | bytes 196616 | tf_op jit(solution)/shard_map/ppermute | solution.py:253
  17.8 0.2 shard_map.97
  18.0 0.7 %collective-permute-done.5 = bf16[8,4096]{1,0:T(8,128)(2,1)S(1)} collective-permute-done((bf16[8,4096]{1,0:T(8,128)(2,1)S(1)}, bf16[8,4096]{1,0:T(8,128)(2,1)S(1)}, u32[]{:S(2)}, u32[]{:S(2)}) %collective-permute-start.5) | collective-permute-done | bytes 65568 | tf_op jit(solution)/shard_map/ppermute | solution.py:253
  18.7 1.6 %collective-permute-start.6 = (bf16[4,4096]{1,0:T(4,128)(2,1)S(1)}, bf16[4,4096]{1,0:T(4,128)(2,1)S(1)}, u32[]{:S(2)}, u32[]{:S(2)}) collective-permute-start(bf16[4,4096]{1,0:T(4,128)(2,1)S(1)} %slice.19), channel_id=1, source_target_pairs={{0,3},{1,2},{2,1},{3,0},{4,7},{5,6},{6,5},{7,4},{8,11},{9,10},{10,... | collective-permute-start | bytes 98312 | tf_op jit(solution)/shard_map/ppermute | solution.py:253
  20.3 1.5 %collective-permute-start.7 = (bf16[8,4352]{1,0:T(8,128)(2,1)S(1)}, bf16[8,4352]{1,0:T(8,128)(2,1)S(1)}, u32[]{:S(2)}, u32[]{:S(2)}) collective-permute-start(bf16[8,4352]{1,0:T(8,128)(2,1)S(1)} %get-tuple-element.44), channel_id=1, source_target_pairs={{0,8},{8,0},{1,9},{9,1},{2,10},{10,2},{3,11},{11,3},{4,12},{12,4},... | collective-permute-start | bytes 208904 | tf_op jit(solution)/shard_map/ppermute | solution.py:260
  21.9 0.3 %collective-permute-done.6 = bf16[4,4096]{1,0:T(4,128)(2,1)S(1)} collective-permute-done((bf16[4,4096]{1,0:T(4,128)(2,1)S(1)}, bf16[4,4096]{1,0:T(4,128)(2,1)S(1)}, u32[]{:S(2)}, u32[]{:S(2)}) %collective-permute-start.6) | collective-permute-done | bytes 32800 | tf_op jit(solution)/shard_map/ppermute | solution.py:253
  22.2 2.6 %collective-permute-start.8 = (bf16[2,4096]{1,0:T(2,128)(2,1)S(1)}, bf16[2,4096]{1,0:T(2,128)(2,1)S(1)}, u32[]{:S(2)}, u32[]{:S(2)}) collective-permute-start(bf16[2,4096]{1,0:T(2,128)(2,1)S(1)} %slice.20), channel_id=1, source_target_pairs={{0,5},{1,4},{2,7},{3,6},{4,1},{5,0},{6,3},{7,2},{8,13},{9,12},{10,... | collective-permute-start | bytes 49160 | tf_op jit(solution)/shard_map/ppermute | solution.py:253
  24.8 0.0 collective-permute-done.7.far
  24.8 1.3 %shard_map.98 = (bf16[2048,128]{1,0:T(8,128)(2,1)}, bf16[128,2048]{1,0:T(8,128)(2,1)}) custom-call(bf16[8,8448]{1,0:T(8,128)(2,1)S(1)} %get-tuple-element.39.full, bf16[8,4352]{1,0:T(8,128)(2,1)S(1)} %collective-permute-done.7.far), custom_call_target="tpu_custom_call" | custom-call | bytes 2097152 | tf_op jit(solution)/shard_map/pallas_call | solution.py:262
  26.2 0.2 collective-permute-done.8.came
  26.3 0.7 %shard_map.99 = (bf16[1,4096]{1,0:T(2,128)(2,1)}, bf16[1,4096]{1,0:T(2,128)(2,1)}) custom-call(f32[4,4096]{1,0:T(4,128)S(1)} %convert_add_fusion.1.part, bf16[2,4096]{1,0:T(2,128)(2,1)S(1)} %collective-permute-done.8.came, f32[1,4096]{1,0:T(1,128)S(1)} %copy-done.2, f32[3,1,4096]{2,1,0:T(1,128)S(1)} %get-tuple-element.48.tail, ...), custom_call_target="tpu_custom_call" | custom-call | tf_op jit(solution)/shard_map/pallas_call | solution.py:280
  (10 shorter events, 0.2 us)
Async XLA Ops:
  0.6 4.1 %collective-permute-start = (bf16[1,4096]{1,0:T(2,128)(2,1)}, bf16[1,4096]{1,0:T(2,128)(2,1)S(1)}, u32[]{:S(2)}, u32[]{:S(2)}) collective-permute-start(bf16[1,4096]{1,0:T(2,128)(2,1)} %bitcast.30), channel_id=1, source_target_pairs={{0,17},{1,16},{2,19},{3,18},{4,21},{5,20},{6,23},{7,22},{8,25},{9,... | collective-permute-start | bytes 24584 | tf_op jit(solution)/shard_map/ppermute | solution.py:212
  3.1 3.4 %collective-permute-start.1 = (bf16[1,4096]{1,0:T(2,128)(2,1)}, bf16[1,4096]{1,0:T(2,128)(2,1)S(1)}, u32[]{:S(2)}, u32[]{:S(2)}) collective-permute-start(bf16[1,4096]{1,0:T(2,128)(2,1)} %bitcast.31), channel_id=1, source_target_pairs={{0,17},{1,16},{2,19},{3,18},{4,21},{5,20},{6,23},{7,22},{8,25},{9,... | collective-permute-start | bytes 24584 | tf_op jit(solution)/shard_map/ppermute | solution.py:213
  3.2 1.2 %copy-start = (bf16[1,4096,128]{2,1,0:T(8,128)(2,1)S(1)}, bf16[1,4096,128]{2,1,0:T(8,128)(2,1)}, u32[]{:S(2)}) copy-start(bf16[1,4096,128]{2,1,0:T(8,128)(2,1)} %param.10) | copy-start | bytes 3145732
  4.4 2.1 %copy-start.3 = (bf16[1,1,1,4096]{3,2,1,0:T(2,128)(2,1)S(1)}, bf16[1,1,1,4096]{3,2,1,0:T(2,128)(2,1)}, u32[]{:S(2)}) copy-start(bf16[1,1,1,4096]{3,2,1,0:T(2,128)(2,1)} %param.8) | copy-start | bytes 24580
  4.4 5.1 %copy-start.1 = (bf16[1,128,4096]{2,1,0:T(8,128)(2,1)S(1)}, bf16[1,128,4096]{2,1,0:T(8,128)(2,1)}, u32[]{:S(2)}) copy-start(bf16[1,128,4096]{2,1,0:T(8,128)(2,1)} %param.11) | copy-start | bytes 3145732
  6.6 4.5 %collective-permute-start.2 = (bf16[3,4096]{1,0:T(4,128)(2,1)S(1)}, bf16[3,4096]{1,0:T(4,128)(2,1)S(1)}, u32[]{:S(2)}, u32[]{:S(2)}) collective-permute-start(bf16[3,4096]{1,0:T(4,128)(2,1)S(1)} %bitcast.27), channel_id=1, source_target_pairs={{0,5},{1,4},{2,7},{3,6},{4,1},{5,0},{6,3},{7,2},{8,13},{9,12},{10,... | collective-permute-start | bytes 73736 | tf_op jit(solution)/shard_map/ppermute | solution.py:221
  9.5 7.0 %copy-start.2 = (f32[1,4096]{1,0:T(1,128)S(1)}, f32[1,4096]{1,0:T(1,128)}, u32[]{:S(2)}) copy-start(f32[1,4096]{1,0:T(1,128)} %gain.3) | copy-start | bytes 49156
  11.3 3.6 %collective-permute-start.3 = (bf16[3,2,4096]{2,1,0:T(2,128)(2,1)S(1)}, bf16[3,2,4096]{2,1,0:T(2,128)(2,1)S(1)}, u32[]{:S(2)}, u32[]{:S(2)}) collective-permute-start(bf16[3,2,4096]{2,1,0:T(2,128)(2,1)S(1)} %pad_maximum_fusion.2), channel_id=1, source_target_pairs={{0,3},{1,2},{2,1},{3,0},{4,7},{5,6},{6,5},{7,4},{8,11},{9,10},{10,... | collective-permute-start | bytes 147464 | tf_op jit(solution)/shard_map/ppermute | solution.py:221
  15.0 1.5 %collective-permute-start.4 = (bf16[3,4,4096]{2,1,0:T(4,128)(2,1)S(1)}, bf16[3,4,4096]{2,1,0:T(4,128)(2,1)S(1)}, u32[]{:S(2)}, u32[]{:S(2)}) collective-permute-start(bf16[3,4,4096]{2,1,0:T(4,128)(2,1)S(1)} %pad_maximum_fusion.held), channel_id=1, source_target_pairs={{0,1},{1,0},{2,3},{3,2},{4,5},{5,4},{6,7},{7,6},{8,9},{9,8},{10,11... | collective-permute-start | bytes 294920 | tf_op jit(solution)/shard_map/ppermute | solution.py:225
  17.4 1.3 %collective-permute-start.5 = (bf16[8,4096]{1,0:T(8,128)(2,1)S(1)}, bf16[8,4096]{1,0:T(8,128)(2,1)S(1)}, u32[]{:S(2)}, u32[]{:S(2)}) collective-permute-start(bf16[8,4096]{1,0:T(8,128)(2,1)S(1)} %get-tuple-element.38), channel_id=1, source_target_pairs={{0,1},{1,0},{2,3},{3,2},{4,5},{5,4},{6,7},{7,6},{8,9},{9,8},{10,11... | collective-permute-start | bytes 196616 | tf_op jit(solution)/shard_map/ppermute | solution.py:253
  18.7 3.4 %collective-permute-start.6 = (bf16[4,4096]{1,0:T(4,128)(2,1)S(1)}, bf16[4,4096]{1,0:T(4,128)(2,1)S(1)}, u32[]{:S(2)}, u32[]{:S(2)}) collective-permute-start(bf16[4,4096]{1,0:T(4,128)(2,1)S(1)} %slice.19), channel_id=1, source_target_pairs={{0,3},{1,2},{2,1},{3,0},{4,7},{5,6},{6,5},{7,4},{8,11},{9,10},{10,... | collective-permute-start | bytes 98312 | tf_op jit(solution)/shard_map/ppermute | solution.py:253
  20.3 4.5 %collective-permute-start.7 = (bf16[8,4352]{1,0:T(8,128)(2,1)S(1)}, bf16[8,4352]{1,0:T(8,128)(2,1)S(1)}, u32[]{:S(2)}, u32[]{:S(2)}) collective-permute-start(bf16[8,4352]{1,0:T(8,128)(2,1)S(1)} %get-tuple-element.44), channel_id=1, source_target_pairs={{0,8},{8,0},{1,9},{9,1},{2,10},{10,2},{3,11},{11,3},{4,12},{12,4},... | collective-permute-start | bytes 208904 | tf_op jit(solution)/shard_map/ppermute | solution.py:260
  22.2 4.1 %collective-permute-start.8 = (bf16[2,4096]{1,0:T(2,128)(2,1)S(1)}, bf16[2,4096]{1,0:T(2,128)(2,1)S(1)}, u32[]{:S(2)}, u32[]{:S(2)}) collective-permute-start(bf16[2,4096]{1,0:T(2,128)(2,1)S(1)} %slice.20), channel_id=1, source_target_pairs={{0,5},{1,4},{2,7},{3,6},{4,1},{5,0},{6,3},{7,2},{8,13},{9,12},{10,... | collective-permute-start | bytes 49160 | tf_op jit(solution)/shard_map/ppermute | solution.py:253

commit v5 on v4

--- a/solution.py
+++ b/solution.py
@@ -48,21 +48,15 @@
     return lax.dot_general(left, right, ((contract[:1], contract[1:]), ((), ())), preferred_element_type=jnp.float32)
 
 
-def block_kernel(rows, held, other, gain, wide, tall, send, keep, full, leaving):
-    half, width = held.shape[1], held.shape[2]
-    count, units = 2 * half, wide.shape[1] // 2
+def block_kernel(rows, held, gain, w_in, w_out_t, tall, send, keep, full, leaving):
+    count, width = held.shape[1], held.shape[2]
+    units = w_in.shape[1]
     f32, bf16 = jnp.float32, jnp.bfloat16
-
-    def joined(first, second):
-        return jnp.concatenate([first.astype(f32), second.astype(f32)], axis=0)
-
-    cotan = joined(other[1], held[1]).astype(bf16)
-    d_acted = dot(cotan, wide[:, :units], (1, 0))
-    nhat_fwd, _ = norm_rows(joined(other[0], held[0]))
-    nhat_bwd, _ = norm_rows(joined(held[2], other[2]))
-    normed_bwd = nhat_bwd * gain[...]
-    entering = jnp.concatenate([nhat_fwd * gain[...], normed_bwd], axis=0).astype(bf16)
-    hidden = dot(entering, wide[:, units:], (1, 0))
+    cotan = held[1]
+    d_acted = dot(cotan, w_out_t[...], (1, 0))
+    nhat, _ = norm_rows(jnp.concatenate([held[0].astype(f32), held[2].astype(f32)], axis=0))
+    normed = (nhat * gain[...]).astype(bf16)
+    hidden = dot(normed, w_in[...], (1, 0))
     value, slope = gelu_pair(hidden)
     d_hidden = d_acted * slope[count:]
     leaving[...] = jnp.zeros_like(leaving)
@@ -73,34 +67,45 @@
     part = dot(leaving[...].astype(bf16), tall[...], (1, 0))
     send[...] = part[count:].astype(bf16)
     keep[...] = part[:count]
-    full[:, :width] = normed_bwd.astype(bf16)
+    full[:, :width] = (nhat[count:] * gain[...]).astype(bf16)
     full[:, width : 2 * width] = cotan
-    full[:, 2 * width : 2 * width + units] = value[count:].astype(bf16)
-    full[:, 2 * width + units :] = d_hidden.astype(bf16)
-
-
-def side_kernel(rows, held, other, full, away, tail, tail_rstd):
-    f32 = jnp.float32
-    width = held.shape[2]
-    mid = width // 2
-    away[:, width:] = full[:, 2 * width :]
-    upper = lax.axis_index("mirror") == 0
-
-    @pl.when(upper)
-    def _():
-        away[:, :mid] = full[:, mid:width]
-        away[:, mid:width] = full[:, width + mid : 2 * width]
-
-    @pl.when(jnp.logical_not(upper))
-    def _():
-        away[:, :mid] = full[:, :mid]
-        away[:, mid:width] = full[:, width : width + mid]
-
-    nhat, rstd = norm_rows(held[2, :rows].astype(f32))
-    tail[0] = other[0, :rows].astype(f32)
-    tail[1] = other[1, :rows].astype(f32)
+    low = units // 2
+    value, d_hidden = value[count:].astype(bf16), d_hidden.astype(bf16)
+    for side in range(2):
+        start = 2 * width + 2 * side * low
+        full[:, start : start + low] = value[:, side * low : (side + 1) * low]
+        full[:, start + low : start + 2 * low] = d_hidden[:, side * low : (side + 1) * low]
+
+
+def row_kernel(fwd_in, bwd_in, stash, tail, tail_rstd):
+    nhat, rstd = norm_rows(stash[...].astype(jnp.float32))
+    tail[0] = fwd_in[...].astype(jnp.float32)
+    tail[1] = bwd_in[...].astype(jnp.float32)
     tail[2] = nhat
     tail_rstd[...] = jnp.broadcast_to(rstd, tail_rstd.shape)
+
+
+def side_kernel(width, full, peer, own, away):
+    count, low, mid = full.shape[0], own.shape[1] - width, width // 2
+    upper = lax.axis_index("mirror") == 0
+    for ref in (own, away):
+        ref[:count, width:] = full[:, 2 * width : 2 * width + low]
+        ref[count:, width:] = peer[:, 2 * width + low :]
+    for source, target in ((full, slice(0, count)), (peer, slice(count, 2 * count))):
+
+        @pl.when(upper)
+        def _(source=source, target=target):
+            own[target, :mid] = source[:, :mid]
+            own[target, mid:width] = source[:, width : width + mid]
+            away[target, :mid] = source[:, mid:width]
+            away[target, mid:width] = source[:, width + mid : 2 * width]
+
+        @pl.when(jnp.logical_not(upper))
+        def _(source=source, target=target):
+            own[target, :mid] = source[:, mid:width]
+            own[target, mid:width] = source[:, width + mid : 2 * width]
+            away[target, :mid] = source[:, :mid]
+            away[target, mid:width] = source[:, width : width + mid]
 
 
 def load_kernel(chunks, source, target, sems):
@@ -128,48 +133,39 @@
     )(weights)
 
 
-def prepare_kernel(w_in, w_out, wide, tall):
-    units = w_in.shape[1]
-    first, second = w_in[...], w_out[...]
-    tall[:units] = second
-    tall[units:] = first.T
-    wide[:, :units] = second.T
-    wide[:, units:] = first
-
-
-def prepared(w_in, w_out):
-    width, units = w_in.shape
-    size = w_in.size * w_in.dtype.itemsize
+def prepare_kernel(in_own, in_peer, out_own, out_peer, w_in, w_out_t, tall):
+    low = in_own.shape[1]
+    w_in[:, :low] = in_own[...]
+    w_in[:, low:] = in_peer[...]
+    w_out_t[:, :low] = out_own[...].T
+    w_out_t[:, low:] = out_peer[...].T
+    tall[:low] = out_own[...]
+    tall[low : 2 * low] = out_peer[...]
+    tall[2 * low : 3 * low] = in_own[...].T
+    tall[3 * low :] = in_peer[...].T
+
+
+def prepared(in_own, in_peer, out_own, out_peer):
+    width, low = in_own.shape
+    size = in_own.size * in_own.dtype.itemsize
     return pl.pallas_call(
         prepare_kernel,
         out_shape=(
-            jax.ShapeDtypeStruct((width, 2 * units), w_in.dtype),
-            jax.ShapeDtypeStruct((2 * units, width), w_in.dtype),
+            jax.ShapeDtypeStruct((width, 2 * low), in_own.dtype),
+            jax.ShapeDtypeStruct((width, 2 * low), in_own.dtype),
+            jax.ShapeDtypeStruct((4 * low, width), in_own.dtype),
         ),
-        in_specs=[VMEM] * 2,
-        out_specs=[VMEM] * 2,
-        compiler_params=pltpu.CompilerParams(vmem_limit_bytes=max(4 << 20, 10 * size)),
-        cost_estimate=pl.CostEstimate(flops=0, bytes_accessed=4 * size, transcendentals=0),
-    )(w_in, w_out)
-
-
-def outer_kernel(chunks, full, far, first_out, second_out, pair, first, second, sems):
-    rows, (mid, units) = far.shape[0], first.shape
-    width = 2 * mid
+        in_specs=[VMEM] * 4,
+        out_specs=[VMEM] * 3,
+        compiler_params=pltpu.CompilerParams(vmem_limit_bytes=max(4 << 20, 4 * size)),
+        cost_estimate=pl.CostEstimate(flops=0, bytes_accessed=6 * size, transcendentals=0),
+    )(in_own, in_peer, out_own, out_peer)
+
+
+def outer_kernel(chunks, own, far, first_out, second_out, pair, first, second, sems):
+    rows, (mid, units) = own.shape[0], first.shape
+    pair[:rows] = own[...]
     pair[rows:] = far[...]
-    pair[:rows, width:] = full[:, 2 * width :]
-    upper = lax.axis_index("mirror") == 0
-
-    @pl.when(upper)
-    def _():
-        pair[:rows, :mid] = full[:, :mid]
-        pair[:rows, mid:width] = full[:, width : width + mid]
-
-    @pl.when(jnp.logical_not(upper))
-    def _():
-        pair[:rows, :mid] = full[:, mid:width]
-        pair[:rows, mid:width] = full[:, width + mid : 2 * width]
-
     value = pair[:, 2 * mid : 2 * mid + units]
     d_hidden = pair[:, 2 * mid + units :]
     copies = []
@@ -209,52 +205,61 @@
     masks = [(1 << bit) | 1 for bit in range(bits - 1, 0, -1)]
     rows, width = sent_fwd.shape[2], sent_fwd.shape[3]
     units = w_in.shape[2]
-    fwd_in = lax.ppermute(sent_fwd[0, 0], AXES, relay_pairs(sections, mirrors, count, 1, 1))
-    bwd_in = lax.ppermute(sent_bwd[0, 0], AXES, relay_pairs(sections, mirrors, count, 1, -1))
+    fwd_in = lax.ppermute(sent_fwd[0, 0], AXES, relay_pairs(sections, mirrors, count, 0, 1))
+    bwd_in = lax.ppermute(sent_bwd[0, 0], AXES, relay_pairs(sections, mirrors, count, 0, -1))
     w_first = loaded(w_in[0], 4)
     fwd_in, bwd_in, w_first = lax.optimization_barrier((fwd_in, bwd_in, w_first))
     w_second = loaded(w_out[0], 4)
-    wide, tall = prepared(w_first, w_second)
+    peer_first = lax.ppermute(w_first, "dp", xor_pairs(count, 1))
+    peer_second = lax.ppermute(w_second, "dp", xor_pairs(count, 1))
+    tail, tail_rstd = pl.pallas_call(
+        row_kernel,
+        out_shape=(
+            jax.ShapeDtypeStruct((3, rows, width), jnp.float32),
+            jax.ShapeDtypeStruct((rows, 128), jnp.float32),
+        ),
+        in_specs=[VMEM] * 3,
+        out_specs=[VMEM] * 2,
+        compiler_params=pltpu.CompilerParams(vmem_limit_bytes=max(4 << 20, 40 * rows * width * 4)),
+    )(fwd_in, bwd_in, stash[0, 0])
     held = jnp.stack([fwd_in, bwd_in, stash[0, 0]])
     for mask in masks:
         flat = held.reshape(-1, width) if held.shape[1] == 1 else held
         other = lax.ppermute(flat, "dp", xor_pairs(count, mask)).reshape(held.shape)
         if mask == masks[0]:
-            other, wide, tall = lax.optimization_barrier((other, wide, tall))
+            other, w_second, tail, tail_rstd = lax.optimization_barrier((other, w_second, tail, tail_rstd))
+            weights = prepared(w_first, peer_first, w_second, peer_second)
+        if mask == masks[-1]:
+            other, *weights = lax.optimization_barrier((other, *weights))
         held = jnp.concatenate([held, other], axis=1)
-    other = lax.ppermute(held, "dp", xor_pairs(count, 1))
     half = held.shape[1]
     limit = pltpu.CompilerParams(vmem_limit_bytes=max(8 << 20, 40 * half * width * 4))
     send, keep, full = pl.pallas_call(
         functools.partial(block_kernel, rows),
         out_shape=(
-            jax.ShapeDtypeStruct((2 * half, width), jnp.bfloat16),
-            jax.ShapeDtypeStruct((2 * half, width), jnp.float32),
-            jax.ShapeDtypeStruct((2 * half, 2 * width + 2 * units), jnp.bfloat16),
+            jax.ShapeDtypeStruct((half, width), jnp.bfloat16),
+            jax.ShapeDtypeStruct((half, width), jnp.float32),
+            jax.ShapeDtypeStruct((half, 2 * width + 4 * units), jnp.bfloat16),
         ),
         in_specs=[VMEM] * 5,
         out_specs=[VMEM] * 3,
-        scratch_shapes=[pltpu.VMEM((4 * half, 2 * units), jnp.float32)],
+        scratch_shapes=[pltpu.VMEM((2 * half, 4 * units), jnp.float32)],
         compiler_params=limit,
-    )(held, other, gain, wide, tall)
-    away, tail, tail_rstd = pl.pallas_call(
-        functools.partial(side_kernel, rows),
-        out_shape=(
-            jax.ShapeDtypeStruct((2 * half, width + 2 * units), jnp.bfloat16),
-            jax.ShapeDtypeStruct((3, rows, width), jnp.float32),
-            jax.ShapeDtypeStruct((rows, 128), jnp.float32),
-        ),
-        in_specs=[VMEM] * 3,
-        out_specs=[VMEM] * 3,
-        compiler_params=pltpu.CompilerParams(vmem_limit_bytes=max(4 << 20, 40 * rows * width * 4)),
-    )(held, other, full)
-    scatter = [1] + masks[::-1]
+    )(held, gain, *weights)
+    peer = lax.ppermute(full, "dp", xor_pairs(count, 1))
+    low = jax.ShapeDtypeStruct((2 * half, width + 2 * units), jnp.bfloat16)
+    own, away = pl.pallas_call(
+        functools.partial(side_kernel, width),
+        out_shape=(low, low),
+        in_specs=[VMEM] * 2,
+        out_specs=[VMEM] * 2,
+        compiler_params=pltpu.CompilerParams(vmem_limit_bytes=4 << 20),
+    )(full, peer)
+    scatter = masks[::-1]
     for step, mask in enumerate(scatter):
         came = lax.ppermute(send, "dp", xor_pairs(count, mask))
         if step + 1 < len(scatter):
             part = keep + came.astype(jnp.float32)
-            if step == 0:
-                part, away, tail, tail_rstd = lax.optimization_barrier((part, away, tail, tail_rstd))
             half = part.shape[0] // 2
             send, keep = part[half:].astype(jnp.bfloat16), part[:half]
     far = lax.ppermute(away, "mirror", xor_pairs(mirrors, 1))
@@ -275,7 +280,7 @@
         ],
         compiler_params=pltpu.CompilerParams(vmem_limit_bytes=max(6 << 20, 24 * far.size)),
         cost_estimate=pl.CostEstimate(flops=0, bytes_accessed=8 * mid * units, transcendentals=0),
-    )(full, far)
+    )(own, far)
     part, grad_first, grad_second = lax.optimization_barrier((part, grad_first, grad_second))
     fwd_out, bwd_out = pl.pallas_call(
         functools.partial(tail_kernel, rows),

time: 27.2 us -> 26.6 us (0.978)
  waiting for transfers between devices: 6.68 us -> 3.6 us
  Pallas kernels: 4.11 us -> 5.64 us
  local copies, waits for them, and re-layouts: 1.35 us -> 2.36 us
    unnamed x9, local copies, waits for them, and re-layouts: 1.27 us -> 2.29 us
    ppermute x2, waiting for transfers between devices: 2.69 us -> 1.69 us  [on_device(): other = lax.ppermute(flat, 'dp', xor_pairs(count, mask)).reshape(held.shape)]
    ppermute x1 -> x3, waiting for transfers between devices: 0.94 us -> 0.01 us  [the longest x1 0.01 us: on_device(): peer = lax.ppermute(full, 'dp', xor_pairs(count, 1))]
    pallas_call x1, Pallas kernels: 0.67 us -> 1.55 us  [prepared(): pl.pallas_call(prepare_kernel, out_shape=(jax.ShapeDtypeStruct((width, 2...]
    pallas_call x1, Pallas kernels: 0.91 us -> 1.53 us  [on_device(): pl.pallas_call(functools.partial(block_kernel, rows), out_shape=(jax.Shap...]
    ppermute x3 -> x2, starting transfers between devices: 4.63 us -> 4.01 us  [on_device(): came = lax.ppermute(send, 'dp', xor_pairs(count, mask))]
    ppermute x1, starting transfers between devices: 2.44 us -> 3 us  [on_device(): lax.ppermute(sent_fwd[0, 0], AXES, relay_pairs(sections, mirrors, count,...]
    ppermute x3 -> x2, waiting for transfers between devices: 1.09 us -> 0.61 us  [on_device(): came = lax.ppermute(send, 'dp', xor_pairs(count, mask))]
  transfers between devices with their start and end apart: 9 -> 10, of which waited for: 8 -> 5; matrix products, arithmetic and copies ran while one was open for 0% -> 1% of each run, Pallas kernels for 9% -> 13%
where the time goes in v5:
time: 26.6 us; the launch traced here: 26.4 us
  starting transfers between devices  13.7 us (52%)
  Pallas kernels  5.64 us (21%)
  waiting for transfers between devices  3.6 us (14%)
  local copies, waits for them, and re-layouts  2.36 us (9%)
  between operations  0.75 us (3%)
  other arithmetic  0.39 us (1%)
    ppermute x2, starting transfers between devices, on_device(): other = lax.ppermute(flat, 'dp', xor_pairs(count, mask)).reshape(held.shape)  4.46 us
    ppermute x2, starting transfers between devices, on_device(): came = lax.ppermute(send, 'dp', xor_pairs(count, mask))  4.01 us
    ppermute x1, starting transfers between devices, on_device(): lax.ppermute(sent_fwd[0, 0], AXES, relay_pairs(sections, mirrors, count,...  3 us
    unnamed x9, local copies, waits for them, and re-layouts  2.29 us
    ppermute x2, waiting for transfers between devices, on_device(): other = lax.ppermute(flat, 'dp', xor_pairs(count, mask)).reshape(held.shape)  1.69 us
    ppermute x1, starting transfers between devices, on_device(): far = lax.ppermute(away, 'mirror', xor_pairs(mirrors, 1))  1.58 us
    pallas_call x1, Pallas kernels, prepared(): pl.pallas_call(prepare_kernel, out_shape=(jax.ShapeDtypeStruct((width, 2...  1.55 us
    pallas_call x1, Pallas kernels, on_device(): pl.pallas_call(functools.partial(block_kernel, rows), out_shape=(jax.Shap...  1.53 us
  transfers between devices with their start and end apart: 10, of which 5 were waited for; matrix products, arithmetic and copies ran while one was open for 1% of the time, Pallas kernels for 13%

profile of v5, /device:TPU:0, one launch (start us, length us, event | category | flops | bytes accessed | tf_op | source)
XLA Modules:
  0.0 26.4 jit_solution(11277774228181503005)
XLA Ops:
  0.6 3.0 %collective-permute-start = (bf16[1,4096]{1,0:T(2,128)(2,1)}, bf16[1,4096]{1,0:T(2,128)(2,1)S(1)}, u32[]{:S(2)}, u32[]{:S(2)}) collective-permute-start(bf16[1,4096]{1,0:T(2,128)(2,1)} %bitcast.32), channel_id=1, source_target_pairs={{0,16},{1,17},{2,18},{3,19},{4,20},{5,21},{6,22},{7,23},{8,24},{9,... | collective-permute-start | bytes 24584 | tf_op jit(solution)/shard_map/ppermute | solution.py:208
  3.6 0.1 collective-permute-start.1
  3.7 1.2 %copy-done = bf16[1,128,4096]{2,1,0:T(8,128)(2,1)S(1)} copy-done((bf16[1,128,4096]{2,1,0:T(8,128)(2,1)S(1)}, bf16[1,128,4096]{2,1,0:T(8,128)(2,1)}, u32[]{:S(2)}) %copy-start) | copy-done | bytes 1048600
  4.9 0.1 shard_map.94.out_own
  5.1 0.1 collective-permute-start.5
  5.1 1.0 %copy-done.1 = bf16[1,4096,128]{2,1,0:T(8,128)(2,1)S(1)} copy-done((bf16[1,4096,128]{2,1,0:T(8,128)(2,1)S(1)}, bf16[1,4096,128]{2,1,0:T(8,128)(2,1)}, u32[]{:S(2)}) %copy-start.1) | copy-done | bytes 1048600
  6.2 0.1 shard_map.93.in_own
  6.3 0.0 collective-permute-done.fwd_in
  6.3 1.3 %collective-permute-done.1.bwd_in = bf16[1,4096]{1,0:T(2,128)(2,1)S(1)} collective-permute-done((bf16[1,4096]{1,0:T(2,128)(2,1)}, bf16[1,4096]{1,0:T(2,128)(2,1)S(1)}, u32[]{:S(2)}, u32[]{:S(2)}) %collective-permute-start.1) | collective-permute-done | bytes 8224 | tf_op jit(solution)/shard_map/ppermute | solution.py:209
  7.6 0.0 collective-permute-start.4
  7.6 0.1 pad_maximum_fusion.1
  7.7 2.8 %collective-permute-start.2 = (bf16[3,4096]{1,0:T(4,128)(2,1)S(1)}, bf16[3,4096]{1,0:T(4,128)(2,1)S(1)}, u32[]{:S(2)}, u32[]{:S(2)}) collective-permute-start(bf16[3,4096]{1,0:T(4,128)(2,1)S(1)} %bitcast.29), channel_id=1, source_target_pairs={{0,5},{1,4},{2,7},{3,6},{4,1},{5,0},{6,3},{7,2},{8,13},{9,12},{10,... | collective-permute-start | bytes 73736 | tf_op jit(solution)/shard_map/ppermute | solution.py:228
  10.5 0.2 shard_map.95
  10.7 1.4 %collective-permute-done.2 = bf16[3,4096]{1,0:T(4,128)(2,1)S(1)} collective-permute-done((bf16[3,4096]{1,0:T(4,128)(2,1)S(1)}, bf16[3,4096]{1,0:T(4,128)(2,1)S(1)}, u32[]{:S(2)}, u32[]{:S(2)}) %collective-permute-start.2) | collective-permute-done | bytes 24608 | tf_op jit(solution)/shard_map/ppermute | solution.py:228
  12.1 0.1 pad_maximum_fusion.2
  12.3 0.0 copy-start.3
  12.3 1.7 %collective-permute-start.3 = (bf16[3,2,4096]{2,1,0:T(2,128)(2,1)S(1)}, bf16[3,2,4096]{2,1,0:T(2,128)(2,1)S(1)}, u32[]{:S(2)}, u32[]{:S(2)}) collective-permute-start(bf16[3,2,4096]{2,1,0:T(2,128)(2,1)S(1)} %pad_maximum_fusion.2), channel_id=1, source_target_pairs={{0,3},{1,2},{2,1},{3,0},{4,7},{5,6},{6,5},{7,4},{8,11},{9,10},{10,... | collective-permute-start | bytes 147464 | tf_op jit(solution)/shard_map/ppermute | solution.py:228
  14.0 0.0 collective-permute-done.5.out_peer
  14.0 1.6 %shard_map.96 = (bf16[4096,256]{1,0:T(8,128)(2,1)S(1)}, bf16[4096,256]{1,0:T(8,128)(2,1)S(1)}, bf16[512,4096]{1,0:T(8,128)(2,1)S(1)}) custom-call(bf16[4096,128]{1,0:T(8,128)(2,1)S(1)} %shard_map.93.in_own, bf16[4096,128]{1,0:T(8,128)(2,1)S(1)} %collective-permute-done.4.in_peer, bf16[128,4096]{1,0:T(8,128)(2,1)S(1)} %shard_map.94.out_own, ...), custom_call_target="tpu_custom_call" | custom-call | bytes 6291456 | tf_op jit(solution)/shard_map/pallas_call | solution.py:151
  15.5 0.3 %collective-permute-done.3 = bf16[3,2,4096]{2,1,0:T(2,128)(2,1)S(1)} collective-permute-done((bf16[3,2,4096]{2,1,0:T(2,128)(2,1)S(1)}, bf16[3,2,4096]{2,1,0:T(2,128)(2,1)S(1)}, u32[]{:S(2)}, u32[]{:S(2)}) %collective-permute-start.3) | collective-permute-done | bytes 49184 | tf_op jit(solution)/shard_map/ppermute | solution.py:228
  15.9 0.2 pad_maximum_fusion.held
  16.0 1.5 %shard_map.97 = (bf16[4,4096]{1,0:T(4,128)(2,1)S(1)}, f32[4,4096]{1,0:T(4,128)S(1)}, bf16[4,8704]{1,0:T(4,128)(2,1)S(1)}) custom-call(bf16[3,4,4096]{2,1,0:T(4,128)(2,1)S(1)} %pad_maximum_fusion.held, f32[1,4096]{1,0:T(1,128)S(1)} %copy-done.3, bf16[4096,256]{1,0:T(8,128)(2,1)S(1)} %get-tuple-element.43.w_in, ...), custom_call_target="tpu_custom_call" | custom-call | tf_op jit(solution)/shard_map/pallas_call | solution.py:237
  17.6 0.5 %collective-permute-start.7 = (bf16[4,8704]{1,0:T(4,128)(2,1)S(1)}, bf16[4,8704]{1,0:T(4,128)(2,1)S(1)}, u32[]{:S(2)}, u32[]{:S(2)}) collective-permute-start(bf16[4,8704]{1,0:T(4,128)(2,1)S(1)} %get-tuple-element.48.full), channel_id=1, source_target_pairs={{0,1},{1,0},{2,3},{3,2},{4,5},{5,4},{6,7},{7,6},{8,9},{9,8},{10,11... | collective-permute-start | bytes 208904 | tf_op jit(solution)/shard_map/ppermute | solution.py:249
  18.0 1.5 %collective-permute-start.6 = (bf16[4,4096]{1,0:T(4,128)(2,1)S(1)}, bf16[4,4096]{1,0:T(4,128)(2,1)S(1)}, u32[]{:S(2)}, u32[]{:S(2)}) collective-permute-start(bf16[4,4096]{1,0:T(4,128)(2,1)S(1)} %get-tuple-element.47), channel_id=1, source_target_pairs={{0,3},{1,2},{2,1},{3,0},{4,7},{5,6},{6,5},{7,4},{8,11},{9,10},{10,... | collective-permute-start | bytes 98312 | tf_op jit(solution)/shard_map/ppermute | solution.py:260
  19.5 0.0 collective-permute-done.7.peer
  19.5 1.6 %collective-permute-start.8 = (bf16[8,4352]{1,0:T(8,128)(2,1)S(1)}, bf16[8,4352]{1,0:T(8,128)(2,1)S(1)}, u32[]{:S(2)}, u32[]{:S(2)}) collective-permute-start(bf16[8,4352]{1,0:T(8,128)(2,1)S(1)} %get-tuple-element.50), channel_id=1, source_target_pairs={{0,8},{8,0},{1,9},{9,1},{2,10},{10,2},{3,11},{11,3},{4,12},{12,4},... | collective-permute-start | bytes 208904 | tf_op jit(solution)/shard_map/ppermute | solution.py:265
  21.1 0.4 %collective-permute-done.6 = bf16[4,4096]{1,0:T(4,128)(2,1)S(1)} collective-permute-done((bf16[4,4096]{1,0:T(4,128)(2,1)S(1)}, bf16[4,4096]{1,0:T(4,128)(2,1)S(1)}, u32[]{:S(2)}, u32[]{:S(2)}) %collective-permute-start.6) | collective-permute-done | bytes 32800 | tf_op jit(solution)/shard_map/ppermute | solution.py:260
  21.5 2.6 %collective-permute-start.9 = (bf16[2,4096]{1,0:T(2,128)(2,1)S(1)}, bf16[2,4096]{1,0:T(2,128)(2,1)S(1)}, u32[]{:S(2)}, u32[]{:S(2)}) collective-permute-start(bf16[2,4096]{1,0:T(2,128)(2,1)S(1)} %slice.7), channel_id=1, source_target_pairs={{0,5},{1,4},{2,7},{3,6},{4,1},{5,0},{6,3},{7,2},{8,13},{9,12},{10,... | collective-permute-start | bytes 49160 | tf_op jit(solution)/shard_map/ppermute | solution.py:260
  24.1 0.0 collective-permute-done.8.far
  24.1 1.3 %shard_map.99 = (bf16[2048,128]{1,0:T(8,128)(2,1)}, bf16[128,2048]{1,0:T(8,128)(2,1)}) custom-call(bf16[8,4352]{1,0:T(8,128)(2,1)S(1)} %get-tuple-element.49.own, bf16[8,4352]{1,0:T(8,128)(2,1)S(1)} %collective-permute-done.8.far), custom_call_target="tpu_custom_call" | custom-call | bytes 2097152 | tf_op jit(solution)/shard_map/pallas_call | solution.py:267
  25.4 0.3 collective-permute-done.9.came
  25.6 0.7 %shard_map.100 = (bf16[1,4096]{1,0:T(2,128)(2,1)}, bf16[1,4096]{1,0:T(2,128)(2,1)}) custom-call(f32[4,4096]{1,0:T(4,128)S(1)} %convert_add_fusion.part, bf16[2,4096]{1,0:T(2,128)(2,1)S(1)} %collective-permute-done.9.came, f32[1,4096]{1,0:T(1,128)S(1)} %copy-done.3, f32[3,1,4096]{2,1,0:T(1,128)S(1)} %get-tuple-element.54.tail, ...), custom_call_target="tpu_custom_call" | custom-call | tf_op jit(solution)/shard_map/pallas_call | solution.py:285
  (11 shorter events, 0.2 us)
Async XLA Ops:
  0.6 5.7 %collective-permute-start = (bf16[1,4096]{1,0:T(2,128)(2,1)}, bf16[1,4096]{1,0:T(2,128)(2,1)S(1)}, u32[]{:S(2)}, u32[]{:S(2)}) collective-permute-start(bf16[1,4096]{1,0:T(2,128)(2,1)} %bitcast.32), channel_id=1, source_target_pairs={{0,16},{1,17},{2,18},{3,19},{4,20},{5,21},{6,22},{7,23},{8,24},{9,... | collective-permute-start | bytes 24584 | tf_op jit(solution)/shard_map/ppermute | solution.py:208
  3.6 3.9 %collective-permute-start.1 = (bf16[1,4096]{1,0:T(2,128)(2,1)}, bf16[1,4096]{1,0:T(2,128)(2,1)S(1)}, u32[]{:S(2)}, u32[]{:S(2)}) collective-permute-start(bf16[1,4096]{1,0:T(2,128)(2,1)} %bitcast.33), channel_id=1, source_target_pairs={{0,16},{1,17},{2,18},{3,19},{4,20},{5,21},{6,22},{7,23},{8,24},{9,... | collective-permute-start | bytes 24584 | tf_op jit(solution)/shard_map/ppermute | solution.py:209
  3.7 1.2 %copy-start = (bf16[1,128,4096]{2,1,0:T(8,128)(2,1)S(1)}, bf16[1,128,4096]{2,1,0:T(8,128)(2,1)}, u32[]{:S(2)}) copy-start(bf16[1,128,4096]{2,1,0:T(8,128)(2,1)} %param.11) | copy-start | bytes 3145732
  4.9 1.2 %copy-start.1 = (bf16[1,4096,128]{2,1,0:T(8,128)(2,1)S(1)}, bf16[1,4096,128]{2,1,0:T(8,128)(2,1)}, u32[]{:S(2)}) copy-start(bf16[1,4096,128]{2,1,0:T(8,128)(2,1)} %param.10) | copy-start | bytes 3145732
  4.9 2.6 %copy-start.2 = (bf16[1,1,1,4096]{3,2,1,0:T(2,128)(2,1)S(1)}, bf16[1,1,1,4096]{3,2,1,0:T(2,128)(2,1)}, u32[]{:S(2)}) copy-start(bf16[1,1,1,4096]{3,2,1,0:T(2,128)(2,1)} %param.8) | copy-start | bytes 24580
  5.1 8.9 %collective-permute-start.5 = (bf16[128,4096]{1,0:T(8,128)(2,1)S(1)}, bf16[128,4096]{1,0:T(8,128)(2,1)S(1)}, u32[]{:S(2)}, u32[]{:S(2)}) collective-permute-start(bf16[128,4096]{1,0:T(8,128)(2,1)S(1)} %shard_map.94.out_own), channel_id=1, source_target_pairs={{0,1},{1,0},{2,3},{3,2},{4,5},{5,4},{6,7},{7,6},{8,9},{9,8},{10,11... | collective-permute-start | bytes 3145736 | tf_op jit(solution)/shard_map/ppermute | solution.py:214
  7.6 6.4 %collective-permute-start.4 = (bf16[4096,128]{1,0:T(8,128)(2,1)S(1)}, bf16[4096,128]{1,0:T(8,128)(2,1)S(1)}, u32[]{:S(2)}, u32[]{:S(2)}) collective-permute-start(bf16[4096,128]{1,0:T(8,128)(2,1)S(1)} %shard_map.93.in_own), channel_id=1, source_target_pairs={{0,1},{1,0},{2,3},{3,2},{4,5},{5,4},{6,7},{7,6},{8,9},{9,8},{10,11... | collective-permute-start | bytes 3145736 | tf_op jit(solution)/shard_map/ppermute | solution.py:213
  7.7 4.4 %collective-permute-start.2 = (bf16[3,4096]{1,0:T(4,128)(2,1)S(1)}, bf16[3,4096]{1,0:T(4,128)(2,1)S(1)}, u32[]{:S(2)}, u32[]{:S(2)}) collective-permute-start(bf16[3,4096]{1,0:T(4,128)(2,1)S(1)} %bitcast.29), channel_id=1, source_target_pairs={{0,5},{1,4},{2,7},{3,6},{4,1},{5,0},{6,3},{7,2},{8,13},{9,12},{10,... | collective-permute-start | bytes 73736 | tf_op jit(solution)/shard_map/ppermute | solution.py:228
  12.3 3.8 %copy-start.3 = (f32[1,4096]{1,0:T(1,128)S(1)}, f32[1,4096]{1,0:T(1,128)}, u32[]{:S(2)}) copy-start(f32[1,4096]{1,0:T(1,128)} %gain.3) | copy-start | bytes 49156
  12.3 3.6 %collective-permute-start.3 = (bf16[3,2,4096]{2,1,0:T(2,128)(2,1)S(1)}, bf16[3,2,4096]{2,1,0:T(2,128)(2,1)S(1)}, u32[]{:S(2)}, u32[]{:S(2)}) collective-permute-start(bf16[3,2,4096]{2,1,0:T(2,128)(2,1)S(1)} %pad_maximum_fusion.2), channel_id=1, source_target_pairs={{0,3},{1,2},{2,1},{3,0},{4,7},{5,6},{6,5},{7,4},{8,11},{9,10},{10,... | collective-permute-start | bytes 147464 | tf_op jit(solution)/shard_map/ppermute | solution.py:228
  17.6 1.9 %collective-permute-start.7 = (bf16[4,8704]{1,0:T(4,128)(2,1)S(1)}, bf16[4,8704]{1,0:T(4,128)(2,1)S(1)}, u32[]{:S(2)}, u32[]{:S(2)}) collective-permute-start(bf16[4,8704]{1,0:T(4,128)(2,1)S(1)} %get-tuple-element.48.full), channel_id=1, source_target_pairs={{0,1},{1,0},{2,3},{3,2},{4,5},{5,4},{6,7},{7,6},{8,9},{9,8},{10,11... | collective-permute-start | bytes 208904 | tf_op jit(solution)/shard_map/ppermute | solution.py:249
  18.0 3.4 %collective-permute-start.6 = (bf16[4,4096]{1,0:T(4,128)(2,1)S(1)}, bf16[4,4096]{1,0:T(4,128)(2,1)S(1)}, u32[]{:S(2)}, u32[]{:S(2)}) collective-permute-start(bf16[4,4096]{1,0:T(4,128)(2,1)S(1)} %get-tuple-element.47), channel_id=1, source_target_pairs={{0,3},{1,2},{2,1},{3,0},{4,7},{5,6},{6,5},{7,4},{8,11},{9,10},{10,... | collective-permute-start | bytes 98312 | tf_op jit(solution)/shard_map/ppermute | solution.py:260
  19.5 4.5 %collective-permute-start.8 = (bf16[8,4352]{1,0:T(8,128)(2,1)S(1)}, bf16[8,4352]{1,0:T(8,128)(2,1)S(1)}, u32[]{:S(2)}, u32[]{:S(2)}) collective-permute-start(bf16[8,4352]{1,0:T(8,128)(2,1)S(1)} %get-tuple-element.50), channel_id=1, source_target_pairs={{0,8},{8,0},{1,9},{9,1},{2,10},{10,2},{3,11},{11,3},{4,12},{12,4},... | collective-permute-start | bytes 208904 | tf_op jit(solution)/shard_map/ppermute | solution.py:265
  21.5 4.1 %collective-permute-start.9 = (bf16[2,4096]{1,0:T(2,128)(2,1)S(1)}, bf16[2,4096]{1,0:T(2,128)(2,1)S(1)}, u32[]{:S(2)}, u32[]{:S(2)}) collective-permute-start(bf16[2,4096]{1,0:T(2,128)(2,1)S(1)} %slice.7), channel_id=1, source_target_pairs={{0,5},{1,4},{2,7},{3,6},{4,1},{5,0},{6,3},{7,2},{8,13},{9,12},{10,... | collective-permute-start | bytes 49160 | tf_op jit(solution)/shard_map/ppermute | solution.py:260

commit v6 on v5

--- a/solution.py
+++ b/solution.py
@@ -48,13 +48,17 @@
     return lax.dot_general(left, right, ((contract[:1], contract[1:]), ((), ())), preferred_element_type=jnp.float32)
 
 
-def block_kernel(rows, held, gain, w_in, w_out_t, tall, send, keep, full, leaving):
-    count, width = held.shape[1], held.shape[2]
+def block_kernel(rows, held, other, gain, w_in, w_out_t, tall, send, keep, full, leaving):
+    count, width = 2 * held.shape[1], held.shape[2]
     units = w_in.shape[1]
     f32, bf16 = jnp.float32, jnp.bfloat16
-    cotan = held[1]
+
+    def joined(*arrays):
+        return jnp.concatenate([piece[array].astype(f32) for array in arrays for piece in (held, other)], axis=0)
+
+    cotan = joined(1).astype(bf16)
     d_acted = dot(cotan, w_out_t[...], (1, 0))
-    nhat, _ = norm_rows(jnp.concatenate([held[0].astype(f32), held[2].astype(f32)], axis=0))
+    nhat, _ = norm_rows(joined(0, 2))
     normed = (nhat * gain[...]).astype(bf16)
     hidden = dot(normed, w_in[...], (1, 0))
     value, slope = gelu_pair(hidden)
@@ -77,12 +81,25 @@
         full[:, start + low : start + 2 * low] = d_hidden[:, side * low : (side + 1) * low]
 
 
-def row_kernel(fwd_in, bwd_in, stash, tail, tail_rstd):
+def row_kernel(stash, nhat_out, rstd_out):
     nhat, rstd = norm_rows(stash[...].astype(jnp.float32))
-    tail[0] = fwd_in[...].astype(jnp.float32)
-    tail[1] = bwd_in[...].astype(jnp.float32)
-    tail[2] = nhat
-    tail_rstd[...] = jnp.broadcast_to(rstd, tail_rstd.shape)
+    nhat_out[...] = nhat
+    rstd_out[...] = jnp.broadcast_to(rstd, rstd_out.shape)
+
+
+def stack_kernel(rows, pair, stash, held):
+    held[: 2 * rows] = pair[...]
+    held[2 * rows :] = stash[...]
+
+
+def merge_kernel(held, other, merged):
+    count = merged.shape[1] // 2
+    for array in range(3):
+        pieces = [
+            (ref[array] if len(ref.shape) == 3 else ref[array * count : (array + 1) * count]).astype(jnp.float32)
+            for ref in (held, other)
+        ]
+        merged[array] = jnp.concatenate(pieces, axis=0).astype(merged.dtype)
 
 
 def side_kernel(width, full, peer, own, away):
@@ -184,18 +201,18 @@
         copy.wait()
 
 
-def tail_kernel(rows, part, came, gain, tail, tail_rstd, fwd_out, bwd_out):
+def tail_kernel(rows, part, came, gain, pair, nhat_in, rstd, fwd_out, bwd_out):
     f32 = jnp.float32
     branch = part[:rows] + came[:rows].astype(f32)
-    fwd_out[...] = (tail[0] + branch).astype(fwd_out.dtype)
+    fwd_out[...] = (pair[:rows].astype(f32) + branch).astype(fwd_out.dtype)
     scaled = (part[rows : 2 * rows] + came[rows:].astype(f32)) * gain[...]
-    nhat = tail[2]
-    d_input = tail_rstd[:, :1] * (
+    nhat = nhat_in[...]
+    d_input = rstd[:, :1] * (
         scaled
         - jnp.mean(scaled, axis=-1, keepdims=True)
         - nhat * jnp.mean(scaled * nhat, axis=-1, keepdims=True)
     )
-    bwd_out[...] = (tail[1] + d_input).astype(bwd_out.dtype)
+    bwd_out[...] = (pair[rows:].astype(f32) + d_input).astype(bwd_out.dtype)
 
 
 def on_device(sent_fwd, sent_bwd, stash, gain, w_in, w_out):
@@ -205,34 +222,55 @@
     masks = [(1 << bit) | 1 for bit in range(bits - 1, 0, -1)]
     rows, width = sent_fwd.shape[2], sent_fwd.shape[3]
     units = w_in.shape[2]
-    fwd_in = lax.ppermute(sent_fwd[0, 0], AXES, relay_pairs(sections, mirrors, count, 0, 1))
-    bwd_in = lax.ppermute(sent_bwd[0, 0], AXES, relay_pairs(sections, mirrors, count, 0, -1))
-    w_first = loaded(w_in[0], 4)
-    fwd_in, bwd_in, w_first = lax.optimization_barrier((fwd_in, bwd_in, w_first))
-    w_second = loaded(w_out[0], 4)
-    peer_first = lax.ppermute(w_first, "dp", xor_pairs(count, 1))
-    peer_second = lax.ppermute(w_second, "dp", xor_pairs(count, 1))
-    tail, tail_rstd = pl.pallas_call(
+    onward, back = [relay_pairs(sections, mirrors, count, 0, sign) for sign in (1, -1)]
+    if onward == back:
+        pair = jnp.concatenate([sent_fwd[0, 0], sent_bwd[0, 0]], axis=0)
+        pair = lax.ppermute(pair, AXES, onward)
+    else:
+        fwd_in = lax.ppermute(sent_fwd[0, 0], AXES, onward)
+        bwd_in = lax.ppermute(sent_bwd[0, 0], AXES, back)
+        pair = jnp.concatenate([fwd_in, bwd_in], axis=0)
+    nhat, rstd = pl.pallas_call(
         row_kernel,
         out_shape=(
-            jax.ShapeDtypeStruct((3, rows, width), jnp.float32),
+            jax.ShapeDtypeStruct((rows, width), jnp.float32),
             jax.ShapeDtypeStruct((rows, 128), jnp.float32),
         ),
-        in_specs=[VMEM] * 3,
+        in_specs=[VMEM],
         out_specs=[VMEM] * 2,
         compiler_params=pltpu.CompilerParams(vmem_limit_bytes=max(4 << 20, 40 * rows * width * 4)),
-    )(fwd_in, bwd_in, stash[0, 0])
-    held = jnp.stack([fwd_in, bwd_in, stash[0, 0]])
+    )(stash[0, 0])
+    w_second = loaded(w_out[0], 4)
+    peer_second = lax.ppermute(w_second, "dp", xor_pairs(count, 1))
+    pair, w_second, source = lax.optimization_barrier((pair, w_second, w_in[0]))
+    peer_first = lax.ppermute(source, "dp", xor_pairs(count, 1))
+    w_first = loaded(w_in[0], 4)
+    held = pl.pallas_call(
+        functools.partial(stack_kernel, rows),
+        out_shape=jax.ShapeDtypeStruct((3 * rows, width), jnp.bfloat16),
+        in_specs=[VMEM] * 2,
+        out_specs=VMEM,
+        compiler_params=pltpu.CompilerParams(vmem_limit_bytes=max(4 << 20, 24 * rows * width)),
+    )(pair, stash[0, 0])
+    slots = rows
     for mask in masks:
-        flat = held.reshape(-1, width) if held.shape[1] == 1 else held
-        other = lax.ppermute(flat, "dp", xor_pairs(count, mask)).reshape(held.shape)
+        other = lax.ppermute(held, "dp", xor_pairs(count, mask))
         if mask == masks[0]:
-            other, w_second, tail, tail_rstd = lax.optimization_barrier((other, w_second, tail, tail_rstd))
             weights = prepared(w_first, peer_first, w_second, peer_second)
         if mask == masks[-1]:
             other, *weights = lax.optimization_barrier((other, *weights))
-        held = jnp.concatenate([held, other], axis=1)
-    half = held.shape[1]
+            break
+        slots *= 2
+        held = pl.pallas_call(
+            merge_kernel,
+            out_shape=jax.ShapeDtypeStruct((3, slots, width), jnp.bfloat16),
+            in_specs=[VMEM] * 2,
+            out_specs=VMEM,
+            compiler_params=pltpu.CompilerParams(vmem_limit_bytes=max(4 << 20, 48 * slots * width)),
+        )(held, other)
+        if mask == masks[0]:
+            held, w_first, nhat, rstd = lax.optimization_barrier((held, w_first, nhat, rstd))
+    half = 2 * slots
     limit = pltpu.CompilerParams(vmem_limit_bytes=max(8 << 20, 40 * half * width * 4))
     send, keep, full = pl.pallas_call(
         functools.partial(block_kernel, rows),
@@ -241,11 +279,11 @@
             jax.ShapeDtypeStruct((half, width), jnp.float32),
             jax.ShapeDtypeStruct((half, 2 * width + 4 * units), jnp.bfloat16),
         ),
-        in_specs=[VMEM] * 5,
+        in_specs=[VMEM] * 6,
         out_specs=[VMEM] * 3,
         scratch_shapes=[pltpu.VMEM((2 * half, 4 * units), jnp.float32)],
         compiler_params=limit,
-    )(held, gain, *weights)
+    )(held, other, gain, *weights)
     peer = lax.ppermute(full, "dp", xor_pairs(count, 1))
     low = jax.ShapeDtypeStruct((2 * half, width + 2 * units), jnp.bfloat16)
     own, away = pl.pallas_call(
@@ -285,10 +323,10 @@
     fwd_out, bwd_out = pl.pallas_call(
         functools.partial(tail_kernel, rows),
         out_shape=(jax.ShapeDtypeStruct((rows, width), jnp.bfloat16),) * 2,
-        in_specs=[VMEM] * 5,
+        in_specs=[VMEM] * 6,
         out_specs=[VMEM] * 2,
         compiler_params=pltpu.CompilerParams(vmem_limit_bytes=max(4 << 20, 40 * rows * width * 4)),
-    )(part, came, gain, tail, tail_rstd)
+    )(part, came, gain, pair, nhat, rstd)
     return (fwd_out[None, None], bwd_out[None, None], grad_first[None], grad_second[None])
 
 

time: 26.6 us -> 25.6 us (0.962)
  waiting for transfers between devices: 3.6 us -> 2.48 us
  other arithmetic: 0.39 us -> 0.8 us
  local copies, waits for them, and re-layouts: 2.36 us -> 1.99 us
    ppermute x5 -> x4, waiting for transfers between devices: 2.98 us -> 1.86 us  [the longest x2 1.56 us: on_device(): other = lax.ppermute(held, 'dp', xor_pairs(count, mask))]
    concatenate x2 -> x1, other arithmetic: 0.29 us -> 0.78 us  [on_device(): pair = jnp.concatenate([sent_fwd[0, 0], sent_bwd[0, 0]], axis=0)]
    unnamed x9 -> x8, local copies, waits for them, and re-layouts: 2.29 us -> 1.97 us
    ppermute x5 -> x4, starting transfers between devices: 7.54 us -> 7.46 us  [the longest x2 4.46 us: on_device(): other = lax.ppermute(held, 'dp', xor_pairs(count, mask))]
  transfers between devices with their start and end apart: 10 -> 9, of which waited for: 5 -> 5; matrix products, arithmetic and copies ran while one was open for 1% -> 0% of each run, Pallas kernels for 13% -> 14%
where the time goes in v6:
time: 25.6 us; the launch traced here: 25.3 us
  starting transfers between devices  13.6 us (53%)
  Pallas kernels  5.75 us (22%)
  waiting for transfers between devices  2.48 us (10%)
  local copies, waits for them, and re-layouts  1.99 us (8%)
  other arithmetic  0.8 us (3%)
  between operations  0.73 us (3%)
    ppermute x2, starting transfers between devices, on_device(): other = lax.ppermute(held, 'dp', xor_pairs(count, mask))  4.46 us
    ppermute x2, starting transfers between devices, on_device(): came = lax.ppermute(send, 'dp', xor_pairs(count, mask))  4.01 us
    ppermute x1, starting transfers between devices, on_device(): pair = lax.ppermute(pair, AXES, onward)  3 us
    unnamed x8, local copies, waits for them, and re-layouts  1.97 us
    ppermute x1, starting transfers between devices, on_device(): far = lax.ppermute(away, 'mirror', xor_pairs(mirrors, 1))  1.58 us
    ppermute x2, waiting for transfers between devices, on_device(): other = lax.ppermute(held, 'dp', xor_pairs(count, mask))  1.56 us
    pallas_call x1, Pallas kernels, on_device(): pl.pallas_call(functools.partial(block_kernel, rows), out_shape=(jax.Shap...  1.55 us
    pallas_call x1, Pallas kernels, prepared(): pl.pallas_call(prepare_kernel, out_shape=(jax.ShapeDtypeStruct((width, 2...  1.55 us
  transfers between devices with their start and end apart: 9, of which 5 were waited for; matrix products, arithmetic and copies ran while one was open for 0% of the time, Pallas kernels for 14%

profile of v6, /device:TPU:0, one launch (start us, length us, event | category | flops | bytes accessed | tf_op | source)
XLA Modules:
  0.0 25.3 jit_solution(5434424867559111834)
XLA Ops:
  0.6 0.0 copy-start.3
  0.6 0.8 %pad_maximum_fusion = bf16[2,4096]{1,0:T(2,128)(2,1)S(1)} fusion(bf16[1,4096]{1,0:T(2,128)(2,1)} %bitcast.14, bf16[1,4096]{1,0:T(2,128)(2,1)} %bitcast.15), kind=kLoop, calls=%fused_computation.2 | loop fusion | flops 32768 | bytes 32768 | tf_op jit(solution)/shard_map/concatenate | solution.py:227
  1.4 3.0 %collective-permute-start = (bf16[2,4096]{1,0:T(2,128)(2,1)S(1)}, bf16[2,4096]{1,0:T(2,128)(2,1)S(1)}, u32[]{:S(2)}, u32[]{:S(2)}) collective-permute-start(bf16[2,4096]{1,0:T(2,128)(2,1)S(1)} %pad_maximum_fusion), channel_id=1, source_target_pairs={{0,16},{1,17},{2,18},{3,19},{4,20},{5,21},{6,22},{7,23},{8,24},{9,... | collective-permute-start | bytes 49160 | tf_op jit(solution)/shard_map/ppermute | solution.py:228
  4.4 1.2 %copy-done = bf16[1,128,4096]{2,1,0:T(8,128)(2,1)S(1)} copy-done((bf16[1,128,4096]{2,1,0:T(8,128)(2,1)S(1)}, bf16[1,128,4096]{2,1,0:T(8,128)(2,1)}, u32[]{:S(2)}) %copy-start) | copy-done | bytes 1048600
  5.7 0.1 shard_map.93.out_own
  5.8 0.1 collective-permute-start.4
  5.9 0.3 %collective-permute-done.pair = bf16[2,4096]{1,0:T(2,128)(2,1)S(1)} collective-permute-done((bf16[2,4096]{1,0:T(2,128)(2,1)S(1)}, bf16[2,4096]{1,0:T(2,128)(2,1)S(1)}, u32[]{:S(2)}, u32[]{:S(2)}) %collective-permute-start) | collective-permute-done | bytes 16416 | tf_op jit(solution)/shard_map/ppermute | solution.py:228
  6.1 0.7 %copy-done.1 = bf16[1,4096,128]{2,1,0:T(8,128)(2,1)S(1)} copy-done((bf16[1,4096,128]{2,1,0:T(8,128)(2,1)S(1)}, bf16[1,4096,128]{2,1,0:T(8,128)(2,1)}, u32[]{:S(2)}) %copy-start.1) | copy-done | bytes 1048600
  6.9 0.0 collective-permute-start.3
  6.9 0.0 copy-done.3
  6.9 2.8 %collective-permute-start.1 = (bf16[3,4096]{1,0:T(4,128)(2,1)S(1)}, bf16[3,4096]{1,0:T(4,128)(2,1)S(1)}, u32[]{:S(2)}, u32[]{:S(2)}) collective-permute-start(bf16[3,4096]{1,0:T(4,128)(2,1)S(1)} %shard_map.94.held), channel_id=1, source_target_pairs={{0,5},{1,4},{2,7},{3,6},{4,1},{5,0},{6,3},{7,2},{8,13},{9,12},{10,... | collective-permute-start | bytes 73736 | tf_op jit(solution)/shard_map/ppermute | solution.py:257
  9.7 0.2 shard_map.97
  9.9 0.1 shard_map.96.in_own
  10.0 1.2 %collective-permute-done.1.other = bf16[3,4096]{1,0:T(4,128)(2,1)S(1)} collective-permute-done((bf16[3,4096]{1,0:T(4,128)(2,1)S(1)}, bf16[3,4096]{1,0:T(4,128)(2,1)S(1)}, u32[]{:S(2)}, u32[]{:S(2)}) %collective-permute-start.1) | collective-permute-done | bytes 24608 | tf_op jit(solution)/shard_map/ppermute | solution.py:257
  11.3 0.1 shard_map.95.held
  11.3 0.0 copy-start.2
  11.4 1.7 %collective-permute-start.2 = (bf16[3,2,4096]{2,1,0:T(2,128)(2,1)S(1)}, bf16[3,2,4096]{2,1,0:T(2,128)(2,1)S(1)}, u32[]{:S(2)}, u32[]{:S(2)}) collective-permute-start(bf16[3,2,4096]{2,1,0:T(2,128)(2,1)S(1)} %shard_map.95.held), channel_id=1, source_target_pairs={{0,3},{1,2},{2,1},{3,0},{4,7},{5,6},{6,5},{7,4},{8,11},{9,10},{10,... | collective-permute-start | bytes 147464 | tf_op jit(solution)/shard_map/ppermute | solution.py:257
  13.0 0.0 collective-permute-done.4.out_peer
  13.0 0.0 collective-permute-done.3.in_peer
  13.1 1.6 %shard_map.98 = (bf16[4096,256]{1,0:T(8,128)(2,1)S(1)}, bf16[4096,256]{1,0:T(8,128)(2,1)S(1)}, bf16[512,4096]{1,0:T(8,128)(2,1)S(1)}) custom-call(bf16[4096,128]{1,0:T(8,128)(2,1)S(1)} %shard_map.96.in_own, bf16[4096,128]{1,0:T(8,128)(2,1)S(1)} %collective-permute-done.3.in_peer, bf16[128,4096]{1,0:T(8,128)(2,1)S(1)} %shard_map.93.out_own, ...), custom_call_target="tpu_custom_call" | custom-call | bytes 6291456 | tf_op jit(solution)/shard_map/pallas_call | solution.py:168
  14.6 0.3 %collective-permute-done.2.other = bf16[3,2,4096]{2,1,0:T(2,128)(2,1)S(1)} collective-permute-done((bf16[3,2,4096]{2,1,0:T(2,128)(2,1)S(1)}, bf16[3,2,4096]{2,1,0:T(2,128)(2,1)S(1)}, u32[]{:S(2)}, u32[]{:S(2)}) %collective-permute-start.2) | collective-permute-done | bytes 49184 | tf_op jit(solution)/shard_map/ppermute | solution.py:257
  14.9 1.6 %shard_map.99 = (bf16[4,4096]{1,0:T(4,128)(2,1)S(1)}, f32[4,4096]{1,0:T(4,128)S(1)}, bf16[4,8704]{1,0:T(4,128)(2,1)S(1)}) custom-call(bf16[3,2,4096]{2,1,0:T(2,128)(2,1)S(1)} %shard_map.95.held, bf16[3,2,4096]{2,1,0:T(2,128)(2,1)S(1)} %collective-permute-done.2.other, f32[1,4096]{1,0:T(1,128)S(1)} %copy-done.2, ...), custom_call_target="tpu_custom_call" | custom-call | tf_op jit(solution)/shard_map/pallas_call | solution.py:275
  16.5 0.5 %collective-permute-start.6 = (bf16[4,8704]{1,0:T(4,128)(2,1)S(1)}, bf16[4,8704]{1,0:T(4,128)(2,1)S(1)}, u32[]{:S(2)}, u32[]{:S(2)}) collective-permute-start(bf16[4,8704]{1,0:T(4,128)(2,1)S(1)} %get-tuple-element.46.full), channel_id=1, source_target_pairs={{0,1},{1,0},{2,3},{3,2},{4,5},{5,4},{6,7},{7,6},{8,9},{9,8},{10,11... | collective-permute-start | bytes 208904 | tf_op jit(solution)/shard_map/ppermute | solution.py:287
  16.9 1.5 %collective-permute-start.5 = (bf16[4,4096]{1,0:T(4,128)(2,1)S(1)}, bf16[4,4096]{1,0:T(4,128)(2,1)S(1)}, u32[]{:S(2)}, u32[]{:S(2)}) collective-permute-start(bf16[4,4096]{1,0:T(4,128)(2,1)S(1)} %get-tuple-element.45), channel_id=1, source_target_pairs={{0,3},{1,2},{2,1},{3,0},{4,7},{5,6},{6,5},{7,4},{8,11},{9,10},{10,... | collective-permute-start | bytes 98312 | tf_op jit(solution)/shard_map/ppermute | solution.py:298
  18.4 0.0 collective-permute-done.6.peer
  18.5 1.6 %collective-permute-start.7 = (bf16[8,4352]{1,0:T(8,128)(2,1)S(1)}, bf16[8,4352]{1,0:T(8,128)(2,1)S(1)}, u32[]{:S(2)}, u32[]{:S(2)}) collective-permute-start(bf16[8,4352]{1,0:T(8,128)(2,1)S(1)} %get-tuple-element.48), channel_id=1, source_target_pairs={{0,8},{8,0},{1,9},{9,1},{2,10},{10,2},{3,11},{11,3},{4,12},{12,4},... | collective-permute-start | bytes 208904 | tf_op jit(solution)/shard_map/ppermute | solution.py:303
  20.0 0.4 %collective-permute-done.5 = bf16[4,4096]{1,0:T(4,128)(2,1)S(1)} collective-permute-done((bf16[4,4096]{1,0:T(4,128)(2,1)S(1)}, bf16[4,4096]{1,0:T(4,128)(2,1)S(1)}, u32[]{:S(2)}, u32[]{:S(2)}) %collective-permute-start.5) | collective-permute-done | bytes 32800 | tf_op jit(solution)/shard_map/ppermute | solution.py:298
  20.4 2.6 %collective-permute-start.8 = (bf16[2,4096]{1,0:T(2,128)(2,1)S(1)}, bf16[2,4096]{1,0:T(2,128)(2,1)S(1)}, u32[]{:S(2)}, u32[]{:S(2)}) collective-permute-start(bf16[2,4096]{1,0:T(2,128)(2,1)S(1)} %slice.7), channel_id=1, source_target_pairs={{0,5},{1,4},{2,7},{3,6},{4,1},{5,0},{6,3},{7,2},{8,13},{9,12},{10,... | collective-permute-start | bytes 49160 | tf_op jit(solution)/shard_map/ppermute | solution.py:298
  23.0 0.0 collective-permute-done.7.far
  23.0 1.3 %shard_map.101 = (bf16[2048,128]{1,0:T(8,128)(2,1)}, bf16[128,2048]{1,0:T(8,128)(2,1)}) custom-call(bf16[8,4352]{1,0:T(8,128)(2,1)S(1)} %get-tuple-element.47.own, bf16[8,4352]{1,0:T(8,128)(2,1)S(1)} %collective-permute-done.7.far), custom_call_target="tpu_custom_call" | custom-call | bytes 2097152 | tf_op jit(solution)/shard_map/pallas_call | solution.py:305
  24.3 0.3 %collective-permute-done.8.came = bf16[2,4096]{1,0:T(2,128)(2,1)S(1)} collective-permute-done((bf16[2,4096]{1,0:T(2,128)(2,1)S(1)}, bf16[2,4096]{1,0:T(2,128)(2,1)S(1)}, u32[]{:S(2)}, u32[]{:S(2)}) %collective-permute-start.8) | collective-permute-done | bytes 16416 | tf_op jit(solution)/shard_map/ppermute | solution.py:298
  24.6 0.7 %shard_map.102 = (bf16[1,4096]{1,0:T(2,128)(2,1)}, bf16[1,4096]{1,0:T(2,128)(2,1)}) custom-call(f32[4,4096]{1,0:T(4,128)S(1)} %convert_add_fusion.part, bf16[2,4096]{1,0:T(2,128)(2,1)S(1)} %collective-permute-done.8.came, f32[1,4096]{1,0:T(1,128)S(1)} %copy-done.2, bf16[2,4096]{1,0:T(2,128)(2,1)S(1)} %collective-permute-done.pair, ...), custom_call_target="tpu_custom_call" | custom-call | tf_op jit(solution)/shard_map/pallas_call | solution.py:323
  (7 shorter events, 0.1 us)
Async XLA Ops:
  0.6 6.3 %copy-start.3 = (bf16[1,1,1,4096]{3,2,1,0:T(2,128)(2,1)S(1)}, bf16[1,1,1,4096]{3,2,1,0:T(2,128)(2,1)}, u32[]{:S(2)}) copy-start(bf16[1,1,1,4096]{3,2,1,0:T(2,128)(2,1)} %param.8) | copy-start | bytes 24580
  1.4 4.7 %collective-permute-start = (bf16[2,4096]{1,0:T(2,128)(2,1)S(1)}, bf16[2,4096]{1,0:T(2,128)(2,1)S(1)}, u32[]{:S(2)}, u32[]{:S(2)}) collective-permute-start(bf16[2,4096]{1,0:T(2,128)(2,1)S(1)} %pad_maximum_fusion), channel_id=1, source_target_pairs={{0,16},{1,17},{2,18},{3,19},{4,20},{5,21},{6,22},{7,23},{8,24},{9,... | collective-permute-start | bytes 49160 | tf_op jit(solution)/shard_map/ppermute | solution.py:228
  4.4 1.2 %copy-start = (bf16[1,128,4096]{2,1,0:T(8,128)(2,1)S(1)}, bf16[1,128,4096]{2,1,0:T(8,128)(2,1)}, u32[]{:S(2)}) copy-start(bf16[1,128,4096]{2,1,0:T(8,128)(2,1)} %param.11) | copy-start | bytes 3145732
  5.7 1.2 %copy-start.1 = (bf16[1,4096,128]{2,1,0:T(8,128)(2,1)S(1)}, bf16[1,4096,128]{2,1,0:T(8,128)(2,1)}, u32[]{:S(2)}) copy-start(bf16[1,4096,128]{2,1,0:T(8,128)(2,1)} %param.10) | copy-start | bytes 3145732
  5.8 7.3 %collective-permute-start.4 = (bf16[128,4096]{1,0:T(8,128)(2,1)S(1)}, bf16[128,4096]{1,0:T(8,128)(2,1)S(1)}, u32[]{:S(2)}, u32[]{:S(2)}) collective-permute-start(bf16[128,4096]{1,0:T(8,128)(2,1)S(1)} %shard_map.93.out_own), channel_id=1, source_target_pairs={{0,1},{1,0},{2,3},{3,2},{4,5},{5,4},{6,7},{7,6},{8,9},{9,8},{10,11... | collective-permute-start | bytes 3145736 | tf_op jit(solution)/shard_map/ppermute | solution.py:244
  6.9 6.2 %collective-permute-start.3 = (bf16[4096,128]{1,0:T(8,128)(2,1)S(1)}, bf16[4096,128]{1,0:T(8,128)(2,1)S(1)}, u32[]{:S(2)}, u32[]{:S(2)}) collective-permute-start(bf16[4096,128]{1,0:T(8,128)(2,1)S(1)} %bitcast.10), channel_id=1, source_target_pairs={{0,1},{1,0},{2,3},{3,2},{4,5},{5,4},{6,7},{7,6},{8,9},{9,8},{10,11... | collective-permute-start | bytes 3145736 | tf_op jit(solution)/shard_map/ppermute | solution.py:246
  6.9 4.4 %collective-permute-start.1 = (bf16[3,4096]{1,0:T(4,128)(2,1)S(1)}, bf16[3,4096]{1,0:T(4,128)(2,1)S(1)}, u32[]{:S(2)}, u32[]{:S(2)}) collective-permute-start(bf16[3,4096]{1,0:T(4,128)(2,1)S(1)} %shard_map.94.held), channel_id=1, source_target_pairs={{0,5},{1,4},{2,7},{3,6},{4,1},{5,0},{6,3},{7,2},{8,13},{9,12},{10,... | collective-permute-start | bytes 73736 | tf_op jit(solution)/shard_map/ppermute | solution.py:257
  11.3 3.6 %copy-start.2 = (f32[1,4096]{1,0:T(1,128)S(1)}, f32[1,4096]{1,0:T(1,128)}, u32[]{:S(2)}) copy-start(f32[1,4096]{1,0:T(1,128)} %gain.3) | copy-start | bytes 49156
  11.4 3.6 %collective-permute-start.2 = (bf16[3,2,4096]{2,1,0:T(2,128)(2,1)S(1)}, bf16[3,2,4096]{2,1,0:T(2,128)(2,1)S(1)}, u32[]{:S(2)}, u32[]{:S(2)}) collective-permute-start(bf16[3,2,4096]{2,1,0:T(2,128)(2,1)S(1)} %shard_map.95.held), channel_id=1, source_target_pairs={{0,3},{1,2},{2,1},{3,0},{4,7},{5,6},{6,5},{7,4},{8,11},{9,10},{10,... | collective-permute-start | bytes 147464 | tf_op jit(solution)/shard_map/ppermute | solution.py:257
  16.5 1.9 %collective-permute-start.6 = (bf16[4,8704]{1,0:T(4,128)(2,1)S(1)}, bf16[4,8704]{1,0:T(4,128)(2,1)S(1)}, u32[]{:S(2)}, u32[]{:S(2)}) collective-permute-start(bf16[4,8704]{1,0:T(4,128)(2,1)S(1)} %get-tuple-element.46.full), channel_id=1, source_target_pairs={{0,1},{1,0},{2,3},{3,2},{4,5},{5,4},{6,7},{7,6},{8,9},{9,8},{10,11... | collective-permute-start | bytes 208904 | tf_op jit(solution)/shard_map/ppermute | solution.py:287
  16.9 3.4 %collective-permute-start.5 = (bf16[4,4096]{1,0:T(4,128)(2,1)S(1)}, bf16[4,4096]{1,0:T(4,128)(2,1)S(1)}, u32[]{:S(2)}, u32[]{:S(2)}) collective-permute-start(bf16[4,4096]{1,0:T(4,128)(2,1)S(1)} %get-tuple-element.45), channel_id=1, source_target_pairs={{0,3},{1,2},{2,1},{3,0},{4,7},{5,6},{6,5},{7,4},{8,11},{9,10},{10,... | collective-permute-start | bytes 98312 | tf_op jit(solution)/shard_map/ppermute | solution.py:298
  18.5 4.5 %collective-permute-start.7 = (bf16[8,4352]{1,0:T(8,128)(2,1)S(1)}, bf16[8,4352]{1,0:T(8,128)(2,1)S(1)}, u32[]{:S(2)}, u32[]{:S(2)}) collective-permute-start(bf16[8,4352]{1,0:T(8,128)(2,1)S(1)} %get-tuple-element.48), channel_id=1, source_target_pairs={{0,8},{8,0},{1,9},{9,1},{2,10},{10,2},{3,11},{11,3},{4,12},{12,4},... | collective-permute-start | bytes 208904 | tf_op jit(solution)/shard_map/ppermute | solution.py:303
  20.4 4.1 %collective-permute-start.8 = (bf16[2,4096]{1,0:T(2,128)(2,1)S(1)}, bf16[2,4096]{1,0:T(2,128)(2,1)S(1)}, u32[]{:S(2)}, u32[]{:S(2)}) collective-permute-start(bf16[2,4096]{1,0:T(2,128)(2,1)S(1)} %slice.7), channel_id=1, source_target_pairs={{0,5},{1,4},{2,7},{3,6},{4,1},{5,0},{6,3},{7,2},{8,13},{9,12},{10,... | collective-permute-start | bytes 49160 | tf_op jit(solution)/shard_map/ppermute | solution.py:298

commit v7 on v6

--- a/solution.py
+++ b/solution.py
@@ -48,13 +48,25 @@
     return lax.dot_general(left, right, ((contract[:1], contract[1:]), ((), ())), preferred_element_type=jnp.float32)
 
 
-def block_kernel(rows, held, other, gain, w_in, w_out_t, tall, send, keep, full, leaving):
-    count, width = 2 * held.shape[1], held.shape[2]
+def of_array(ref, array):
+    if len(ref.shape) == 3:
+        return ref[array].astype(jnp.float32)
+    rows = ref.shape[0] // 3
+    return ref[array * rows : (array + 1) * rows].astype(jnp.float32)
+
+
+def block_kernel(rows, outer, second, fourth, gain, w_in, w_out_t, tall, send, keep, full, leaving):
+    count, width = keep.shape
     units = w_in.shape[1]
     f32, bf16 = jnp.float32, jnp.bfloat16
 
     def joined(*arrays):
-        return jnp.concatenate([piece[array].astype(f32) for array in arrays for piece in (held, other)], axis=0)
+        pieces = []
+        for array in arrays:
+            both = of_array(outer, array)
+            near = both.shape[0] // 2
+            pieces += [both[:near], of_array(second, array), both[near:], of_array(fourth, array)]
+        return jnp.concatenate(pieces, axis=0)
 
     cotan = joined(1).astype(bf16)
     d_acted = dot(cotan, w_out_t[...], (1, 0))
@@ -93,12 +105,8 @@
 
 
 def merge_kernel(held, other, merged):
-    count = merged.shape[1] // 2
     for array in range(3):
-        pieces = [
-            (ref[array] if len(ref.shape) == 3 else ref[array * count : (array + 1) * count]).astype(jnp.float32)
-            for ref in (held, other)
-        ]
+        pieces = [of_array(ref, array) for ref in (held, other)]
         merged[array] = jnp.concatenate(pieces, axis=0).astype(merged.dtype)
 
 
@@ -240,26 +248,25 @@
         out_specs=[VMEM] * 2,
         compiler_params=pltpu.CompilerParams(vmem_limit_bytes=max(4 << 20, 40 * rows * width * 4)),
     )(stash[0, 0])
+    peer_first, peer_second = [lax.ppermute(source, "dp", xor_pairs(count, 1)) for source in (w_in[0], w_out[0])]
+    w_first = loaded(w_in[0], 4)
+    pair, w_first = lax.optimization_barrier((pair, w_first))
     w_second = loaded(w_out[0], 4)
-    peer_second = lax.ppermute(w_second, "dp", xor_pairs(count, 1))
-    pair, w_second, source = lax.optimization_barrier((pair, w_second, w_in[0]))
-    peer_first = lax.ppermute(source, "dp", xor_pairs(count, 1))
-    w_first = loaded(w_in[0], 4)
     held = pl.pallas_call(
         functools.partial(stack_kernel, rows),
         out_shape=jax.ShapeDtypeStruct((3 * rows, width), jnp.bfloat16),
         in_specs=[VMEM] * 2,
         out_specs=VMEM,
         compiler_params=pltpu.CompilerParams(vmem_limit_bytes=max(4 << 20, 24 * rows * width)),
+        cost_estimate=pl.CostEstimate(flops=20 * 10**9, bytes_accessed=10**5, transcendentals=0),
     )(pair, stash[0, 0])
     slots = rows
-    for mask in masks:
-        other = lax.ppermute(held, "dp", xor_pairs(count, mask))
-        if mask == masks[0]:
-            weights = prepared(w_first, peer_first, w_second, peer_second)
-        if mask == masks[-1]:
-            other, *weights = lax.optimization_barrier((other, *weights))
-            break
+
+    def from_peer(value, mask):
+        return lax.ppermute(value, "dp", xor_pairs(count, mask))
+
+    for mask in masks[:-2]:
+        other = from_peer(held, mask)
         slots *= 2
         held = pl.pallas_call(
             merge_kernel,
@@ -268,8 +275,21 @@
             out_specs=VMEM,
             compiler_params=pltpu.CompilerParams(vmem_limit_bytes=max(4 << 20, 48 * slots * width)),
         )(held, other)
-        if mask == masks[0]:
-            held, w_first, nhat, rstd = lax.optimization_barrier((held, w_first, nhat, rstd))
+    second = from_peer(held, masks[-2])
+    third = from_peer(held, masks[-1])
+    second, w_second, nhat, rstd = lax.optimization_barrier((second, w_second, nhat, rstd))
+    fourth = from_peer(second, masks[-1])
+    weights = prepared(w_first, peer_first, w_second, peer_second)
+    fourth, *weights = lax.optimization_barrier((fourth, *weights))
+    slots *= 2
+    outer = pl.pallas_call(
+        merge_kernel,
+        out_shape=jax.ShapeDtypeStruct((3, slots, width), jnp.bfloat16),
+        in_specs=[VMEM] * 2,
+        out_specs=VMEM,
+        compiler_params=pltpu.CompilerParams(vmem_limit_bytes=max(4 << 20, 48 * slots * width)),
+        cost_estimate=pl.CostEstimate(flops=10 * 10**9, bytes_accessed=10**5, transcendentals=0),
+    )(held, third)
     half = 2 * slots
     limit = pltpu.CompilerParams(vmem_limit_bytes=max(8 << 20, 40 * half * width * 4))
     send, keep, full = pl.pallas_call(
@@ -279,11 +299,11 @@
             jax.ShapeDtypeStruct((half, width), jnp.float32),
             jax.ShapeDtypeStruct((half, 2 * width + 4 * units), jnp.bfloat16),
         ),
-        in_specs=[VMEM] * 6,
+        in_specs=[VMEM] * 7,
         out_specs=[VMEM] * 3,
         scratch_shapes=[pltpu.VMEM((2 * half, 4 * units), jnp.float32)],
         compiler_params=limit,
-    )(held, other, gain, *weights)
+    )(outer, second, fourth, gain, *weights)
     peer = lax.ppermute(full, "dp", xor_pairs(count, 1))
     low = jax.ShapeDtypeStruct((2 * half, width + 2 * units), jnp.bfloat16)
     own, away = pl.pallas_call(

time: 25.6 us -> 25 us (0.977)
  starting transfers between devices: 13.6 us -> 15.3 us
  waiting for transfers between devices: 2.48 us -> 0.83 us
  local copies, waits for them, and re-layouts: 1.99 us -> 1.26 us
    ppermute x4 -> x5, starting transfers between devices: 4.53 us -> 6.39 us  [the longest x3 5.88 us: from_peer(): return lax.ppermute(value, 'dp', xor_pairs(count, mask))]
    ppermute x4 -> x5, waiting for transfers between devices: 1.57 us -> 0.36 us  [the longest x3 0.36 us: from_peer(): return lax.ppermute(value, 'dp', xor_pairs(count, mask))]
    unnamed x8, local copies, waits for them, and re-layouts: 1.97 us -> 1.24 us
    ppermute x1, starting transfers between devices: 0.45 us -> 0.12 us  [on_device(): peer = lax.ppermute(full, 'dp', xor_pairs(count, 1))]
    ppermute x1, waiting for transfers between devices: 0.29 us -> 0.01 us  [on_device(): pair = lax.ppermute(pair, AXES, onward)]
  transfers between devices with their start and end apart: 9 -> 10, of which waited for: 5 -> 3; matrix products, arithmetic and copies ran while one was open for 0% -> 0% of each run, Pallas kernels for 14% -> 14%
where the time goes in v7:
time: 25 us; the launch traced here: 24.8 us
  starting transfers between devices  15.3 us (61%)
  Pallas kernels  5.79 us (23%)
  local copies, waits for them, and re-layouts  1.26 us (5%)
  waiting for transfers between devices  0.83 us (3%)
  other arithmetic  0.8 us (3%)
  between operations  0.77 us (3%)
    ppermute x3, starting transfers between devices, from_peer(): return lax.ppermute(value, 'dp', xor_pairs(count, mask))  5.88 us
    ppermute x2, starting transfers between devices, on_device(): came = lax.ppermute(send, 'dp', xor_pairs(count, mask))  4.23 us
    ppermute x1, starting transfers between devices, on_device(): pair = lax.ppermute(pair, AXES, onward)  3 us
    pallas_call x1, Pallas kernels, on_device(): pl.pallas_call(functools.partial(block_kernel, rows), out_shape=(jax.Shap...  1.59 us
    ppermute x1, starting transfers between devices, on_device(): far = lax.ppermute(away, 'mirror', xor_pairs(mirrors, 1))  1.58 us
    pallas_call x1, Pallas kernels, prepared(): pl.pallas_call(prepare_kernel, out_shape=(jax.ShapeDtypeStruct((width, 2...  1.55 us
    pallas_call x1, Pallas kernels, on_device(): pl.pallas_call(functools.partial(outer_kernel, 8), out_shape=(jax.ShapeDt...  1.31 us
    unnamed x8, local copies, waits for them, and re-layouts  1.24 us
  transfers between devices with their start and end apart: 10, of which 3 were waited for; matrix products, arithmetic and copies ran while one was open for 0% of the time, Pallas kernels for 14%

profile of v7, /device:TPU:0, one launch (start us, length us, event | category | flops | bytes accessed | tf_op | source)
XLA Modules:
  0.0 24.8 jit_solution(11995028017337333820)
XLA Ops:
  0.6 0.8 %pad_maximum_fusion = bf16[2,4096]{1,0:T(2,128)(2,1)S(1)} fusion(bf16[1,4096]{1,0:T(2,128)(2,1)} %bitcast.15, bf16[1,4096]{1,0:T(2,128)(2,1)} %bitcast.16), kind=kLoop, calls=%fused_computation.2 | loop fusion | flops 32768 | bytes 32768 | tf_op jit(solution)/shard_map/concatenate | solution.py:235
  1.4 3.0 %collective-permute-start = (bf16[2,4096]{1,0:T(2,128)(2,1)S(1)}, bf16[2,4096]{1,0:T(2,128)(2,1)S(1)}, u32[]{:S(2)}, u32[]{:S(2)}) collective-permute-start(bf16[2,4096]{1,0:T(2,128)(2,1)S(1)} %pad_maximum_fusion), channel_id=1, source_target_pairs={{0,16},{1,17},{2,18},{3,19},{4,20},{5,21},{6,22},{7,23},{8,24},{9,... | collective-permute-start | bytes 49160 | tf_op jit(solution)/shard_map/ppermute | solution.py:236
  4.4 0.0 collective-permute-start.4
  4.4 0.5 %collective-permute-start.5 = (bf16[128,4096]{1,0:T(8,128)(2,1)}, bf16[128,4096]{1,0:T(8,128)(2,1)S(1)}, u32[]{:S(2)}, u32[]{:S(2)}) collective-permute-start(bf16[128,4096]{1,0:T(8,128)(2,1)} %bitcast.11), channel_id=1, source_target_pairs={{0,1},{1,0},{2,3},{3,2},{4,5},{5,4},{6,7},{7,6},{8,9},{9,8},{10,11... | collective-permute-start | bytes 3145736 | tf_op jit(solution)/shard_map/ppermute | solution.py:251
  4.9 1.2 %copy-done = bf16[1,4096,128]{2,1,0:T(8,128)(2,1)S(1)} copy-done((bf16[1,4096,128]{2,1,0:T(8,128)(2,1)S(1)}, bf16[1,4096,128]{2,1,0:T(8,128)(2,1)}, u32[]{:S(2)}) %copy-start) | copy-done | bytes 1048600
  6.2 0.1 shard_map.93.in_own
  6.3 0.0 collective-permute-done.pair
  6.3 0.0 copy-start.1
  6.3 2.3 %collective-permute-start.2 = (bf16[3,4096]{1,0:T(4,128)(2,1)S(1)}, bf16[3,4096]{1,0:T(4,128)(2,1)S(1)}, u32[]{:S(2)}, u32[]{:S(2)}) collective-permute-start(bf16[3,4096]{1,0:T(4,128)(2,1)S(1)} %shard_map.94.held), channel_id=1, source_target_pairs={{0,5},{1,4},{2,7},{3,6},{4,1},{5,0},{6,3},{7,2},{8,13},{9,12},{10,... | collective-permute-start | bytes 73736 | tf_op jit(solution)/shard_map/ppermute | solution.py:266
  8.6 2.0 %collective-permute-start.1 = (bf16[3,4096]{1,0:T(4,128)(2,1)S(1)}, bf16[3,4096]{1,0:T(4,128)(2,1)S(1)}, u32[]{:S(2)}, u32[]{:S(2)}) collective-permute-start(bf16[3,4096]{1,0:T(4,128)(2,1)S(1)} %shard_map.94.held), channel_id=1, source_target_pairs={{0,3},{1,2},{2,1},{3,0},{4,7},{5,6},{6,5},{7,4},{8,11},{9,10},{10,... | collective-permute-start | bytes 73736 | tf_op jit(solution)/shard_map/ppermute | solution.py:266
  10.6 0.2 shard_map.97
  10.9 0.1 shard_map.96.out_own
  11.0 0.0 collective-permute-done.2.second
  11.0 1.6 %collective-permute-start.3 = (bf16[3,4096]{1,0:T(4,128)(2,1)S(1)}, bf16[3,4096]{1,0:T(4,128)(2,1)S(1)}, u32[]{:S(2)}, u32[]{:S(2)}) collective-permute-start(bf16[3,4096]{1,0:T(4,128)(2,1)S(1)} %collective-permute-done.2.second), channel_id=1, source_target_pairs={{0,3},{1,2},{2,1},{3,0},{4,7},{5,6},{6,5},{7,4},{8,11},{9,10},{10,... | collective-permute-start | bytes 73736 | tf_op jit(solution)/shard_map/ppermute | solution.py:266
  12.6 0.0 collective-permute-done.1.other
  12.6 0.1 shard_map.95.outer
  12.7 0.0 copy-start.2
  12.7 0.0 collective-permute-done.4.in_peer
  12.7 0.0 collective-permute-done.5.out_peer
  12.7 1.6 %shard_map.98 = (bf16[4096,256]{1,0:T(8,128)(2,1)S(1)}, bf16[4096,256]{1,0:T(8,128)(2,1)S(1)}, bf16[512,4096]{1,0:T(8,128)(2,1)S(1)}) custom-call(bf16[4096,128]{1,0:T(8,128)(2,1)S(1)} %shard_map.93.in_own, bf16[4096,128]{1,0:T(8,128)(2,1)S(1)} %collective-permute-done.4.in_peer, bf16[128,4096]{1,0:T(8,128)(2,1)S(1)} %shard_map.96.out_own, ...), custom_call_target="tpu_custom_call" | custom-call | bytes 6291456 | tf_op jit(solution)/shard_map/pallas_call | solution.py:176
  14.3 0.4 %collective-permute-done.3.fourth = bf16[3,4096]{1,0:T(4,128)(2,1)S(1)} collective-permute-done((bf16[3,4096]{1,0:T(4,128)(2,1)S(1)}, bf16[3,4096]{1,0:T(4,128)(2,1)S(1)}, u32[]{:S(2)}, u32[]{:S(2)}) %collective-permute-start.3) | collective-permute-done | bytes 24608 | tf_op jit(solution)/shard_map/ppermute | solution.py:266
  14.6 1.6 %shard_map.99 = (bf16[4,4096]{1,0:T(4,128)(2,1)S(1)}, f32[4,4096]{1,0:T(4,128)S(1)}, bf16[4,8704]{1,0:T(4,128)(2,1)S(1)}) custom-call(bf16[3,2,4096]{2,1,0:T(2,128)(2,1)S(1)} %shard_map.95.outer, bf16[3,4096]{1,0:T(4,128)(2,1)S(1)} %collective-permute-done.2.second, bf16[3,4096]{1,0:T(4,128)(2,1)S(1)} %collective-permute-done.3.fourth, ...), custom_call_target="tpu_custom_call" | custom-call | tf_op jit(solution)/shard_map/pallas_call | solution.py:295
  16.2 0.1 collective-permute-start.7
  16.3 1.4 %collective-permute-start.6 = (bf16[4,4096]{1,0:T(4,128)(2,1)S(1)}, bf16[4,4096]{1,0:T(4,128)(2,1)S(1)}, u32[]{:S(2)}, u32[]{:S(2)}) collective-permute-start(bf16[4,4096]{1,0:T(4,128)(2,1)S(1)} %get-tuple-element.45), channel_id=1, source_target_pairs={{0,3},{1,2},{2,1},{3,0},{4,7},{5,6},{6,5},{7,4},{8,11},{9,10},{10,... | collective-permute-start | bytes 98312 | tf_op jit(solution)/shard_map/ppermute | solution.py:318
  17.7 0.0 collective-permute-done.7.peer
  17.8 1.6 %collective-permute-start.8 = (bf16[8,4352]{1,0:T(8,128)(2,1)S(1)}, bf16[8,4352]{1,0:T(8,128)(2,1)S(1)}, u32[]{:S(2)}, u32[]{:S(2)}) collective-permute-start(bf16[8,4352]{1,0:T(8,128)(2,1)S(1)} %get-tuple-element.48), channel_id=1, source_target_pairs={{0,8},{8,0},{1,9},{9,1},{2,10},{10,2},{3,11},{11,3},{4,12},{12,4},... | collective-permute-start | bytes 208904 | tf_op jit(solution)/shard_map/ppermute | solution.py:323
  19.4 0.3 %collective-permute-done.6 = bf16[4,4096]{1,0:T(4,128)(2,1)S(1)} collective-permute-done((bf16[4,4096]{1,0:T(4,128)(2,1)S(1)}, bf16[4,4096]{1,0:T(4,128)(2,1)S(1)}, u32[]{:S(2)}, u32[]{:S(2)}) %collective-permute-start.6) | collective-permute-done | bytes 32800 | tf_op jit(solution)/shard_map/ppermute | solution.py:318
  19.8 2.8 %collective-permute-start.9 = (bf16[2,4096]{1,0:T(2,128)(2,1)S(1)}, bf16[2,4096]{1,0:T(2,128)(2,1)S(1)}, u32[]{:S(2)}, u32[]{:S(2)}) collective-permute-start(bf16[2,4096]{1,0:T(2,128)(2,1)S(1)} %slice.7), channel_id=1, source_target_pairs={{0,5},{1,4},{2,7},{3,6},{4,1},{5,0},{6,3},{7,2},{8,13},{9,12},{10,... | collective-permute-start | bytes 49160 | tf_op jit(solution)/shard_map/ppermute | solution.py:318
  22.6 0.0 collective-permute-done.8.far
  22.6 1.3 %shard_map.101 = (bf16[2048,128]{1,0:T(8,128)(2,1)}, bf16[128,2048]{1,0:T(8,128)(2,1)}) custom-call(bf16[8,4352]{1,0:T(8,128)(2,1)S(1)} %get-tuple-element.47.own, bf16[8,4352]{1,0:T(8,128)(2,1)S(1)} %collective-permute-done.8.far), custom_call_target="tpu_custom_call" | custom-call | bytes 2097152 | tf_op jit(solution)/shard_map/pallas_call | solution.py:325
  23.9 0.1 collective-permute-done.9.came
  24.0 0.7 %shard_map.102 = (bf16[1,4096]{1,0:T(2,128)(2,1)}, bf16[1,4096]{1,0:T(2,128)(2,1)}) custom-call(f32[4,4096]{1,0:T(4,128)S(1)} %convert_add_fusion.part, bf16[2,4096]{1,0:T(2,128)(2,1)S(1)} %collective-permute-done.9.came, f32[1,4096]{1,0:T(1,128)S(1)} %copy-done.2, bf16[2,4096]{1,0:T(2,128)(2,1)S(1)} %collective-permute-done.pair, ...), custom_call_target="tpu_custom_call" | custom-call | tf_op jit(solution)/shard_map/pallas_call | solution.py:343
  (9 shorter events, 0.1 us)
Async XLA Ops:
  0.6 5.7 %copy-start.3 = (bf16[1,1,1,4096]{3,2,1,0:T(2,128)(2,1)S(1)}, bf16[1,1,1,4096]{3,2,1,0:T(2,128)(2,1)}, u32[]{:S(2)}) copy-start(bf16[1,1,1,4096]{3,2,1,0:T(2,128)(2,1)} %param.8) | copy-start | bytes 24580
  1.4 4.9 %collective-permute-start = (bf16[2,4096]{1,0:T(2,128)(2,1)S(1)}, bf16[2,4096]{1,0:T(2,128)(2,1)S(1)}, u32[]{:S(2)}, u32[]{:S(2)}) collective-permute-start(bf16[2,4096]{1,0:T(2,128)(2,1)S(1)} %pad_maximum_fusion), channel_id=1, source_target_pairs={{0,16},{1,17},{2,18},{3,19},{4,20},{5,21},{6,22},{7,23},{8,24},{9,... | collective-permute-start | bytes 49160 | tf_op jit(solution)/shard_map/ppermute | solution.py:236
  4.4 8.3 %collective-permute-start.4 = (bf16[4096,128]{1,0:T(8,128)(2,1)}, bf16[4096,128]{1,0:T(8,128)(2,1)S(1)}, u32[]{:S(2)}, u32[]{:S(2)}) collective-permute-start(bf16[4096,128]{1,0:T(8,128)(2,1)} %bitcast.9), channel_id=1, source_target_pairs={{0,1},{1,0},{2,3},{3,2},{4,5},{5,4},{6,7},{7,6},{8,9},{9,8},{10,11... | collective-permute-start | bytes 3145736 | tf_op jit(solution)/shard_map/ppermute | solution.py:251
  4.4 8.3 %collective-permute-start.5 = (bf16[128,4096]{1,0:T(8,128)(2,1)}, bf16[128,4096]{1,0:T(8,128)(2,1)S(1)}, u32[]{:S(2)}, u32[]{:S(2)}) collective-permute-start(bf16[128,4096]{1,0:T(8,128)(2,1)} %bitcast.11), channel_id=1, source_target_pairs={{0,1},{1,0},{2,3},{3,2},{4,5},{5,4},{6,7},{7,6},{8,9},{9,8},{10,11... | collective-permute-start | bytes 3145736 | tf_op jit(solution)/shard_map/ppermute | solution.py:251
  4.9 1.2 %copy-start = (bf16[1,4096,128]{2,1,0:T(8,128)(2,1)S(1)}, bf16[1,4096,128]{2,1,0:T(8,128)(2,1)}, u32[]{:S(2)}) copy-start(bf16[1,4096,128]{2,1,0:T(8,128)(2,1)} %param.10) | copy-start | bytes 3145732
  6.3 4.6 %copy-start.1 = (bf16[1,128,4096]{2,1,0:T(8,128)(2,1)S(1)}, bf16[1,128,4096]{2,1,0:T(8,128)(2,1)}, u32[]{:S(2)}) copy-start(bf16[1,128,4096]{2,1,0:T(8,128)(2,1)} %param.11) | copy-start | bytes 3145732
  6.3 4.7 %collective-permute-start.2 = (bf16[3,4096]{1,0:T(4,128)(2,1)S(1)}, bf16[3,4096]{1,0:T(4,128)(2,1)S(1)}, u32[]{:S(2)}, u32[]{:S(2)}) collective-permute-start(bf16[3,4096]{1,0:T(4,128)(2,1)S(1)} %shard_map.94.held), channel_id=1, source_target_pairs={{0,5},{1,4},{2,7},{3,6},{4,1},{5,0},{6,3},{7,2},{8,13},{9,12},{10,... | collective-permute-start | bytes 73736 | tf_op jit(solution)/shard_map/ppermute | solution.py:266
  8.6 4.0 %collective-permute-start.1 = (bf16[3,4096]{1,0:T(4,128)(2,1)S(1)}, bf16[3,4096]{1,0:T(4,128)(2,1)S(1)}, u32[]{:S(2)}, u32[]{:S(2)}) collective-permute-start(bf16[3,4096]{1,0:T(4,128)(2,1)S(1)} %shard_map.94.held), channel_id=1, source_target_pairs={{0,3},{1,2},{2,1},{3,0},{4,7},{5,6},{6,5},{7,4},{8,11},{9,10},{10,... | collective-permute-start | bytes 73736 | tf_op jit(solution)/shard_map/ppermute | solution.py:266
  11.0 3.6 %collective-permute-start.3 = (bf16[3,4096]{1,0:T(4,128)(2,1)S(1)}, bf16[3,4096]{1,0:T(4,128)(2,1)S(1)}, u32[]{:S(2)}, u32[]{:S(2)}) collective-permute-start(bf16[3,4096]{1,0:T(4,128)(2,1)S(1)} %collective-permute-done.2.second), channel_id=1, source_target_pairs={{0,3},{1,2},{2,1},{3,0},{4,7},{5,6},{6,5},{7,4},{8,11},{9,10},{10,... | collective-permute-start | bytes 73736 | tf_op jit(solution)/shard_map/ppermute | solution.py:266
  12.7 1.9 %copy-start.2 = (f32[1,4096]{1,0:T(1,128)S(1)}, f32[1,4096]{1,0:T(1,128)}, u32[]{:S(2)}) copy-start(f32[1,4096]{1,0:T(1,128)} %gain.3) | copy-start | bytes 49156
  16.2 1.5 %collective-permute-start.7 = (bf16[4,8704]{1,0:T(4,128)(2,1)S(1)}, bf16[4,8704]{1,0:T(4,128)(2,1)S(1)}, u32[]{:S(2)}, u32[]{:S(2)}) collective-permute-start(bf16[4,8704]{1,0:T(4,128)(2,1)S(1)} %get-tuple-element.46.full), channel_id=1, source_target_pairs={{0,1},{1,0},{2,3},{3,2},{4,5},{5,4},{6,7},{7,6},{8,9},{9,8},{10,11... | collective-permute-start | bytes 208904 | tf_op jit(solution)/shard_map/ppermute | solution.py:307
  16.3 3.4 %collective-permute-start.6 = (bf16[4,4096]{1,0:T(4,128)(2,1)S(1)}, bf16[4,4096]{1,0:T(4,128)(2,1)S(1)}, u32[]{:S(2)}, u32[]{:S(2)}) collective-permute-start(bf16[4,4096]{1,0:T(4,128)(2,1)S(1)} %get-tuple-element.45), channel_id=1, source_target_pairs={{0,3},{1,2},{2,1},{3,0},{4,7},{5,6},{6,5},{7,4},{8,11},{9,10},{10,... | collective-permute-start | bytes 98312 | tf_op jit(solution)/shard_map/ppermute | solution.py:318
  17.8 4.8 %collective-permute-start.8 = (bf16[8,4352]{1,0:T(8,128)(2,1)S(1)}, bf16[8,4352]{1,0:T(8,128)(2,1)S(1)}, u32[]{:S(2)}, u32[]{:S(2)}) collective-permute-start(bf16[8,4352]{1,0:T(8,128)(2,1)S(1)} %get-tuple-element.48), channel_id=1, source_target_pairs={{0,8},{8,0},{1,9},{9,1},{2,10},{10,2},{3,11},{11,3},{4,12},{12,4},... | collective-permute-start | bytes 208904 | tf_op jit(solution)/shard_map/ppermute | solution.py:323
  19.8 4.3 %collective-permute-start.9 = (bf16[2,4096]{1,0:T(2,128)(2,1)S(1)}, bf16[2,4096]{1,0:T(2,128)(2,1)S(1)}, u32[]{:S(2)}, u32[]{:S(2)}) collective-permute-start(bf16[2,4096]{1,0:T(2,128)(2,1)S(1)} %slice.7), channel_id=1, source_target_pairs={{0,5},{1,4},{2,7},{3,6},{4,1},{5,0},{6,3},{7,2},{8,13},{9,12},{10,... | collective-permute-start | bytes 49160 | tf_op jit(solution)/shard_map/ppermute | solution.py:318

commit v8 on v7

--- a/solution.py
+++ b/solution.py
@@ -48,6 +48,12 @@
     return lax.dot_general(left, right, ((contract[:1], contract[1:]), ((), ())), preferred_element_type=jnp.float32)
 
 
+def spread(ref, scratch, count):
+    scratch[...] = ref[...].astype(jnp.float32)
+    many = ref.shape[0] // count
+    return jnp.concatenate([scratch[pl.ds(k, count, stride=many), :] for k in range(many)], axis=1)
+
+
 def of_array(ref, array):
     if len(ref.shape) == 3:
         return ref[array].astype(jnp.float32)
@@ -55,18 +61,15 @@
     return ref[array * rows : (array + 1) * rows].astype(jnp.float32)
 
 
-def block_kernel(rows, outer, second, fourth, gain, w_in, w_out_t, tall, send, keep, full, leaving):
+def block_kernel(rows, outer, fourth, gain, w_in, w_out_t, tall, send, keep, full, leaving, *scratch):
     count, width = keep.shape
     units = w_in.shape[1]
     f32, bf16 = jnp.float32, jnp.bfloat16
 
+    last = spread(fourth, scratch[0], 3 * rows) if scratch else fourth
+
     def joined(*arrays):
-        pieces = []
-        for array in arrays:
-            both = of_array(outer, array)
-            near = both.shape[0] // 2
-            pieces += [both[:near], of_array(second, array), both[near:], of_array(fourth, array)]
-        return jnp.concatenate(pieces, axis=0)
+        return jnp.concatenate([of_array(piece, array) for array in arrays for piece in (outer, last)], axis=0)
 
     cotan = joined(1).astype(bf16)
     d_acted = dot(cotan, w_out_t[...], (1, 0))
@@ -99,14 +102,31 @@
     rstd_out[...] = jnp.broadcast_to(rstd, rstd_out.shape)
 
 
-def stack_kernel(rows, pair, stash, held):
-    held[: 2 * rows] = pair[...]
-    held[2 * rows :] = stash[...]
+def stack_kernel(rows, pair, stash, held, *scratch):
+    if not scratch:
+        held[: 2 * rows] = pair[...]
+        held[2 * rows :] = stash[...]
+        return
+    step, many = held.shape[1], pair.shape[1] // held.shape[1]
+    values = jnp.concatenate([pair[...].astype(jnp.float32), stash[...].astype(jnp.float32)], axis=0)
+    for row in range(3 * rows):
+        for k in range(many):
+            scratch[0][many * row + k : many * row + k + 1] = values[row : row + 1, k * step : (k + 1) * step]
+    held[...] = scratch[0][...].astype(held.dtype)
 
 
 def merge_kernel(held, other, merged):
     for array in range(3):
         pieces = [of_array(ref, array) for ref in (held, other)]
+        merged[array] = jnp.concatenate(pieces, axis=0).astype(merged.dtype)
+
+
+def three_kernel(rows, held, second, third, merged, *scratch):
+    refs = held, second, third
+    if scratch:
+        refs = [spread(ref, scratch[0].at[i], 3 * rows) for i, ref in enumerate(refs)]
+    for array in range(3):
+        pieces = [of_array(ref, array) for ref in refs]
         merged[array] = jnp.concatenate(pieces, axis=0).astype(merged.dtype)
 
 
@@ -252,12 +272,16 @@
     w_first = loaded(w_in[0], 4)
     pair, w_first = lax.optimization_barrier((pair, w_first))
     w_second = loaded(w_out[0], 4)
+    packed = len(masks) == 2 and width % 1024 == 0
+    flat = (3 * rows * (width // 128), 128) if packed else (3 * rows, width)
+    pieces = [pltpu.VMEM(flat, jnp.float32)] if packed else []
     held = pl.pallas_call(
         functools.partial(stack_kernel, rows),
-        out_shape=jax.ShapeDtypeStruct((3 * rows, width), jnp.bfloat16),
+        out_shape=jax.ShapeDtypeStruct(flat, jnp.bfloat16),
         in_specs=[VMEM] * 2,
         out_specs=VMEM,
-        compiler_params=pltpu.CompilerParams(vmem_limit_bytes=max(4 << 20, 24 * rows * width)),
+        scratch_shapes=pieces,
+        compiler_params=pltpu.CompilerParams(vmem_limit_bytes=max(4 << 20, 64 * rows * width)),
         cost_estimate=pl.CostEstimate(flops=20 * 10**9, bytes_accessed=10**5, transcendentals=0),
     )(pair, stash[0, 0])
     slots = rows
@@ -283,13 +307,14 @@
     fourth, *weights = lax.optimization_barrier((fourth, *weights))
     slots *= 2
     outer = pl.pallas_call(
-        merge_kernel,
-        out_shape=jax.ShapeDtypeStruct((3, slots, width), jnp.bfloat16),
-        in_specs=[VMEM] * 2,
+        functools.partial(three_kernel, rows),
+        out_shape=jax.ShapeDtypeStruct((3, slots // 2 * 3, width), jnp.bfloat16),
+        in_specs=[VMEM] * 3,
         out_specs=VMEM,
-        compiler_params=pltpu.CompilerParams(vmem_limit_bytes=max(4 << 20, 48 * slots * width)),
+        scratch_shapes=[pltpu.VMEM((3,) + flat, jnp.float32)] if packed else [],
+        compiler_params=pltpu.CompilerParams(vmem_limit_bytes=max(4 << 20, 128 * slots * width)),
         cost_estimate=pl.CostEstimate(flops=10 * 10**9, bytes_accessed=10**5, transcendentals=0),
-    )(held, third)
+    )(held, second, third)
     half = 2 * slots
     limit = pltpu.CompilerParams(vmem_limit_bytes=max(8 << 20, 40 * half * width * 4))
     send, keep, full = pl.pallas_call(
@@ -299,11 +324,11 @@
             jax.ShapeDtypeStruct((half, width), jnp.float32),
             jax.ShapeDtypeStruct((half, 2 * width + 4 * units), jnp.bfloat16),
         ),
-        in_specs=[VMEM] * 7,
+        in_specs=[VMEM] * 6,
         out_specs=[VMEM] * 3,
-        scratch_shapes=[pltpu.VMEM((2 * half, 4 * units), jnp.float32)],
+        scratch_shapes=[pltpu.VMEM((2 * half, 4 * units), jnp.float32)] + pieces,
         compiler_params=limit,
-    )(outer, second, fourth, gain, *weights)
+    )(outer, fourth, gain, *weights)
     peer = lax.ppermute(full, "dp", xor_pairs(count, 1))
     low = jax.ShapeDtypeStruct((2 * half, width + 2 * units), jnp.bfloat16)
     own, away = pl.pallas_call(

time: 25 us -> 24.8 us (level)
  starting transfers between devices: 15.3 us -> 14.8 us
    ppermute x2, starting transfers between devices: 4.23 us -> 3.89 us  [on_device(): came = lax.ppermute(send, 'dp', xor_pairs(count, mask))]
  transfers between devices with their start and end apart: 10 -> 10, of which waited for: 3 -> 3; matrix products, arithmetic and copies ran while one was open for 0% -> 0% of each run, Pallas kernels for 14% -> 15%
where the time goes in v8:
time: 24.8 us; the launch traced here: 24.6 us
  starting transfers between devices  14.8 us (60%)
  Pallas kernels  5.89 us (24%)
  local copies, waits for them, and re-layouts  1.26 us (5%)
  waiting for transfers between devices  1.03 us (4%)
  other arithmetic  0.8 us (3%)
  between operations  0.77 us (3%)
    ppermute x3, starting transfers between devices, from_peer(): return lax.ppermute(value, 'dp', xor_pairs(count, mask))  5.71 us
    ppermute x2, starting transfers between devices, on_device(): came = lax.ppermute(send, 'dp', xor_pairs(count, mask))  3.89 us
    ppermute x1, starting transfers between devices, on_device(): pair = lax.ppermute(pair, AXES, onward)  3 us
    ppermute x1, starting transfers between devices, on_device(): far = lax.ppermute(away, 'mirror', xor_pairs(mirrors, 1))  1.58 us
    pallas_call x1, Pallas kernels, prepared(): pl.pallas_call(prepare_kernel, out_shape=(jax.ShapeDtypeStruct((width, 2...  1.55 us
    pallas_call x1, Pallas kernels, on_device(): pl.pallas_call(functools.partial(block_kernel, rows), out_shape=(jax.Shap...  1.55 us
    pallas_call x1, Pallas kernels, on_device(): pl.pallas_call(functools.partial(outer_kernel, 8), out_shape=(jax.ShapeDt...  1.31 us
    unnamed x8, local copies, waits for them, and re-layouts  1.24 us
  transfers between devices with their start and end apart: 10, of which 3 were waited for; matrix products, arithmetic and copies ran while one was open for 0% of the time, Pallas kernels for 15%

profile of v8, /device:TPU:0, one launch (start us, length us, event | category | flops | bytes accessed | tf_op | source)
XLA Modules:
  0.0 24.6 jit_solution(13709738762744941803)
XLA Ops:
  0.6 0.8 %pad_maximum_fusion = bf16[2,4096]{1,0:T(2,128)(2,1)S(1)} fusion(bf16[1,4096]{1,0:T(2,128)(2,1)} %bitcast.15, bf16[1,4096]{1,0:T(2,128)(2,1)} %bitcast.16), kind=kLoop, calls=%fused_computation.2 | loop fusion | flops 32768 | bytes 32768 | tf_op jit(solution)/shard_map/concatenate | solution.py:255
  1.4 3.0 %collective-permute-start = (bf16[2,4096]{1,0:T(2,128)(2,1)S(1)}, bf16[2,4096]{1,0:T(2,128)(2,1)S(1)}, u32[]{:S(2)}, u32[]{:S(2)}) collective-permute-start(bf16[2,4096]{1,0:T(2,128)(2,1)S(1)} %pad_maximum_fusion), channel_id=1, source_target_pairs={{0,16},{1,17},{2,18},{3,19},{4,20},{5,21},{6,22},{7,23},{8,24},{9,... | collective-permute-start | bytes 49160 | tf_op jit(solution)/shard_map/ppermute | solution.py:256
  4.4 0.0 collective-permute-start.4
  4.4 0.5 %collective-permute-start.5 = (bf16[128,4096]{1,0:T(8,128)(2,1)}, bf16[128,4096]{1,0:T(8,128)(2,1)S(1)}, u32[]{:S(2)}, u32[]{:S(2)}) collective-permute-start(bf16[128,4096]{1,0:T(8,128)(2,1)} %bitcast.11), channel_id=1, source_target_pairs={{0,1},{1,0},{2,3},{3,2},{4,5},{5,4},{6,7},{7,6},{8,9},{9,8},{10,11... | collective-permute-start | bytes 3145736 | tf_op jit(solution)/shard_map/ppermute | solution.py:271
  4.9 1.2 %copy-done = bf16[1,4096,128]{2,1,0:T(8,128)(2,1)S(1)} copy-done((bf16[1,4096,128]{2,1,0:T(8,128)(2,1)S(1)}, bf16[1,4096,128]{2,1,0:T(8,128)(2,1)}, u32[]{:S(2)}) %copy-start) | copy-done | bytes 1048600
  6.2 0.1 shard_map.93.in_own
  6.3 0.0 collective-permute-done.pair
  6.3 0.0 copy-start.1
  6.3 0.1 shard_map.94.held
  6.4 2.3 %collective-permute-start.1 = (bf16[96,128]{1,0:T(8,128)(2,1)S(1)}, bf16[96,128]{1,0:T(8,128)(2,1)S(1)}, u32[]{:S(2)}, u32[]{:S(2)}) collective-permute-start(bf16[96,128]{1,0:T(8,128)(2,1)S(1)} %shard_map.94.held), channel_id=1, source_target_pairs={{0,5},{1,4},{2,7},{3,6},{4,1},{5,0},{6,3},{7,2},{8,13},{9,12},{10,... | collective-permute-start | bytes 73736 | tf_op jit(solution)/shard_map/ppermute | solution.py:290
  8.6 2.0 %collective-permute-start.2 = (bf16[96,128]{1,0:T(8,128)(2,1)S(1)}, bf16[96,128]{1,0:T(8,128)(2,1)S(1)}, u32[]{:S(2)}, u32[]{:S(2)}) collective-permute-start(bf16[96,128]{1,0:T(8,128)(2,1)S(1)} %shard_map.94.held), channel_id=1, source_target_pairs={{0,3},{1,2},{2,1},{3,0},{4,7},{5,6},{6,5},{7,4},{8,11},{9,10},{10,... | collective-permute-start | bytes 73736 | tf_op jit(solution)/shard_map/ppermute | solution.py:290
  10.7 0.2 shard_map.96
  10.9 0.1 shard_map.95.out_own
  11.0 0.0 collective-permute-done.1.second
  11.1 1.4 %collective-permute-start.3 = (bf16[96,128]{1,0:T(8,128)(2,1)S(1)}, bf16[96,128]{1,0:T(8,128)(2,1)S(1)}, u32[]{:S(2)}, u32[]{:S(2)}) collective-permute-start(bf16[96,128]{1,0:T(8,128)(2,1)S(1)} %collective-permute-done.1.second), channel_id=1, source_target_pairs={{0,3},{1,2},{2,1},{3,0},{4,7},{5,6},{6,5},{7,4},{8,11},{9,10},{10,... | collective-permute-start | bytes 73736 | tf_op jit(solution)/shard_map/ppermute | solution.py:290
  12.5 0.0 collective-permute-done.2.third
  12.5 0.2 shard_map.97.outer
  12.6 0.0 copy-start.2
  12.7 0.0 collective-permute-done.4.in_peer
  12.7 0.0 collective-permute-done.5.out_peer
  12.7 1.6 %shard_map.98 = (bf16[4096,256]{1,0:T(8,128)(2,1)S(1)}, bf16[4096,256]{1,0:T(8,128)(2,1)S(1)}, bf16[512,4096]{1,0:T(8,128)(2,1)S(1)}) custom-call(bf16[4096,128]{1,0:T(8,128)(2,1)S(1)} %shard_map.93.in_own, bf16[4096,128]{1,0:T(8,128)(2,1)S(1)} %collective-permute-done.4.in_peer, bf16[128,4096]{1,0:T(8,128)(2,1)S(1)} %shard_map.95.out_own, ...), custom_call_target="tpu_custom_call" | custom-call | bytes 6291456 | tf_op jit(solution)/shard_map/pallas_call | solution.py:196
  14.2 0.3 %collective-permute-done.3.fourth = bf16[96,128]{1,0:T(8,128)(2,1)S(1)} collective-permute-done((bf16[96,128]{1,0:T(8,128)(2,1)S(1)}, bf16[96,128]{1,0:T(8,128)(2,1)S(1)}, u32[]{:S(2)}, u32[]{:S(2)}) %collective-permute-start.3) | collective-permute-done | bytes 24608 | tf_op jit(solution)/shard_map/ppermute | solution.py:290
  14.6 1.5 %shard_map.99 = (bf16[4,4096]{1,0:T(4,128)(2,1)S(1)}, f32[4,4096]{1,0:T(4,128)S(1)}, bf16[4,8704]{1,0:T(4,128)(2,1)S(1)}) custom-call(bf16[3,3,4096]{2,1,0:T(4,128)(2,1)S(1)} %shard_map.97.outer, bf16[96,128]{1,0:T(8,128)(2,1)S(1)} %collective-permute-done.3.fourth, f32[1,4096]{1,0:T(1,128)S(1)} %copy-done.2, bf16[4096,256]{1,0:T(8,128)(2,1)S(1)} %get-tuple-element.41.w_in, ...), custom_call_target="tpu_custom_call" | custom-call | tf_op jit(solution)/shard_map/pallas_call | solution.py:320
  16.1 0.1 collective-permute-start.7
  16.2 1.2 %collective-permute-start.6 = (bf16[4,4096]{1,0:T(4,128)(2,1)S(1)}, bf16[4,4096]{1,0:T(4,128)(2,1)S(1)}, u32[]{:S(2)}, u32[]{:S(2)}) collective-permute-start(bf16[4,4096]{1,0:T(4,128)(2,1)S(1)} %get-tuple-element.45), channel_id=1, source_target_pairs={{0,3},{1,2},{2,1},{3,0},{4,7},{5,6},{6,5},{7,4},{8,11},{9,10},{10,... | collective-permute-start | bytes 98312 | tf_op jit(solution)/shard_map/ppermute | solution.py:343
  17.5 1.6 %collective-permute-start.8 = (bf16[8,4352]{1,0:T(8,128)(2,1)S(1)}, bf16[8,4352]{1,0:T(8,128)(2,1)S(1)}, u32[]{:S(2)}, u32[]{:S(2)}) collective-permute-start(bf16[8,4352]{1,0:T(8,128)(2,1)S(1)} %get-tuple-element.48), channel_id=1, source_target_pairs={{0,8},{8,0},{1,9},{9,1},{2,10},{10,2},{3,11},{11,3},{4,12},{12,4},... | collective-permute-start | bytes 208904 | tf_op jit(solution)/shard_map/ppermute | solution.py:348
  19.1 0.5 %collective-permute-done.6 = bf16[4,4096]{1,0:T(4,128)(2,1)S(1)} collective-permute-done((bf16[4,4096]{1,0:T(4,128)(2,1)S(1)}, bf16[4,4096]{1,0:T(4,128)(2,1)S(1)}, u32[]{:S(2)}, u32[]{:S(2)}) %collective-permute-start.6) | collective-permute-done | bytes 32800 | tf_op jit(solution)/shard_map/ppermute | solution.py:343
  19.7 2.7 %collective-permute-start.9 = (bf16[2,4096]{1,0:T(2,128)(2,1)S(1)}, bf16[2,4096]{1,0:T(2,128)(2,1)S(1)}, u32[]{:S(2)}, u32[]{:S(2)}) collective-permute-start(bf16[2,4096]{1,0:T(2,128)(2,1)S(1)} %slice.7), channel_id=1, source_target_pairs={{0,5},{1,4},{2,7},{3,6},{4,1},{5,0},{6,3},{7,2},{8,13},{9,12},{10,... | collective-permute-start | bytes 49160 | tf_op jit(solution)/shard_map/ppermute | solution.py:343
  22.3 0.0 collective-permute-done.8.far
  22.3 1.3 %shard_map.101 = (bf16[2048,128]{1,0:T(8,128)(2,1)}, bf16[128,2048]{1,0:T(8,128)(2,1)}) custom-call(bf16[8,4352]{1,0:T(8,128)(2,1)S(1)} %get-tuple-element.47.own, bf16[8,4352]{1,0:T(8,128)(2,1)S(1)} %collective-permute-done.8.far), custom_call_target="tpu_custom_call" | custom-call | bytes 2097152 | tf_op jit(solution)/shard_map/pallas_call | solution.py:350
  23.7 0.2 collective-permute-done.9.came
  23.8 0.7 %shard_map.102 = (bf16[1,4096]{1,0:T(2,128)(2,1)}, bf16[1,4096]{1,0:T(2,128)(2,1)}) custom-call(f32[4,4096]{1,0:T(4,128)S(1)} %convert_add_fusion.part, bf16[2,4096]{1,0:T(2,128)(2,1)S(1)} %collective-permute-done.9.came, f32[1,4096]{1,0:T(1,128)S(1)} %copy-done.2, bf16[2,4096]{1,0:T(2,128)(2,1)S(1)} %collective-permute-done.pair, ...), custom_call_target="tpu_custom_call" | custom-call | tf_op jit(solution)/shard_map/pallas_call | solution.py:368
  (9 shorter events, 0.1 us)
Async XLA Ops:
  0.6 5.7 %copy-start.3 = (bf16[1,1,1,4096]{3,2,1,0:T(2,128)(2,1)S(1)}, bf16[1,1,1,4096]{3,2,1,0:T(2,128)(2,1)}, u32[]{:S(2)}) copy-start(bf16[1,1,1,4096]{3,2,1,0:T(2,128)(2,1)} %param.8) | copy-start | bytes 24580
  1.4 4.9 %collective-permute-start = (bf16[2,4096]{1,0:T(2,128)(2,1)S(1)}, bf16[2,4096]{1,0:T(2,128)(2,1)S(1)}, u32[]{:S(2)}, u32[]{:S(2)}) collective-permute-start(bf16[2,4096]{1,0:T(2,128)(2,1)S(1)} %pad_maximum_fusion), channel_id=1, source_target_pairs={{0,16},{1,17},{2,18},{3,19},{4,20},{5,21},{6,22},{7,23},{8,24},{9,... | collective-permute-start | bytes 49160 | tf_op jit(solution)/shard_map/ppermute | solution.py:256
  4.4 8.2 %collective-permute-start.4 = (bf16[4096,128]{1,0:T(8,128)(2,1)}, bf16[4096,128]{1,0:T(8,128)(2,1)S(1)}, u32[]{:S(2)}, u32[]{:S(2)}) collective-permute-start(bf16[4096,128]{1,0:T(8,128)(2,1)} %bitcast.9), channel_id=1, source_target_pairs={{0,1},{1,0},{2,3},{3,2},{4,5},{5,4},{6,7},{7,6},{8,9},{9,8},{10,11... | collective-permute-start | bytes 3145736 | tf_op jit(solution)/shard_map/ppermute | solution.py:271
  4.4 8.2 %collective-permute-start.5 = (bf16[128,4096]{1,0:T(8,128)(2,1)}, bf16[128,4096]{1,0:T(8,128)(2,1)S(1)}, u32[]{:S(2)}, u32[]{:S(2)}) collective-permute-start(bf16[128,4096]{1,0:T(8,128)(2,1)} %bitcast.11), channel_id=1, source_target_pairs={{0,1},{1,0},{2,3},{3,2},{4,5},{5,4},{6,7},{7,6},{8,9},{9,8},{10,11... | collective-permute-start | bytes 3145736 | tf_op jit(solution)/shard_map/ppermute | solution.py:271
  4.9 1.2 %copy-start = (bf16[1,4096,128]{2,1,0:T(8,128)(2,1)S(1)}, bf16[1,4096,128]{2,1,0:T(8,128)(2,1)}, u32[]{:S(2)}) copy-start(bf16[1,4096,128]{2,1,0:T(8,128)(2,1)} %param.10) | copy-start | bytes 3145732
  6.3 4.6 %copy-start.1 = (bf16[1,128,4096]{2,1,0:T(8,128)(2,1)S(1)}, bf16[1,128,4096]{2,1,0:T(8,128)(2,1)}, u32[]{:S(2)}) copy-start(bf16[1,128,4096]{2,1,0:T(8,128)(2,1)} %param.11) | copy-start | bytes 3145732
  6.4 4.7 %collective-permute-start.1 = (bf16[96,128]{1,0:T(8,128)(2,1)S(1)}, bf16[96,128]{1,0:T(8,128)(2,1)S(1)}, u32[]{:S(2)}, u32[]{:S(2)}) collective-permute-start(bf16[96,128]{1,0:T(8,128)(2,1)S(1)} %shard_map.94.held), channel_id=1, source_target_pairs={{0,5},{1,4},{2,7},{3,6},{4,1},{5,0},{6,3},{7,2},{8,13},{9,12},{10,... | collective-permute-start | bytes 73736 | tf_op jit(solution)/shard_map/ppermute | solution.py:290
  8.6 3.8 %collective-permute-start.2 = (bf16[96,128]{1,0:T(8,128)(2,1)S(1)}, bf16[96,128]{1,0:T(8,128)(2,1)S(1)}, u32[]{:S(2)}, u32[]{:S(2)}) collective-permute-start(bf16[96,128]{1,0:T(8,128)(2,1)S(1)} %shard_map.94.held), channel_id=1, source_target_pairs={{0,3},{1,2},{2,1},{3,0},{4,7},{5,6},{6,5},{7,4},{8,11},{9,10},{10,... | collective-permute-start | bytes 73736 | tf_op jit(solution)/shard_map/ppermute | solution.py:290
  11.1 3.5 %collective-permute-start.3 = (bf16[96,128]{1,0:T(8,128)(2,1)S(1)}, bf16[96,128]{1,0:T(8,128)(2,1)S(1)}, u32[]{:S(2)}, u32[]{:S(2)}) collective-permute-start(bf16[96,128]{1,0:T(8,128)(2,1)S(1)} %collective-permute-done.1.second), channel_id=1, source_target_pairs={{0,3},{1,2},{2,1},{3,0},{4,7},{5,6},{6,5},{7,4},{8,11},{9,10},{10,... | collective-permute-start | bytes 73736 | tf_op jit(solution)/shard_map/ppermute | solution.py:290
  12.6 1.9 %copy-start.2 = (f32[1,4096]{1,0:T(1,128)S(1)}, f32[1,4096]{1,0:T(1,128)}, u32[]{:S(2)}) copy-start(f32[1,4096]{1,0:T(1,128)} %gain.3) | copy-start | bytes 49156
  16.1 1.4 %collective-permute-start.7 = (bf16[4,8704]{1,0:T(4,128)(2,1)S(1)}, bf16[4,8704]{1,0:T(4,128)(2,1)S(1)}, u32[]{:S(2)}, u32[]{:S(2)}) collective-permute-start(bf16[4,8704]{1,0:T(4,128)(2,1)S(1)} %get-tuple-element.46.full), channel_id=1, source_target_pairs={{0,1},{1,0},{2,3},{3,2},{4,5},{5,4},{6,7},{7,6},{8,9},{9,8},{10,11... | collective-permute-start | bytes 208904 | tf_op jit(solution)/shard_map/ppermute | solution.py:332
  16.2 3.4 %collective-permute-start.6 = (bf16[4,4096]{1,0:T(4,128)(2,1)S(1)}, bf16[4,4096]{1,0:T(4,128)(2,1)S(1)}, u32[]{:S(2)}, u32[]{:S(2)}) collective-permute-start(bf16[4,4096]{1,0:T(4,128)(2,1)S(1)} %get-tuple-element.45), channel_id=1, source_target_pairs={{0,3},{1,2},{2,1},{3,0},{4,7},{5,6},{6,5},{7,4},{8,11},{9,10},{10,... | collective-permute-start | bytes 98312 | tf_op jit(solution)/shard_map/ppermute | solution.py:343
  17.5 4.8 %collective-permute-start.8 = (bf16[8,4352]{1,0:T(8,128)(2,1)S(1)}, bf16[8,4352]{1,0:T(8,128)(2,1)S(1)}, u32[]{:S(2)}, u32[]{:S(2)}) collective-permute-start(bf16[8,4352]{1,0:T(8,128)(2,1)S(1)} %get-tuple-element.48), channel_id=1, source_target_pairs={{0,8},{8,0},{1,9},{9,1},{2,10},{10,2},{3,11},{11,3},{4,12},{12,4},... | collective-permute-start | bytes 208904 | tf_op jit(solution)/shard_map/ppermute | solution.py:348
  19.7 4.1 %collective-permute-start.9 = (bf16[2,4096]{1,0:T(2,128)(2,1)S(1)}, bf16[2,4096]{1,0:T(2,128)(2,1)S(1)}, u32[]{:S(2)}, u32[]{:S(2)}) collective-permute-start(bf16[2,4096]{1,0:T(2,128)(2,1)S(1)} %slice.7), channel_id=1, source_target_pairs={{0,5},{1,4},{2,7},{3,6},{4,1},{5,0},{6,3},{7,2},{8,13},{9,12},{10,... | collective-permute-start | bytes 49160 | tf_op jit(solution)/shard_map/ppermute | solution.py:343

commit v9 on v8

--- a/solution.py
+++ b/solution.py
@@ -301,7 +301,7 @@
         )(held, other)
     second = from_peer(held, masks[-2])
     third = from_peer(held, masks[-1])
-    second, w_second, nhat, rstd = lax.optimization_barrier((second, w_second, nhat, rstd))
+    second, w_second = lax.optimization_barrier((second, w_second))
     fourth = from_peer(second, masks[-1])
     weights = prepared(w_first, peer_first, w_second, peer_second)
     fourth, *weights = lax.optimization_barrier((fourth, *weights))
@@ -343,6 +343,8 @@
         came = lax.ppermute(send, "dp", xor_pairs(count, mask))
         if step + 1 < len(scatter):
             part = keep + came.astype(jnp.float32)
+            if step == 0:
+                part, nhat, rstd = lax.optimization_barrier((part, nhat, rstd))
             half = part.shape[0] // 2
             send, keep = part[half:].astype(jnp.bfloat16), part[:half]
     far = lax.ppermute(away, "mirror", xor_pairs(mirrors, 1))

time: 24.8 us -> 24.8 us (level)
  waiting for transfers between devices: 1.03 us -> 0.24 us
  starting transfers between devices: 14.8 us -> 15.5 us
    ppermute x2, waiting for transfers between devices: 0.67 us -> 0.22 us  [on_device(): came = lax.ppermute(send, 'dp', xor_pairs(count, mask))]
    ppermute x3, waiting for transfers between devices: 0.34 us -> 0.01 us  [from_peer(): return lax.ppermute(value, 'dp', xor_pairs(count, mask))]
    ppermute x2, starting transfers between devices: 3.89 us -> 4.19 us  [on_device(): came = lax.ppermute(send, 'dp', xor_pairs(count, mask))]
  transfers between devices with their start and end apart: 10 -> 10, of which waited for: 3 -> 2; matrix products, arithmetic and copies ran while one was open for 0% -> 0% of each run, Pallas kernels for 15% -> 15%
where the time goes in v9:
time: 24.8 us; the launch traced here: 24.5 us
  starting transfers between devices  15.5 us (62%)
  Pallas kernels  5.9 us (24%)
  local copies, waits for them, and re-layouts  1.26 us (5%)
  other arithmetic  0.8 us (3%)
  between operations  0.78 us (3%)
    ppermute x3, starting transfers between devices, from_peer(): return lax.ppermute(value, 'dp', xor_pairs(count, mask))  5.95 us
    ppermute x2, starting transfers between devices, on_device(): came = lax.ppermute(send, 'dp', xor_pairs(count, mask))  4.19 us
    ppermute x1, starting transfers between devices, on_device(): pair = lax.ppermute(pair, AXES, onward)  3 us
    ppermute x1, starting transfers between devices, on_device(): far = lax.ppermute(away, 'mirror', xor_pairs(mirrors, 1))  1.58 us
    pallas_call x1, Pallas kernels, prepared(): pl.pallas_call(prepare_kernel, out_shape=(jax.ShapeDtypeStruct((width, 2...  1.55 us
    pallas_call x1, Pallas kernels, on_device(): pl.pallas_call(functools.partial(block_kernel, rows), out_shape=(jax.Shap...  1.55 us
    pallas_call x1, Pallas kernels, on_device(): pl.pallas_call(functools.partial(outer_kernel, 8), out_shape=(jax.ShapeDt...  1.31 us
    unnamed x8, local copies, waits for them, and re-layouts  1.24 us
  transfers between devices with their start and end apart: 10, of which 2 were waited for; matrix products, arithmetic and copies ran while one was open for 0% of the time, Pallas kernels for 15%

profile of v9, /device:TPU:0, one launch (start us, length us, event | category | flops | bytes accessed | tf_op | source)
XLA Modules:
  0.0 24.5 jit_solution(13283281541385183361)
XLA Ops:
  0.6 0.8 %pad_maximum_fusion = bf16[2,4096]{1,0:T(2,128)(2,1)S(1)} fusion(bf16[1,4096]{1,0:T(2,128)(2,1)} %bitcast.15, bf16[1,4096]{1,0:T(2,128)(2,1)} %bitcast.16), kind=kLoop, calls=%fused_computation.2 | loop fusion | flops 32768 | bytes 32768 | tf_op jit(solution)/shard_map/concatenate | solution.py:255
  1.4 3.0 %collective-permute-start = (bf16[2,4096]{1,0:T(2,128)(2,1)S(1)}, bf16[2,4096]{1,0:T(2,128)(2,1)S(1)}, u32[]{:S(2)}, u32[]{:S(2)}) collective-permute-start(bf16[2,4096]{1,0:T(2,128)(2,1)S(1)} %pad_maximum_fusion), channel_id=1, source_target_pairs={{0,16},{1,17},{2,18},{3,19},{4,20},{5,21},{6,22},{7,23},{8,24},{9,... | collective-permute-start | bytes 49160 | tf_op jit(solution)/shard_map/ppermute | solution.py:256
  4.4 0.0 collective-permute-start.4
  4.4 0.5 %collective-permute-start.5 = (bf16[128,4096]{1,0:T(8,128)(2,1)}, bf16[128,4096]{1,0:T(8,128)(2,1)S(1)}, u32[]{:S(2)}, u32[]{:S(2)}) collective-permute-start(bf16[128,4096]{1,0:T(8,128)(2,1)} %bitcast.11), channel_id=1, source_target_pairs={{0,1},{1,0},{2,3},{3,2},{4,5},{5,4},{6,7},{7,6},{8,9},{9,8},{10,11... | collective-permute-start | bytes 3145736 | tf_op jit(solution)/shard_map/ppermute | solution.py:271
  4.9 1.2 %copy-done = bf16[1,4096,128]{2,1,0:T(8,128)(2,1)S(1)} copy-done((bf16[1,4096,128]{2,1,0:T(8,128)(2,1)S(1)}, bf16[1,4096,128]{2,1,0:T(8,128)(2,1)}, u32[]{:S(2)}) %copy-start) | copy-done | bytes 1048600
  6.2 0.1 shard_map.93.in_own
  6.3 0.0 collective-permute-done.pair
  6.3 0.0 copy-start.1
  6.3 0.1 shard_map.94.held
  6.4 2.3 %collective-permute-start.1 = (bf16[96,128]{1,0:T(8,128)(2,1)S(1)}, bf16[96,128]{1,0:T(8,128)(2,1)S(1)}, u32[]{:S(2)}, u32[]{:S(2)}) collective-permute-start(bf16[96,128]{1,0:T(8,128)(2,1)S(1)} %shard_map.94.held), channel_id=1, source_target_pairs={{0,5},{1,4},{2,7},{3,6},{4,1},{5,0},{6,3},{7,2},{8,13},{9,12},{10,... | collective-permute-start | bytes 73736 | tf_op jit(solution)/shard_map/ppermute | solution.py:290
  8.6 2.0 %collective-permute-start.2 = (bf16[96,128]{1,0:T(8,128)(2,1)S(1)}, bf16[96,128]{1,0:T(8,128)(2,1)S(1)}, u32[]{:S(2)}, u32[]{:S(2)}) collective-permute-start(bf16[96,128]{1,0:T(8,128)(2,1)S(1)} %shard_map.94.held), channel_id=1, source_target_pairs={{0,3},{1,2},{2,1},{3,0},{4,7},{5,6},{6,5},{7,4},{8,11},{9,10},{10,... | collective-permute-start | bytes 73736 | tf_op jit(solution)/shard_map/ppermute | solution.py:290
  10.7 0.1 shard_map.95.out_own
  10.8 1.6 %collective-permute-start.3 = (bf16[96,128]{1,0:T(8,128)(2,1)S(1)}, bf16[96,128]{1,0:T(8,128)(2,1)S(1)}, u32[]{:S(2)}, u32[]{:S(2)}) collective-permute-start(bf16[96,128]{1,0:T(8,128)(2,1)S(1)} %collective-permute-done.1.second), channel_id=1, source_target_pairs={{0,3},{1,2},{2,1},{3,0},{4,7},{5,6},{6,5},{7,4},{8,11},{9,10},{10,... | collective-permute-start | bytes 73736 | tf_op jit(solution)/shard_map/ppermute | solution.py:290
  12.5 0.0 collective-permute-done.2.third
  12.5 0.2 shard_map.96.outer
  12.6 0.0 copy-start.2
  12.7 0.0 collective-permute-done.4.in_peer
  12.7 1.6 %shard_map.97 = (bf16[4096,256]{1,0:T(8,128)(2,1)S(1)}, bf16[4096,256]{1,0:T(8,128)(2,1)S(1)}, bf16[512,4096]{1,0:T(8,128)(2,1)S(1)}) custom-call(bf16[4096,128]{1,0:T(8,128)(2,1)S(1)} %shard_map.93.in_own, bf16[4096,128]{1,0:T(8,128)(2,1)S(1)} %collective-permute-done.4.in_peer, bf16[128,4096]{1,0:T(8,128)(2,1)S(1)} %shard_map.95.out_own, ...), custom_call_target="tpu_custom_call" | custom-call | bytes 6291456 | tf_op jit(solution)/shard_map/pallas_call | solution.py:196
  14.2 0.0 collective-permute-done.3.fourth
  14.3 1.5 %shard_map.98 = (bf16[4,4096]{1,0:T(4,128)(2,1)S(1)}, f32[4,4096]{1,0:T(4,128)S(1)}, bf16[4,8704]{1,0:T(4,128)(2,1)S(1)}) custom-call(bf16[3,3,4096]{2,1,0:T(4,128)(2,1)S(1)} %shard_map.96.outer, bf16[96,128]{1,0:T(8,128)(2,1)S(1)} %collective-permute-done.3.fourth, f32[1,4096]{1,0:T(1,128)S(1)} %copy-done.2, bf16[4096,256]{1,0:T(8,128)(2,1)S(1)} %get-tuple-element.40.w_in, ...), custom_call_target="tpu_custom_call" | custom-call | tf_op jit(solution)/shard_map/pallas_call | solution.py:320
  15.8 0.3 %collective-permute-start.7 = (bf16[4,8704]{1,0:T(4,128)(2,1)S(1)}, bf16[4,8704]{1,0:T(4,128)(2,1)S(1)}, u32[]{:S(2)}, u32[]{:S(2)}) collective-permute-start(bf16[4,8704]{1,0:T(4,128)(2,1)S(1)} %get-tuple-element.48.full), channel_id=1, source_target_pairs={{0,1},{1,0},{2,3},{3,2},{4,5},{5,4},{6,7},{7,6},{8,9},{9,8},{10,11... | collective-permute-start | bytes 208904 | tf_op jit(solution)/shard_map/ppermute | solution.py:332
  16.1 1.4 %collective-permute-start.6 = (bf16[4,4096]{1,0:T(4,128)(2,1)S(1)}, bf16[4,4096]{1,0:T(4,128)(2,1)S(1)}, u32[]{:S(2)}, u32[]{:S(2)}) collective-permute-start(bf16[4,4096]{1,0:T(4,128)(2,1)S(1)} %get-tuple-element.44), channel_id=1, source_target_pairs={{0,3},{1,2},{2,1},{3,0},{4,7},{5,6},{6,5},{7,4},{8,11},{9,10},{10,... | collective-permute-start | bytes 98312 | tf_op jit(solution)/shard_map/ppermute | solution.py:343
  17.5 0.2 shard_map.99
  17.7 0.0 collective-permute-done.7.peer
  17.7 0.1 shard_map.100
  17.8 1.6 %collective-permute-start.8 = (bf16[8,4352]{1,0:T(8,128)(2,1)S(1)}, bf16[8,4352]{1,0:T(8,128)(2,1)S(1)}, u32[]{:S(2)}, u32[]{:S(2)}) collective-permute-start(bf16[8,4352]{1,0:T(8,128)(2,1)S(1)} %get-tuple-element.50), channel_id=1, source_target_pairs={{0,8},{8,0},{1,9},{9,1},{2,10},{10,2},{3,11},{11,3},{4,12},{12,4},... | collective-permute-start | bytes 208904 | tf_op jit(solution)/shard_map/ppermute | solution.py:350
  19.4 0.1 collective-permute-done.6
  19.5 2.8 %collective-permute-start.9 = (bf16[2,4096]{1,0:T(2,128)(2,1)S(1)}, bf16[2,4096]{1,0:T(2,128)(2,1)S(1)}, u32[]{:S(2)}, u32[]{:S(2)}) collective-permute-start(bf16[2,4096]{1,0:T(2,128)(2,1)S(1)} %slice.7), channel_id=1, source_target_pairs={{0,5},{1,4},{2,7},{3,6},{4,1},{5,0},{6,3},{7,2},{8,13},{9,12},{10,... | collective-permute-start | bytes 49160 | tf_op jit(solution)/shard_map/ppermute | solution.py:343
  22.3 0.0 collective-permute-done.8.far
  22.3 1.3 %shard_map.101 = (bf16[2048,128]{1,0:T(8,128)(2,1)}, bf16[128,2048]{1,0:T(8,128)(2,1)}) custom-call(bf16[8,4352]{1,0:T(8,128)(2,1)S(1)} %get-tuple-element.49.own, bf16[8,4352]{1,0:T(8,128)(2,1)S(1)} %collective-permute-done.8.far), custom_call_target="tpu_custom_call" | custom-call | bytes 2097152 | tf_op jit(solution)/shard_map/pallas_call | solution.py:352
  23.6 0.1 collective-permute-done.9.came
  23.8 0.7 %shard_map.102 = (bf16[1,4096]{1,0:T(2,128)(2,1)}, bf16[1,4096]{1,0:T(2,128)(2,1)}) custom-call(f32[4,4096]{1,0:T(4,128)S(1)} %convert_add_fusion.part, bf16[2,4096]{1,0:T(2,128)(2,1)S(1)} %collective-permute-done.9.came, f32[1,4096]{1,0:T(1,128)S(1)} %copy-done.2, bf16[2,4096]{1,0:T(2,128)(2,1)S(1)} %collective-permute-done.pair, ...), custom_call_target="tpu_custom_call" | custom-call | tf_op jit(solution)/shard_map/pallas_call | solution.py:370
  (9 shorter events, 0.1 us)
Async XLA Ops:
  0.6 5.7 %copy-start.3 = (bf16[1,1,1,4096]{3,2,1,0:T(2,128)(2,1)S(1)}, bf16[1,1,1,4096]{3,2,1,0:T(2,128)(2,1)}, u32[]{:S(2)}) copy-start(bf16[1,1,1,4096]{3,2,1,0:T(2,128)(2,1)} %param.8) | copy-start | bytes 24580
  1.4 4.9 %collective-permute-start = (bf16[2,4096]{1,0:T(2,128)(2,1)S(1)}, bf16[2,4096]{1,0:T(2,128)(2,1)S(1)}, u32[]{:S(2)}, u32[]{:S(2)}) collective-permute-start(bf16[2,4096]{1,0:T(2,128)(2,1)S(1)} %pad_maximum_fusion), channel_id=1, source_target_pairs={{0,16},{1,17},{2,18},{3,19},{4,20},{5,21},{6,22},{7,23},{8,24},{9,... | collective-permute-start | bytes 49160 | tf_op jit(solution)/shard_map/ppermute | solution.py:256
  4.4 8.2 %collective-permute-start.4 = (bf16[4096,128]{1,0:T(8,128)(2,1)}, bf16[4096,128]{1,0:T(8,128)(2,1)S(1)}, u32[]{:S(2)}, u32[]{:S(2)}) collective-permute-start(bf16[4096,128]{1,0:T(8,128)(2,1)} %bitcast.9), channel_id=1, source_target_pairs={{0,1},{1,0},{2,3},{3,2},{4,5},{5,4},{6,7},{7,6},{8,9},{9,8},{10,11... | collective-permute-start | bytes 3145736 | tf_op jit(solution)/shard_map/ppermute | solution.py:271
  4.4 8.2 %collective-permute-start.5 = (bf16[128,4096]{1,0:T(8,128)(2,1)}, bf16[128,4096]{1,0:T(8,128)(2,1)S(1)}, u32[]{:S(2)}, u32[]{:S(2)}) collective-permute-start(bf16[128,4096]{1,0:T(8,128)(2,1)} %bitcast.11), channel_id=1, source_target_pairs={{0,1},{1,0},{2,3},{3,2},{4,5},{5,4},{6,7},{7,6},{8,9},{9,8},{10,11... | collective-permute-start | bytes 3145736 | tf_op jit(solution)/shard_map/ppermute | solution.py:271
  4.9 1.2 %copy-start = (bf16[1,4096,128]{2,1,0:T(8,128)(2,1)S(1)}, bf16[1,4096,128]{2,1,0:T(8,128)(2,1)}, u32[]{:S(2)}) copy-start(bf16[1,4096,128]{2,1,0:T(8,128)(2,1)} %param.10) | copy-start | bytes 3145732
  6.3 4.4 %copy-start.1 = (bf16[1,128,4096]{2,1,0:T(8,128)(2,1)S(1)}, bf16[1,128,4096]{2,1,0:T(8,128)(2,1)}, u32[]{:S(2)}) copy-start(bf16[1,128,4096]{2,1,0:T(8,128)(2,1)} %param.11) | copy-start | bytes 3145732
  6.4 4.4 %collective-permute-start.1 = (bf16[96,128]{1,0:T(8,128)(2,1)S(1)}, bf16[96,128]{1,0:T(8,128)(2,1)S(1)}, u32[]{:S(2)}, u32[]{:S(2)}) collective-permute-start(bf16[96,128]{1,0:T(8,128)(2,1)S(1)} %shard_map.94.held), channel_id=1, source_target_pairs={{0,5},{1,4},{2,7},{3,6},{4,1},{5,0},{6,3},{7,2},{8,13},{9,12},{10,... | collective-permute-start | bytes 73736 | tf_op jit(solution)/shard_map/ppermute | solution.py:290
  8.6 3.8 %collective-permute-start.2 = (bf16[96,128]{1,0:T(8,128)(2,1)S(1)}, bf16[96,128]{1,0:T(8,128)(2,1)S(1)}, u32[]{:S(2)}, u32[]{:S(2)}) collective-permute-start(bf16[96,128]{1,0:T(8,128)(2,1)S(1)} %shard_map.94.held), channel_id=1, source_target_pairs={{0,3},{1,2},{2,1},{3,0},{4,7},{5,6},{6,5},{7,4},{8,11},{9,10},{10,... | collective-permute-start | bytes 73736 | tf_op jit(solution)/shard_map/ppermute | solution.py:290
  10.8 3.4 %collective-permute-start.3 = (bf16[96,128]{1,0:T(8,128)(2,1)S(1)}, bf16[96,128]{1,0:T(8,128)(2,1)S(1)}, u32[]{:S(2)}, u32[]{:S(2)}) collective-permute-start(bf16[96,128]{1,0:T(8,128)(2,1)S(1)} %collective-permute-done.1.second), channel_id=1, source_target_pairs={{0,3},{1,2},{2,1},{3,0},{4,7},{5,6},{6,5},{7,4},{8,11},{9,10},{10,... | collective-permute-start | bytes 73736 | tf_op jit(solution)/shard_map/ppermute | solution.py:290
  12.6 1.6 %copy-start.2 = (f32[1,4096]{1,0:T(1,128)S(1)}, f32[1,4096]{1,0:T(1,128)}, u32[]{:S(2)}) copy-start(f32[1,4096]{1,0:T(1,128)} %gain.3) | copy-start | bytes 49156
  15.8 1.9 %collective-permute-start.7 = (bf16[4,8704]{1,0:T(4,128)(2,1)S(1)}, bf16[4,8704]{1,0:T(4,128)(2,1)S(1)}, u32[]{:S(2)}, u32[]{:S(2)}) collective-permute-start(bf16[4,8704]{1,0:T(4,128)(2,1)S(1)} %get-tuple-element.48.full), channel_id=1, source_target_pairs={{0,1},{1,0},{2,3},{3,2},{4,5},{5,4},{6,7},{7,6},{8,9},{9,8},{10,11... | collective-permute-start | bytes 208904 | tf_op jit(solution)/shard_map/ppermute | solution.py:332
  16.1 3.3 %collective-permute-start.6 = (bf16[4,4096]{1,0:T(4,128)(2,1)S(1)}, bf16[4,4096]{1,0:T(4,128)(2,1)S(1)}, u32[]{:S(2)}, u32[]{:S(2)}) collective-permute-start(bf16[4,4096]{1,0:T(4,128)(2,1)S(1)} %get-tuple-element.44), channel_id=1, source_target_pairs={{0,3},{1,2},{2,1},{3,0},{4,7},{5,6},{6,5},{7,4},{8,11},{9,10},{10,... | collective-permute-start | bytes 98312 | tf_op jit(solution)/shard_map/ppermute | solution.py:343
  17.8 4.6 %collective-permute-start.8 = (bf16[8,4352]{1,0:T(8,128)(2,1)S(1)}, bf16[8,4352]{1,0:T(8,128)(2,1)S(1)}, u32[]{:S(2)}, u32[]{:S(2)}) collective-permute-start(bf16[8,4352]{1,0:T(8,128)(2,1)S(1)} %get-tuple-element.50), channel_id=1, source_target_pairs={{0,8},{8,0},{1,9},{9,1},{2,10},{10,2},{3,11},{11,3},{4,12},{12,4},... | collective-permute-start | bytes 208904 | tf_op jit(solution)/shard_map/ppermute | solution.py:350
  19.5 4.3 %collective-permute-start.9 = (bf16[2,4096]{1,0:T(2,128)(2,1)S(1)}, bf16[2,4096]{1,0:T(2,128)(2,1)S(1)}, u32[]{:S(2)}, u32[]{:S(2)}) collective-permute-start(bf16[2,4096]{1,0:T(2,128)(2,1)S(1)} %slice.7), channel_id=1, source_target_pairs={{0,5},{1,4},{2,7},{3,6},{4,1},{5,0},{6,3},{7,2},{8,13},{9,12},{10,... | collective-permute-start | bytes 49160 | tf_op jit(solution)/shard_map/ppermute | solution.py:343

commit v10 on v8

--- a/solution.py
+++ b/solution.py
@@ -301,7 +301,7 @@
         )(held, other)
     second = from_peer(held, masks[-2])
     third = from_peer(held, masks[-1])
-    second, w_second, nhat, rstd = lax.optimization_barrier((second, w_second, nhat, rstd))
+    second, nhat, rstd = lax.optimization_barrier((second, nhat, rstd))
     fourth = from_peer(second, masks[-1])
     weights = prepared(w_first, peer_first, w_second, peer_second)
     fourth, *weights = lax.optimization_barrier((fourth, *weights))

time: 24.8 us -> 24.8 us (level)
  no operation moved by 1% of the time
where the time goes in v10:
time: 24.8 us; the launch traced here: 24.6 us
  starting transfers between devices  14.8 us (60%)
  Pallas kernels  5.89 us (24%)
  local copies, waits for them, and re-layouts  1.26 us (5%)
  waiting for transfers between devices  1.03 us (4%)
  other arithmetic  0.8 us (3%)
  between operations  0.77 us (3%)
    ppermute x3, starting transfers between devices, from_peer(): return lax.ppermute(value, 'dp', xor_pairs(count, mask))  5.71 us
    ppermute x2, starting transfers between devices, on_device(): came = lax.ppermute(send, 'dp', xor_pairs(count, mask))  3.89 us
    ppermute x1, starting transfers between devices, on_device(): pair = lax.ppermute(pair, AXES, onward)  3 us
    ppermute x1, starting transfers between devices, on_device(): far = lax.ppermute(away, 'mirror', xor_pairs(mirrors, 1))  1.58 us
    pallas_call x1, Pallas kernels, prepared(): pl.pallas_call(prepare_kernel, out_shape=(jax.ShapeDtypeStruct((width, 2...  1.55 us
    pallas_call x1, Pallas kernels, on_device(): pl.pallas_call(functools.partial(block_kernel, rows), out_shape=(jax.Shap...  1.55 us
    pallas_call x1, Pallas kernels, on_device(): pl.pallas_call(functools.partial(outer_kernel, 8), out_shape=(jax.ShapeDt...  1.31 us
    unnamed x8, local copies, waits for them, and re-layouts  1.24 us
  transfers between devices with their start and end apart: 10, of which 3 were waited for; matrix products, arithmetic and copies ran while one was open for 0% of the time, Pallas kernels for 15%

profile of v10, /device:TPU:0, one launch (start us, length us, event | category | flops | bytes accessed | tf_op | source)
XLA Modules:
  0.0 24.6 jit_solution(13709738762744941803)
XLA Ops:
  0.6 0.8 %pad_maximum_fusion = bf16[2,4096]{1,0:T(2,128)(2,1)S(1)} fusion(bf16[1,4096]{1,0:T(2,128)(2,1)} %bitcast.15, bf16[1,4096]{1,0:T(2,128)(2,1)} %bitcast.16), kind=kLoop, calls=%fused_computation.2 | loop fusion | flops 32768 | bytes 32768 | tf_op jit(solution)/shard_map/concatenate | solution.py:255
  1.4 3.0 %collective-permute-start = (bf16[2,4096]{1,0:T(2,128)(2,1)S(1)}, bf16[2,4096]{1,0:T(2,128)(2,1)S(1)}, u32[]{:S(2)}, u32[]{:S(2)}) collective-permute-start(bf16[2,4096]{1,0:T(2,128)(2,1)S(1)} %pad_maximum_fusion), channel_id=1, source_target_pairs={{0,16},{1,17},{2,18},{3,19},{4,20},{5,21},{6,22},{7,23},{8,24},{9,... | collective-permute-start | bytes 49160 | tf_op jit(solution)/shard_map/ppermute | solution.py:256
  4.4 0.0 collective-permute-start.4
  4.4 0.5 %collective-permute-start.5 = (bf16[128,4096]{1,0:T(8,128)(2,1)}, bf16[128,4096]{1,0:T(8,128)(2,1)S(1)}, u32[]{:S(2)}, u32[]{:S(2)}) collective-permute-start(bf16[128,4096]{1,0:T(8,128)(2,1)} %bitcast.11), channel_id=1, source_target_pairs={{0,1},{1,0},{2,3},{3,2},{4,5},{5,4},{6,7},{7,6},{8,9},{9,8},{10,11... | collective-permute-start | bytes 3145736 | tf_op jit(solution)/shard_map/ppermute | solution.py:271
  4.9 1.2 %copy-done = bf16[1,4096,128]{2,1,0:T(8,128)(2,1)S(1)} copy-done((bf16[1,4096,128]{2,1,0:T(8,128)(2,1)S(1)}, bf16[1,4096,128]{2,1,0:T(8,128)(2,1)}, u32[]{:S(2)}) %copy-start) | copy-done | bytes 1048600
  6.2 0.1 shard_map.93.in_own
  6.3 0.0 collective-permute-done.pair
  6.3 0.0 copy-start.1
  6.3 0.1 shard_map.94.held
  6.4 2.3 %collective-permute-start.1 = (bf16[96,128]{1,0:T(8,128)(2,1)S(1)}, bf16[96,128]{1,0:T(8,128)(2,1)S(1)}, u32[]{:S(2)}, u32[]{:S(2)}) collective-permute-start(bf16[96,128]{1,0:T(8,128)(2,1)S(1)} %shard_map.94.held), channel_id=1, source_target_pairs={{0,5},{1,4},{2,7},{3,6},{4,1},{5,0},{6,3},{7,2},{8,13},{9,12},{10,... | collective-permute-start | bytes 73736 | tf_op jit(solution)/shard_map/ppermute | solution.py:290
  8.6 2.0 %collective-permute-start.2 = (bf16[96,128]{1,0:T(8,128)(2,1)S(1)}, bf16[96,128]{1,0:T(8,128)(2,1)S(1)}, u32[]{:S(2)}, u32[]{:S(2)}) collective-permute-start(bf16[96,128]{1,0:T(8,128)(2,1)S(1)} %shard_map.94.held), channel_id=1, source_target_pairs={{0,3},{1,2},{2,1},{3,0},{4,7},{5,6},{6,5},{7,4},{8,11},{9,10},{10,... | collective-permute-start | bytes 73736 | tf_op jit(solution)/shard_map/ppermute | solution.py:290
  10.7 0.2 shard_map.95
  10.9 0.1 shard_map.97.out_own
  11.0 0.0 collective-permute-done.1.second
  11.1 1.4 %collective-permute-start.3 = (bf16[96,128]{1,0:T(8,128)(2,1)S(1)}, bf16[96,128]{1,0:T(8,128)(2,1)S(1)}, u32[]{:S(2)}, u32[]{:S(2)}) collective-permute-start(bf16[96,128]{1,0:T(8,128)(2,1)S(1)} %collective-permute-done.1.second), channel_id=1, source_target_pairs={{0,3},{1,2},{2,1},{3,0},{4,7},{5,6},{6,5},{7,4},{8,11},{9,10},{10,... | collective-permute-start | bytes 73736 | tf_op jit(solution)/shard_map/ppermute | solution.py:290
  12.5 0.0 collective-permute-done.2.third
  12.5 0.2 shard_map.96.outer
  12.6 0.0 copy-start.2
  12.7 0.0 collective-permute-done.4.in_peer
  12.7 0.0 collective-permute-done.5.out_peer
  12.7 1.6 %shard_map.98 = (bf16[4096,256]{1,0:T(8,128)(2,1)S(1)}, bf16[4096,256]{1,0:T(8,128)(2,1)S(1)}, bf16[512,4096]{1,0:T(8,128)(2,1)S(1)}) custom-call(bf16[4096,128]{1,0:T(8,128)(2,1)S(1)} %shard_map.93.in_own, bf16[4096,128]{1,0:T(8,128)(2,1)S(1)} %collective-permute-done.4.in_peer, bf16[128,4096]{1,0:T(8,128)(2,1)S(1)} %shard_map.97.out_own, ...), custom_call_target="tpu_custom_call" | custom-call | bytes 6291456 | tf_op jit(solution)/shard_map/pallas_call | solution.py:196
  14.2 0.3 %collective-permute-done.3.fourth = bf16[96,128]{1,0:T(8,128)(2,1)S(1)} collective-permute-done((bf16[96,128]{1,0:T(8,128)(2,1)S(1)}, bf16[96,128]{1,0:T(8,128)(2,1)S(1)}, u32[]{:S(2)}, u32[]{:S(2)}) %collective-permute-start.3) | collective-permute-done | bytes 24608 | tf_op jit(solution)/shard_map/ppermute | solution.py:290
  14.6 1.5 %shard_map.99 = (bf16[4,4096]{1,0:T(4,128)(2,1)S(1)}, f32[4,4096]{1,0:T(4,128)S(1)}, bf16[4,8704]{1,0:T(4,128)(2,1)S(1)}) custom-call(bf16[3,3,4096]{2,1,0:T(4,128)(2,1)S(1)} %shard_map.96.outer, bf16[96,128]{1,0:T(8,128)(2,1)S(1)} %collective-permute-done.3.fourth, f32[1,4096]{1,0:T(1,128)S(1)} %copy-done.2, bf16[4096,256]{1,0:T(8,128)(2,1)S(1)} %get-tuple-element.39.w_in, ...), custom_call_target="tpu_custom_call" | custom-call | tf_op jit(solution)/shard_map/pallas_call | solution.py:320
  16.1 0.1 collective-permute-start.7
  16.2 1.2 %collective-permute-start.6 = (bf16[4,4096]{1,0:T(4,128)(2,1)S(1)}, bf16[4,4096]{1,0:T(4,128)(2,1)S(1)}, u32[]{:S(2)}, u32[]{:S(2)}) collective-permute-start(bf16[4,4096]{1,0:T(4,128)(2,1)S(1)} %get-tuple-element.43), channel_id=1, source_target_pairs={{0,3},{1,2},{2,1},{3,0},{4,7},{5,6},{6,5},{7,4},{8,11},{9,10},{10,... | collective-permute-start | bytes 98312 | tf_op jit(solution)/shard_map/ppermute | solution.py:343
  17.5 1.6 %collective-permute-start.8 = (bf16[8,4352]{1,0:T(8,128)(2,1)S(1)}, bf16[8,4352]{1,0:T(8,128)(2,1)S(1)}, u32[]{:S(2)}, u32[]{:S(2)}) collective-permute-start(bf16[8,4352]{1,0:T(8,128)(2,1)S(1)} %get-tuple-element.46), channel_id=1, source_target_pairs={{0,8},{8,0},{1,9},{9,1},{2,10},{10,2},{3,11},{11,3},{4,12},{12,4},... | collective-permute-start | bytes 208904 | tf_op jit(solution)/shard_map/ppermute | solution.py:348
  19.1 0.5 %collective-permute-done.6 = bf16[4,4096]{1,0:T(4,128)(2,1)S(1)} collective-permute-done((bf16[4,4096]{1,0:T(4,128)(2,1)S(1)}, bf16[4,4096]{1,0:T(4,128)(2,1)S(1)}, u32[]{:S(2)}, u32[]{:S(2)}) %collective-permute-start.6) | collective-permute-done | bytes 32800 | tf_op jit(solution)/shard_map/ppermute | solution.py:343
  19.7 2.7 %collective-permute-start.9 = (bf16[2,4096]{1,0:T(2,128)(2,1)S(1)}, bf16[2,4096]{1,0:T(2,128)(2,1)S(1)}, u32[]{:S(2)}, u32[]{:S(2)}) collective-permute-start(bf16[2,4096]{1,0:T(2,128)(2,1)S(1)} %slice.7), channel_id=1, source_target_pairs={{0,5},{1,4},{2,7},{3,6},{4,1},{5,0},{6,3},{7,2},{8,13},{9,12},{10,... | collective-permute-start | bytes 49160 | tf_op jit(solution)/shard_map/ppermute | solution.py:343
  22.3 0.0 collective-permute-done.8.far
  22.3 1.3 %shard_map.101 = (bf16[2048,128]{1,0:T(8,128)(2,1)}, bf16[128,2048]{1,0:T(8,128)(2,1)}) custom-call(bf16[8,4352]{1,0:T(8,128)(2,1)S(1)} %get-tuple-element.45.own, bf16[8,4352]{1,0:T(8,128)(2,1)S(1)} %collective-permute-done.8.far), custom_call_target="tpu_custom_call" | custom-call | bytes 2097152 | tf_op jit(solution)/shard_map/pallas_call | solution.py:350
  23.7 0.2 collective-permute-done.9.came
  23.8 0.7 %shard_map.102 = (bf16[1,4096]{1,0:T(2,128)(2,1)}, bf16[1,4096]{1,0:T(2,128)(2,1)}) custom-call(f32[4,4096]{1,0:T(4,128)S(1)} %convert_add_fusion.part, bf16[2,4096]{1,0:T(2,128)(2,1)S(1)} %collective-permute-done.9.came, f32[1,4096]{1,0:T(1,128)S(1)} %copy-done.2, bf16[2,4096]{1,0:T(2,128)(2,1)S(1)} %collective-permute-done.pair, ...), custom_call_target="tpu_custom_call" | custom-call | tf_op jit(solution)/shard_map/pallas_call | solution.py:368
  (9 shorter events, 0.1 us)
Async XLA Ops:
  0.6 5.7 %copy-start.3 = (bf16[1,1,1,4096]{3,2,1,0:T(2,128)(2,1)S(1)}, bf16[1,1,1,4096]{3,2,1,0:T(2,128)(2,1)}, u32[]{:S(2)}) copy-start(bf16[1,1,1,4096]{3,2,1,0:T(2,128)(2,1)} %param.8) | copy-start | bytes 24580
  1.4 4.9 %collective-permute-start = (bf16[2,4096]{1,0:T(2,128)(2,1)S(1)}, bf16[2,4096]{1,0:T(2,128)(2,1)S(1)}, u32[]{:S(2)}, u32[]{:S(2)}) collective-permute-start(bf16[2,4096]{1,0:T(2,128)(2,1)S(1)} %pad_maximum_fusion), channel_id=1, source_target_pairs={{0,16},{1,17},{2,18},{3,19},{4,20},{5,21},{6,22},{7,23},{8,24},{9,... | collective-permute-start | bytes 49160 | tf_op jit(solution)/shard_map/ppermute | solution.py:256
  4.4 8.2 %collective-permute-start.4 = (bf16[4096,128]{1,0:T(8,128)(2,1)}, bf16[4096,128]{1,0:T(8,128)(2,1)S(1)}, u32[]{:S(2)}, u32[]{:S(2)}) collective-permute-start(bf16[4096,128]{1,0:T(8,128)(2,1)} %bitcast.9), channel_id=1, source_target_pairs={{0,1},{1,0},{2,3},{3,2},{4,5},{5,4},{6,7},{7,6},{8,9},{9,8},{10,11... | collective-permute-start | bytes 3145736 | tf_op jit(solution)/shard_map/ppermute | solution.py:271
  4.4 8.2 %collective-permute-start.5 = (bf16[128,4096]{1,0:T(8,128)(2,1)}, bf16[128,4096]{1,0:T(8,128)(2,1)S(1)}, u32[]{:S(2)}, u32[]{:S(2)}) collective-permute-start(bf16[128,4096]{1,0:T(8,128)(2,1)} %bitcast.11), channel_id=1, source_target_pairs={{0,1},{1,0},{2,3},{3,2},{4,5},{5,4},{6,7},{7,6},{8,9},{9,8},{10,11... | collective-permute-start | bytes 3145736 | tf_op jit(solution)/shard_map/ppermute | solution.py:271
  4.9 1.2 %copy-start = (bf16[1,4096,128]{2,1,0:T(8,128)(2,1)S(1)}, bf16[1,4096,128]{2,1,0:T(8,128)(2,1)}, u32[]{:S(2)}) copy-start(bf16[1,4096,128]{2,1,0:T(8,128)(2,1)} %param.10) | copy-start | bytes 3145732
  6.3 4.6 %copy-start.1 = (bf16[1,128,4096]{2,1,0:T(8,128)(2,1)S(1)}, bf16[1,128,4096]{2,1,0:T(8,128)(2,1)}, u32[]{:S(2)}) copy-start(bf16[1,128,4096]{2,1,0:T(8,128)(2,1)} %param.11) | copy-start | bytes 3145732
  6.4 4.7 %collective-permute-start.1 = (bf16[96,128]{1,0:T(8,128)(2,1)S(1)}, bf16[96,128]{1,0:T(8,128)(2,1)S(1)}, u32[]{:S(2)}, u32[]{:S(2)}) collective-permute-start(bf16[96,128]{1,0:T(8,128)(2,1)S(1)} %shard_map.94.held), channel_id=1, source_target_pairs={{0,5},{1,4},{2,7},{3,6},{4,1},{5,0},{6,3},{7,2},{8,13},{9,12},{10,... | collective-permute-start | bytes 73736 | tf_op jit(solution)/shard_map/ppermute | solution.py:290
  8.6 3.8 %collective-permute-start.2 = (bf16[96,128]{1,0:T(8,128)(2,1)S(1)}, bf16[96,128]{1,0:T(8,128)(2,1)S(1)}, u32[]{:S(2)}, u32[]{:S(2)}) collective-permute-start(bf16[96,128]{1,0:T(8,128)(2,1)S(1)} %shard_map.94.held), channel_id=1, source_target_pairs={{0,3},{1,2},{2,1},{3,0},{4,7},{5,6},{6,5},{7,4},{8,11},{9,10},{10,... | collective-permute-start | bytes 73736 | tf_op jit(solution)/shard_map/ppermute | solution.py:290
  11.1 3.5 %collective-permute-start.3 = (bf16[96,128]{1,0:T(8,128)(2,1)S(1)}, bf16[96,128]{1,0:T(8,128)(2,1)S(1)}, u32[]{:S(2)}, u32[]{:S(2)}) collective-permute-start(bf16[96,128]{1,0:T(8,128)(2,1)S(1)} %collective-permute-done.1.second), channel_id=1, source_target_pairs={{0,3},{1,2},{2,1},{3,0},{4,7},{5,6},{6,5},{7,4},{8,11},{9,10},{10,... | collective-permute-start | bytes 73736 | tf_op jit(solution)/shard_map/ppermute | solution.py:290
  12.6 1.9 %copy-start.2 = (f32[1,4096]{1,0:T(1,128)S(1)}, f32[1,4096]{1,0:T(1,128)}, u32[]{:S(2)}) copy-start(f32[1,4096]{1,0:T(1,128)} %gain.3) | copy-start | bytes 49156
  16.1 1.4 %collective-permute-start.7 = (bf16[4,8704]{1,0:T(4,128)(2,1)S(1)}, bf16[4,8704]{1,0:T(4,128)(2,1)S(1)}, u32[]{:S(2)}, u32[]{:S(2)}) collective-permute-start(bf16[4,8704]{1,0:T(4,128)(2,1)S(1)} %get-tuple-element.44.full), channel_id=1, source_target_pairs={{0,1},{1,0},{2,3},{3,2},{4,5},{5,4},{6,7},{7,6},{8,9},{9,8},{10,11... | collective-permute-start | bytes 208904 | tf_op jit(solution)/shard_map/ppermute | solution.py:332
  16.2 3.4 %collective-permute-start.6 = (bf16[4,4096]{1,0:T(4,128)(2,1)S(1)}, bf16[4,4096]{1,0:T(4,128)(2,1)S(1)}, u32[]{:S(2)}, u32[]{:S(2)}) collective-permute-start(bf16[4,4096]{1,0:T(4,128)(2,1)S(1)} %get-tuple-element.43), channel_id=1, source_target_pairs={{0,3},{1,2},{2,1},{3,0},{4,7},{5,6},{6,5},{7,4},{8,11},{9,10},{10,... | collective-permute-start | bytes 98312 | tf_op jit(solution)/shard_map/ppermute | solution.py:343
  17.5 4.8 %collective-permute-start.8 = (bf16[8,4352]{1,0:T(8,128)(2,1)S(1)}, bf16[8,4352]{1,0:T(8,128)(2,1)S(1)}, u32[]{:S(2)}, u32[]{:S(2)}) collective-permute-start(bf16[8,4352]{1,0:T(8,128)(2,1)S(1)} %get-tuple-element.46), channel_id=1, source_target_pairs={{0,8},{8,0},{1,9},{9,1},{2,10},{10,2},{3,11},{11,3},{4,12},{12,4},... | collective-permute-start | bytes 208904 | tf_op jit(solution)/shard_map/ppermute | solution.py:348
  19.7 4.1 %collective-permute-start.9 = (bf16[2,4096]{1,0:T(2,128)(2,1)S(1)}, bf16[2,4096]{1,0:T(2,128)(2,1)S(1)}, u32[]{:S(2)}, u32[]{:S(2)}) collective-permute-start(bf16[2,4096]{1,0:T(2,128)(2,1)S(1)} %slice.7), channel_id=1, source_target_pairs={{0,5},{1,4},{2,7},{3,6},{4,1},{5,0},{6,3},{7,2},{8,13},{9,12},{10,... | collective-permute-start | bytes 49160 | tf_op jit(solution)/shard_map/ppermute | solution.py:343

commit v11 on v9

--- a/solution.py
+++ b/solution.py
@@ -301,7 +301,6 @@
         )(held, other)
     second = from_peer(held, masks[-2])
     third = from_peer(held, masks[-1])
-    second, w_second = lax.optimization_barrier((second, w_second))
     fourth = from_peer(second, masks[-1])
     weights = prepared(w_first, peer_first, w_second, peer_second)
     fourth, *weights = lax.optimization_barrier((fourth, *weights))

time: 24.8 us -> 24.8 us (level)
  no operation moved by 1% of the time
where the time goes in v11:
time: 24.8 us; the launch traced here: 24.5 us
  starting transfers between devices  15.5 us (62%)
  Pallas kernels  5.9 us (24%)
  local copies, waits for them, and re-layouts  1.26 us (5%)
  other arithmetic  0.8 us (3%)
  between operations  0.78 us (3%)
    ppermute x3, starting transfers between devices, from_peer(): return lax.ppermute(value, 'dp', xor_pairs(count, mask))  5.95 us
    ppermute x2, starting transfers between devices, on_device(): came = lax.ppermute(send, 'dp', xor_pairs(count, mask))  4.19 us
    ppermute x1, starting transfers between devices, on_device(): pair = lax.ppermute(pair, AXES, onward)  3 us
    ppermute x1, starting transfers between devices, on_device(): far = lax.ppermute(away, 'mirror', xor_pairs(mirrors, 1))  1.58 us
    pallas_call x1, Pallas kernels, prepared(): pl.pallas_call(prepare_kernel, out_shape=(jax.ShapeDtypeStruct((width, 2...  1.55 us
    pallas_call x1, Pallas kernels, on_device(): pl.pallas_call(functools.partial(block_kernel, rows), out_shape=(jax.Shap...  1.55 us
    pallas_call x1, Pallas kernels, on_device(): pl.pallas_call(functools.partial(outer_kernel, 8), out_shape=(jax.ShapeDt...  1.31 us
    unnamed x8, local copies, waits for them, and re-layouts  1.24 us
  transfers between devices with their start and end apart: 10, of which 2 were waited for; matrix products, arithmetic and copies ran while one was open for 0% of the time, Pallas kernels for 15%

profile of v11, /device:TPU:0, one launch (start us, length us, event | category | flops | bytes accessed | tf_op | source)
XLA Modules:
  0.0 24.5 jit_solution(13283281541385183361)
XLA Ops:
  0.6 0.8 %pad_maximum_fusion = bf16[2,4096]{1,0:T(2,128)(2,1)S(1)} fusion(bf16[1,4096]{1,0:T(2,128)(2,1)} %bitcast.15, bf16[1,4096]{1,0:T(2,128)(2,1)} %bitcast.16), kind=kLoop, calls=%fused_computation.2 | loop fusion | flops 32768 | bytes 32768 | tf_op jit(solution)/shard_map/concatenate | solution.py:255
  1.4 3.0 %collective-permute-start = (bf16[2,4096]{1,0:T(2,128)(2,1)S(1)}, bf16[2,4096]{1,0:T(2,128)(2,1)S(1)}, u32[]{:S(2)}, u32[]{:S(2)}) collective-permute-start(bf16[2,4096]{1,0:T(2,128)(2,1)S(1)} %pad_maximum_fusion), channel_id=1, source_target_pairs={{0,16},{1,17},{2,18},{3,19},{4,20},{5,21},{6,22},{7,23},{8,24},{9,... | collective-permute-start | bytes 49160 | tf_op jit(solution)/shard_map/ppermute | solution.py:256
  4.4 0.0 collective-permute-start.4
  4.4 0.5 %collective-permute-start.5 = (bf16[128,4096]{1,0:T(8,128)(2,1)}, bf16[128,4096]{1,0:T(8,128)(2,1)S(1)}, u32[]{:S(2)}, u32[]{:S(2)}) collective-permute-start(bf16[128,4096]{1,0:T(8,128)(2,1)} %bitcast.11), channel_id=1, source_target_pairs={{0,1},{1,0},{2,3},{3,2},{4,5},{5,4},{6,7},{7,6},{8,9},{9,8},{10,11... | collective-permute-start | bytes 3145736 | tf_op jit(solution)/shard_map/ppermute | solution.py:271
  4.9 1.2 %copy-done = bf16[1,4096,128]{2,1,0:T(8,128)(2,1)S(1)} copy-done((bf16[1,4096,128]{2,1,0:T(8,128)(2,1)S(1)}, bf16[1,4096,128]{2,1,0:T(8,128)(2,1)}, u32[]{:S(2)}) %copy-start) | copy-done | bytes 1048600
  6.2 0.1 shard_map.93.in_own
  6.3 0.0 collective-permute-done.pair
  6.3 0.0 copy-start.1
  6.3 0.1 shard_map.94.held
  6.4 2.3 %collective-permute-start.1 = (bf16[96,128]{1,0:T(8,128)(2,1)S(1)}, bf16[96,128]{1,0:T(8,128)(2,1)S(1)}, u32[]{:S(2)}, u32[]{:S(2)}) collective-permute-start(bf16[96,128]{1,0:T(8,128)(2,1)S(1)} %shard_map.94.held), channel_id=1, source_target_pairs={{0,5},{1,4},{2,7},{3,6},{4,1},{5,0},{6,3},{7,2},{8,13},{9,12},{10,... | collective-permute-start | bytes 73736 | tf_op jit(solution)/shard_map/ppermute | solution.py:290
  8.6 2.0 %collective-permute-start.2 = (bf16[96,128]{1,0:T(8,128)(2,1)S(1)}, bf16[96,128]{1,0:T(8,128)(2,1)S(1)}, u32[]{:S(2)}, u32[]{:S(2)}) collective-permute-start(bf16[96,128]{1,0:T(8,128)(2,1)S(1)} %shard_map.94.held), channel_id=1, source_target_pairs={{0,3},{1,2},{2,1},{3,0},{4,7},{5,6},{6,5},{7,4},{8,11},{9,10},{10,... | collective-permute-start | bytes 73736 | tf_op jit(solution)/shard_map/ppermute | solution.py:290
  10.7 0.1 shard_map.96.out_own
  10.8 1.6 %collective-permute-start.3 = (bf16[96,128]{1,0:T(8,128)(2,1)S(1)}, bf16[96,128]{1,0:T(8,128)(2,1)S(1)}, u32[]{:S(2)}, u32[]{:S(2)}) collective-permute-start(bf16[96,128]{1,0:T(8,128)(2,1)S(1)} %collective-permute-done.1.second), channel_id=1, source_target_pairs={{0,3},{1,2},{2,1},{3,0},{4,7},{5,6},{6,5},{7,4},{8,11},{9,10},{10,... | collective-permute-start | bytes 73736 | tf_op jit(solution)/shard_map/ppermute | solution.py:290
  12.5 0.0 collective-permute-done.2.third
  12.5 0.2 shard_map.95.outer
  12.6 0.0 copy-start.2
  12.7 0.0 collective-permute-done.4.in_peer
  12.7 1.6 %shard_map.97 = (bf16[4096,256]{1,0:T(8,128)(2,1)S(1)}, bf16[4096,256]{1,0:T(8,128)(2,1)S(1)}, bf16[512,4096]{1,0:T(8,128)(2,1)S(1)}) custom-call(bf16[4096,128]{1,0:T(8,128)(2,1)S(1)} %shard_map.93.in_own, bf16[4096,128]{1,0:T(8,128)(2,1)S(1)} %collective-permute-done.4.in_peer, bf16[128,4096]{1,0:T(8,128)(2,1)S(1)} %shard_map.96.out_own, ...), custom_call_target="tpu_custom_call" | custom-call | bytes 6291456 | tf_op jit(solution)/shard_map/pallas_call | solution.py:196
  14.2 0.0 collective-permute-done.3.fourth
  14.3 1.5 %shard_map.98 = (bf16[4,4096]{1,0:T(4,128)(2,1)S(1)}, f32[4,4096]{1,0:T(4,128)S(1)}, bf16[4,8704]{1,0:T(4,128)(2,1)S(1)}) custom-call(bf16[3,3,4096]{2,1,0:T(4,128)(2,1)S(1)} %shard_map.95.outer, bf16[96,128]{1,0:T(8,128)(2,1)S(1)} %collective-permute-done.3.fourth, f32[1,4096]{1,0:T(1,128)S(1)} %copy-done.2, bf16[4096,256]{1,0:T(8,128)(2,1)S(1)} %get-tuple-element.36.w_in, ...), custom_call_target="tpu_custom_call" | custom-call | tf_op jit(solution)/shard_map/pallas_call | solution.py:319
  15.8 0.3 %collective-permute-start.7 = (bf16[4,8704]{1,0:T(4,128)(2,1)S(1)}, bf16[4,8704]{1,0:T(4,128)(2,1)S(1)}, u32[]{:S(2)}, u32[]{:S(2)}) collective-permute-start(bf16[4,8704]{1,0:T(4,128)(2,1)S(1)} %get-tuple-element.44.full), channel_id=1, source_target_pairs={{0,1},{1,0},{2,3},{3,2},{4,5},{5,4},{6,7},{7,6},{8,9},{9,8},{10,11... | collective-permute-start | bytes 208904 | tf_op jit(solution)/shard_map/ppermute | solution.py:331
  16.1 1.4 %collective-permute-start.6 = (bf16[4,4096]{1,0:T(4,128)(2,1)S(1)}, bf16[4,4096]{1,0:T(4,128)(2,1)S(1)}, u32[]{:S(2)}, u32[]{:S(2)}) collective-permute-start(bf16[4,4096]{1,0:T(4,128)(2,1)S(1)} %get-tuple-element.40), channel_id=1, source_target_pairs={{0,3},{1,2},{2,1},{3,0},{4,7},{5,6},{6,5},{7,4},{8,11},{9,10},{10,... | collective-permute-start | bytes 98312 | tf_op jit(solution)/shard_map/ppermute | solution.py:342
  17.5 0.2 shard_map.99
  17.7 0.0 collective-permute-done.7.peer
  17.7 0.1 shard_map.100
  17.8 1.6 %collective-permute-start.8 = (bf16[8,4352]{1,0:T(8,128)(2,1)S(1)}, bf16[8,4352]{1,0:T(8,128)(2,1)S(1)}, u32[]{:S(2)}, u32[]{:S(2)}) collective-permute-start(bf16[8,4352]{1,0:T(8,128)(2,1)S(1)} %get-tuple-element.46), channel_id=1, source_target_pairs={{0,8},{8,0},{1,9},{9,1},{2,10},{10,2},{3,11},{11,3},{4,12},{12,4},... | collective-permute-start | bytes 208904 | tf_op jit(solution)/shard_map/ppermute | solution.py:349
  19.4 0.1 collective-permute-done.6
  19.5 2.8 %collective-permute-start.9 = (bf16[2,4096]{1,0:T(2,128)(2,1)S(1)}, bf16[2,4096]{1,0:T(2,128)(2,1)S(1)}, u32[]{:S(2)}, u32[]{:S(2)}) collective-permute-start(bf16[2,4096]{1,0:T(2,128)(2,1)S(1)} %slice.7), channel_id=1, source_target_pairs={{0,5},{1,4},{2,7},{3,6},{4,1},{5,0},{6,3},{7,2},{8,13},{9,12},{10,... | collective-permute-start | bytes 49160 | tf_op jit(solution)/shard_map/ppermute | solution.py:342
  22.3 0.0 collective-permute-done.8.far
  22.3 1.3 %shard_map.101 = (bf16[2048,128]{1,0:T(8,128)(2,1)}, bf16[128,2048]{1,0:T(8,128)(2,1)}) custom-call(bf16[8,4352]{1,0:T(8,128)(2,1)S(1)} %get-tuple-element.45.own, bf16[8,4352]{1,0:T(8,128)(2,1)S(1)} %collective-permute-done.8.far), custom_call_target="tpu_custom_call" | custom-call | bytes 2097152 | tf_op jit(solution)/shard_map/pallas_call | solution.py:351
  23.6 0.1 collective-permute-done.9.came
  23.8 0.7 %shard_map.102 = (bf16[1,4096]{1,0:T(2,128)(2,1)}, bf16[1,4096]{1,0:T(2,128)(2,1)}) custom-call(f32[4,4096]{1,0:T(4,128)S(1)} %convert_add_fusion.part, bf16[2,4096]{1,0:T(2,128)(2,1)S(1)} %collective-permute-done.9.came, f32[1,4096]{1,0:T(1,128)S(1)} %copy-done.2, bf16[2,4096]{1,0:T(2,128)(2,1)S(1)} %collective-permute-done.pair, ...), custom_call_target="tpu_custom_call" | custom-call | tf_op jit(solution)/shard_map/pallas_call | solution.py:369
  (9 shorter events, 0.1 us)
Async XLA Ops:
  0.6 5.7 %copy-start.3 = (bf16[1,1,1,4096]{3,2,1,0:T(2,128)(2,1)S(1)}, bf16[1,1,1,4096]{3,2,1,0:T(2,128)(2,1)}, u32[]{:S(2)}) copy-start(bf16[1,1,1,4096]{3,2,1,0:T(2,128)(2,1)} %param.8) | copy-start | bytes 24580
  1.4 4.9 %collective-permute-start = (bf16[2,4096]{1,0:T(2,128)(2,1)S(1)}, bf16[2,4096]{1,0:T(2,128)(2,1)S(1)}, u32[]{:S(2)}, u32[]{:S(2)}) collective-permute-start(bf16[2,4096]{1,0:T(2,128)(2,1)S(1)} %pad_maximum_fusion), channel_id=1, source_target_pairs={{0,16},{1,17},{2,18},{3,19},{4,20},{5,21},{6,22},{7,23},{8,24},{9,... | collective-permute-start | bytes 49160 | tf_op jit(solution)/shard_map/ppermute | solution.py:256
  4.4 8.2 %collective-permute-start.4 = (bf16[4096,128]{1,0:T(8,128)(2,1)}, bf16[4096,128]{1,0:T(8,128)(2,1)S(1)}, u32[]{:S(2)}, u32[]{:S(2)}) collective-permute-start(bf16[4096,128]{1,0:T(8,128)(2,1)} %bitcast.9), channel_id=1, source_target_pairs={{0,1},{1,0},{2,3},{3,2},{4,5},{5,4},{6,7},{7,6},{8,9},{9,8},{10,11... | collective-permute-start | bytes 3145736 | tf_op jit(solution)/shard_map/ppermute | solution.py:271
  4.4 8.2 %collective-permute-start.5 = (bf16[128,4096]{1,0:T(8,128)(2,1)}, bf16[128,4096]{1,0:T(8,128)(2,1)S(1)}, u32[]{:S(2)}, u32[]{:S(2)}) collective-permute-start(bf16[128,4096]{1,0:T(8,128)(2,1)} %bitcast.11), channel_id=1, source_target_pairs={{0,1},{1,0},{2,3},{3,2},{4,5},{5,4},{6,7},{7,6},{8,9},{9,8},{10,11... | collective-permute-start | bytes 3145736 | tf_op jit(solution)/shard_map/ppermute | solution.py:271
  4.9 1.2 %copy-start = (bf16[1,4096,128]{2,1,0:T(8,128)(2,1)S(1)}, bf16[1,4096,128]{2,1,0:T(8,128)(2,1)}, u32[]{:S(2)}) copy-start(bf16[1,4096,128]{2,1,0:T(8,128)(2,1)} %param.10) | copy-start | bytes 3145732
  6.3 4.4 %copy-start.1 = (bf16[1,128,4096]{2,1,0:T(8,128)(2,1)S(1)}, bf16[1,128,4096]{2,1,0:T(8,128)(2,1)}, u32[]{:S(2)}) copy-start(bf16[1,128,4096]{2,1,0:T(8,128)(2,1)} %param.11) | copy-start | bytes 3145732
  6.4 4.4 %collective-permute-start.1 = (bf16[96,128]{1,0:T(8,128)(2,1)S(1)}, bf16[96,128]{1,0:T(8,128)(2,1)S(1)}, u32[]{:S(2)}, u32[]{:S(2)}) collective-permute-start(bf16[96,128]{1,0:T(8,128)(2,1)S(1)} %shard_map.94.held), channel_id=1, source_target_pairs={{0,5},{1,4},{2,7},{3,6},{4,1},{5,0},{6,3},{7,2},{8,13},{9,12},{10,... | collective-permute-start | bytes 73736 | tf_op jit(solution)/shard_map/ppermute | solution.py:290
  8.6 3.8 %collective-permute-start.2 = (bf16[96,128]{1,0:T(8,128)(2,1)S(1)}, bf16[96,128]{1,0:T(8,128)(2,1)S(1)}, u32[]{:S(2)}, u32[]{:S(2)}) collective-permute-start(bf16[96,128]{1,0:T(8,128)(2,1)S(1)} %shard_map.94.held), channel_id=1, source_target_pairs={{0,3},{1,2},{2,1},{3,0},{4,7},{5,6},{6,5},{7,4},{8,11},{9,10},{10,... | collective-permute-start | bytes 73736 | tf_op jit(solution)/shard_map/ppermute | solution.py:290
  10.8 3.4 %collective-permute-start.3 = (bf16[96,128]{1,0:T(8,128)(2,1)S(1)}, bf16[96,128]{1,0:T(8,128)(2,1)S(1)}, u32[]{:S(2)}, u32[]{:S(2)}) collective-permute-start(bf16[96,128]{1,0:T(8,128)(2,1)S(1)} %collective-permute-done.1.second), channel_id=1, source_target_pairs={{0,3},{1,2},{2,1},{3,0},{4,7},{5,6},{6,5},{7,4},{8,11},{9,10},{10,... | collective-permute-start | bytes 73736 | tf_op jit(solution)/shard_map/ppermute | solution.py:290
  12.6 1.6 %copy-start.2 = (f32[1,4096]{1,0:T(1,128)S(1)}, f32[1,4096]{1,0:T(1,128)}, u32[]{:S(2)}) copy-start(f32[1,4096]{1,0:T(1,128)} %gain.3) | copy-start | bytes 49156
  15.8 1.9 %collective-permute-start.7 = (bf16[4,8704]{1,0:T(4,128)(2,1)S(1)}, bf16[4,8704]{1,0:T(4,128)(2,1)S(1)}, u32[]{:S(2)}, u32[]{:S(2)}) collective-permute-start(bf16[4,8704]{1,0:T(4,128)(2,1)S(1)} %get-tuple-element.44.full), channel_id=1, source_target_pairs={{0,1},{1,0},{2,3},{3,2},{4,5},{5,4},{6,7},{7,6},{8,9},{9,8},{10,11... | collective-permute-start | bytes 208904 | tf_op jit(solution)/shard_map/ppermute | solution.py:331
  16.1 3.3 %collective-permute-start.6 = (bf16[4,4096]{1,0:T(4,128)(2,1)S(1)}, bf16[4,4096]{1,0:T(4,128)(2,1)S(1)}, u32[]{:S(2)}, u32[]{:S(2)}) collective-permute-start(bf16[4,4096]{1,0:T(4,128)(2,1)S(1)} %get-tuple-element.40), channel_id=1, source_target_pairs={{0,3},{1,2},{2,1},{3,0},{4,7},{5,6},{6,5},{7,4},{8,11},{9,10},{10,... | collective-permute-start | bytes 98312 | tf_op jit(solution)/shard_map/ppermute | solution.py:342
  17.8 4.6 %collective-permute-start.8 = (bf16[8,4352]{1,0:T(8,128)(2,1)S(1)}, bf16[8,4352]{1,0:T(8,128)(2,1)S(1)}, u32[]{:S(2)}, u32[]{:S(2)}) collective-permute-start(bf16[8,4352]{1,0:T(8,128)(2,1)S(1)} %get-tuple-element.46), channel_id=1, source_target_pairs={{0,8},{8,0},{1,9},{9,1},{2,10},{10,2},{3,11},{11,3},{4,12},{12,4},... | collective-permute-start | bytes 208904 | tf_op jit(solution)/shard_map/ppermute | solution.py:349
  19.5 4.3 %collective-permute-start.9 = (bf16[2,4096]{1,0:T(2,128)(2,1)S(1)}, bf16[2,4096]{1,0:T(2,128)(2,1)S(1)}, u32[]{:S(2)}, u32[]{:S(2)}) collective-permute-start(bf16[2,4096]{1,0:T(2,128)(2,1)S(1)} %slice.7), channel_id=1, source_target_pairs={{0,5},{1,4},{2,7},{3,6},{4,1},{5,0},{6,3},{7,2},{8,13},{9,12},{10,... | collective-permute-start | bytes 49160 | tf_op jit(solution)/shard_map/ppermute | solution.py:342
